TPU v7x, 32 devices: a whole 2x2x4 slice. The times are simulated.
32 devices in a mesh: dom: 4 (over y, x), sub: 8 (over z, core).
Axes of the slice: x: 2, y: 2, z: 4, core: 2. Of those that a mesh axis runs over, the one named last changes fastest.
Arguments:
- positions: float32 [3, 262144], P(None, ('dom', 'sub')), may hold values from -6 to 6
- masses: float32 [262144], P(('dom', 'sub')), may hold values from 0.0002 to 0.002
- velocities: float32 [3, 262144], P(None, ('dom', 'sub')), may hold values from -6 to 6
- destinations: int32 [262144, 1], P(('dom', 'sub')), may hold values from 0 to 7; in each aligned block of 8192 rows (0 to 8191, 8192 to 16383, ...) at most 1280 rows name the same one
- readers: int32 [4, 4, 8, 80], P(None, None, 'sub'), may hold values from 0 to 1, as said below
- near_local: int32 [2, 6144], P(None, ('dom', 'sub')), may hold values from 0 to 79, as said below
- near_remote: int32 [3, 6144], P(None, ('dom', 'sub')), may hold values from 0 to 79, as said below
Outputs:
- acceleration: float32 [3, 327680], P(None, ('dom', 'sub'))
- kicked: float32 [3, 327680], P(None, ('dom', 'sub'))
Inputs may be any that keep to these rules, and one draw needn't show every extreme that they name: `destinations`: in the particles of one device, at most 1280 share one destination, and some destination has exactly 1280 in some device. `readers`: no domain reads its own leaves. Of one device's leaves, at most 32 are read by one other domain, and every device has a domain that reads exactly 32 of them. `near_local`: both rows are leaves of the device that owns the pair. `near_remote`: row 0 is a target leaf of the owning device; row 1 a domain other than the owner's; row 2 a leaf of the device at that domain with the owner's sub index that the owner's domain reads.
All inputs are finite; a program needn't handle non-finite values.
Results may differ from a plain program's by a relative error of at most 0.0003.
Values sent between devices are 32-bit elements; how exact they have to be, the bound alone decides.
No kernel may reach another device: no remote copies, remote signals or barrier semaphores. Data moves between devices by JAX's collectives and lax.ppermute only.
A program may use at most 64 MiB of HBM per device.

v0:
```python
import math

import jax
import jax.numpy as jnp
from jax import lax
from jax.sharding import PartitionSpec as P

SLOTS = 32


softening = 0.01
gravity = 4.0
kick_time = 0.5


def tile_forces(target_pos, sources):
    delta = sources[:3, :, None, :] - target_pos[:, :, :, None]
    dist_sq = jnp.sum(delta * delta, axis=0) + softening
    inverse = lax.rsqrt(dist_sq)
    weight = sources[3][:, None, :] * inverse * inverse * inverse
    return jnp.sum(weight[None] * delta, axis=-1)


def pair_forces(targets, sources, target_ids, source_ids, weights):
    pairs = target_ids.shape[0]
    block = math.gcd(pairs, 64)

    def step(index, total):
        start = index * block
        tgt_block = lax.dynamic_slice_in_dim(target_ids, start, block)
        src_block = lax.dynamic_slice_in_dim(source_ids, start, block)
        wgt_block = lax.dynamic_slice_in_dim(weights, start, block)
        near = tile_forces(
            jnp.take(targets, tgt_block, axis=1), jnp.take(sources, src_block, axis=1)
        )
        return total.at[:, tgt_block].add(near * wgt_block[None, :, None])

    empty = jnp.zeros((3, targets.shape[1], targets.shape[2]), jnp.float32)
    return lax.fori_loop(0, pairs // block, step, empty)


def remote_forces(leaves, readers, near_remote):
    n_dom = lax.axis_size("dom")
    my_dom = lax.axis_index("dom")
    leaf_size = leaves.shape[2]
    reads = readers[:, :, 0, :]
    table = jnp.take(reads, my_dom, axis=0)
    source_dom = near_remote[1]
    source_leaf = near_remote[2]
    valid = table[source_dom, source_leaf].astype(jnp.float32)
    slots = SLOTS
    wanted = jnp.take(reads, my_dom, axis=1)
    position = jnp.cumsum(wanted, axis=1) - wanted
    picker = wanted[:, None, :] * (
        position[:, None, :] == jnp.arange(slots, dtype=jnp.int32)[None, :, None]
    ).astype(jnp.int32)
    bundle = jnp.einsum(
        "psl,cln->cpsn", picker.astype(jnp.float32), leaves[:4], precision=lax.Precision.HIGHEST
    )
    bundle = bundle.reshape(4, n_dom, slots * leaf_size)
    arrived = lax.all_to_all(bundle, "dom", split_axis=1, concat_axis=1, tiled=True)
    sources = arrived.reshape(4, n_dom * slots, leaf_size)
    lookup = jnp.cumsum(table, axis=1) - table
    source_index = source_dom * slots + lookup[source_dom, source_leaf]
    return pair_forces(leaves[:3], sources, near_remote[0], source_index, valid)


def on_device(positions, masses, velocities, destinations, readers, near_local, near_remote):
    n_sub = lax.axis_size("sub")
    count = positions.shape[1]
    capacity = 5 * count // (4 * n_sub)
    leaf_size = 128
    state = jnp.concatenate([positions, masses[None, :], velocities], axis=0)
    target = destinations[:, 0]
    onehot = (target[:, None] == jnp.arange(n_sub, dtype=jnp.int32)[None, :]).astype(jnp.int32)
    before = jnp.cumsum(onehot, axis=0) - onehot
    rank = jnp.sum(before * onehot, axis=1)
    slot = target * capacity + rank
    outgoing = jnp.zeros((7, n_sub * capacity), jnp.float32).at[:, slot].set(state)
    outgoing = outgoing.reshape(7, n_sub, capacity)
    arrived = lax.all_to_all(outgoing, "sub", split_axis=1, concat_axis=1, tiled=True)
    leaves = arrived.reshape(7, n_sub * capacity // leaf_size, leaf_size)
    unit_weights = jnp.ones((near_local.shape[1],), jnp.float32)
    remote = remote_forces(leaves, readers, near_remote)
    local = pair_forces(leaves[:3], leaves[:4], near_local[0], near_local[1], unit_weights)
    accel = gravity * (local + remote)
    accel = jnp.where(leaves[3][None] > 0.0, accel, jnp.zeros_like(accel))
    kicked = leaves[4:7] + kick_time * accel
    total = leaves.shape[1] * leaf_size
    return (accel.reshape(3, total), kicked.reshape(3, total))


def solution(mesh):
    in_specs = (
        P(None, ("dom", "sub")),
        P(("dom", "sub")),
        P(None, ("dom", "sub")),
        P(("dom", "sub"), None),
        P(None, None, "sub", None),
        P(None, ("dom", "sub")),
        P(None, ("dom", "sub")),
    )
    out_specs = (P(None, ("dom", "sub")), P(None, ("dom", "sub")))
    return jax.shard_map(
        on_device, mesh=mesh, in_specs=in_specs, out_specs=out_specs, check_vma=False
    )
```

profile of v0, /device:TPU:0, one launch (start us, length us, event | category | flops | bytes accessed | tf_op | source)
XLA Modules:
  0.0 165.9 jit_solution(1746959946932785675)
XLA Ops:
  0.6 0.8 fusion.9
  1.4 2.4 %reduce-window.6 = s32[8,64,128]{2,1,0:T(8,128)S(1)} reduce-window(s32[8,64,128]{2,1,0:T(8,128)S(1)} %fusion.9, s32[]{:T(128)} %constant.209.clone.1), window={size=1x1x128 pad=0_0x0_0x127_0}, to_apply=%region_0.0 | reduce-window | flops 8323072 | bytes 524292 | tf_op jit(solution)/shard_map/reduce-window
  3.8 0.3 slice_reduce_fusion
  4.1 0.2 reduce-window.9
  4.4 0.1 add_bitcast_fusion
  4.5 1.0 fusion.8
  5.5 0.8 compare_select_fusion.4
  6.3 1.1 maximum_bitcast_fusion
  7.4 2.7 %copy.92 = f32[8192,7]{1,0:T(8,128)} copy(f32[8192,7]{0,1:T(8,128)S(1)} %maximum_bitcast_fusion) | data formatting | bytes 458752 | tf_op jit(solution)/shard_map/concatenate | solution.py:73
  10.1 23.5 %scatter_custom_fusion.2 = f32[7,10240]{0,1:T(8,128)} fusion(s32[8192]{0:T(1024)S(1)} %bitcast.118, f32[8192,7]{1,0:T(8,128)} %copy.92, f32[]{:T(128)} %constant.207.clone.1), kind=kCustom, calls=%fused_computation.36 | custom fusion | bytes 287232 | tf_op jit(solution)/shard_map/scatter | solution.py:79
  33.6 4.0 %copy.93 = f32[7,8,1280]{2,0,1:T(8,128)} copy(f32[7,8,1280]{0,2,1:T(8,128)} %bitcast.105) | data formatting | bytes 573440 | tf_op jit(solution)/shard_map/reshape | solution.py:80
  37.6 6.3 %all-to-all-start = ((f32[7,8,1280]{2,0,1:T(8,128)}), f32[7,8,1280]{2,0,1:T(8,128)S(1)}, u32[]{:S(2)}, u32[]{:S(2)}) async-start(f32[7,8,1280]{2,0,1:T(8,128)} %copy.93), calls=%async_computation | async-start | bytes 655360 | tf_op jit(solution)/shard_map/all_to_all | solution.py:81
  44.0 0.3 reduce_window_sum.34
  44.3 1.9 %gather_fusion.5 = s32[192]{0:T(256)S(1)} fusion(s32[4,80]{1,0:T(4,128)S(1)} %select_bitcast_fusion.5, s32[192]{0:T(256)S(1)} %bitcast.103), kind=kCustom, calls=%fused_computation.5 | custom fusion | bytes 3072 | tf_op jit(solution)/shard_map/gather | solution.py:50
  46.2 1.9 %gather_fusion.4 = s32[192]{0:T(256)S(1)} fusion(s32[4,80]{1,0:T(4,128)S(1)} %fusion.29, s32[192]{0:T(256)S(1)} %bitcast.104), kind=kCustom, calls=%fused_computation.4 | custom fusion | bytes 3072 | tf_op jit(solution)/shard_map/gather | solution.py:64
  48.2 0.3 reduce_window_sum.35
  48.5 6.6 %all-to-all-done = f32[7,8,1280]{2,0,1:T(8,128)S(1)} async-done(((f32[7,8,1280]{2,0,1:T(8,128)}), f32[7,8,1280]{2,0,1:T(8,128)S(1)}, u32[]{:S(2)}, u32[]{:S(2)}) %all-to-all-start) | async-done | bytes 286752 | tf_op jit(solution)/shard_map/all_to_all | solution.py:81
  55.1 0.4 convolution_bitcast_fusion
  55.6 0.9 copy.101
  56.5 3.7 %all-to-all-start.1 = ((f32[4,4,4096]{2,0,1:T(4,128)}), f32[4,4,4096]{2,0,1:T(4,128)S(1)}, u32[]{:S(2)}, u32[]{:S(2)}) async-start(f32[4,4,4096]{2,0,1:T(4,128)} %copy.101), calls=%async_computation.1 | async-start | bytes 524288 | tf_op jit(solution)/shard_map/all_to_all | solution.py:61
  60.3 52.0 %while.28 = (s32[]{:T(128)}, f32[3,80,128]{2,0,1:T(4,128)S(1)}, s32[192]{0:T(256)S(1)}, s32[192]{0:T(256)S(1)}, f32[4,80,128]{2,0,1:T(4,128)S(1)}, /*index=5*/f3...) while((s32[]{:T(128)}, f32[3,80,128]{2,0,1:T(4,128)S(1)}, s32[192]{0:T(256)S(1)}, ...), condition=%wide.region_8.10_spmd, body=%wide.region_4.0_spmd.sunk | while | flops 22080260 | bytes 19180192 | solution.py:39
  60.4 0.7 gather_fusion
  61.1 0.1 select_bitcast_fusion.10
  61.2 0.7 gather_fusion.1
  61.9 0.1 select_bitcast_fusion.11
  62.1 4.1 %fusion.34 = f32[64,128,128]{2,1,0:T(8,128)S(1)} fusion(f32[3,64,128]{2,1,0:T(8,128)S(1)} %copy.137, f32[3,64,128]{2,1,0:T(8,128)S(1)} %copy.138), kind=kLoop, calls=%fused_computation.11.clone.1 | loop fusion | flops 8388608 | bytes 4390912 | tf_op jit(solution)/shard_map/while/body/eval_jaxpr/reduce_sum | solution.py:18
  66.2 0.9 multiply_multiply_fusion.4
  67.2 7.6 %fusion.35 = f32[3,64,128]{2,1,0:T(8,128)S(1)} fusion(f32[64,128,128]{2,1,0:T(8,128)S(1)} %multiply_multiply_fusion.4, f32[3,64,128]{2,1,0:T(8,128)S(1)} %copy.137, f32[3,64,128]{2,1,0:T(8,128)S(1)} %copy.138), kind=kLoop, calls=%fused_computation.12.clone.1 | loop fusion | flops 9412608 | bytes 4489216 | tf_op jit(solution)/shard_map/while/body/eval_jaxpr/reduce_sum | solution.py:21
  74.9 2.7 %scatter_fusion = f32[3,80,128]{2,0,1:T(4,128)S(1)} fusion(f32[3,80,128]{2,0,1:T(4,128)S(1)} %get-tuple-element.513, s32[64]{0:T(128)S(1)} %get-tuple-element.454, f32[64,3,128]{2,1,0:T(4,128)S(1)} %copy.139), kind=kCustom, calls=%fused_computation.6.clone.1 | custom fusion | flops 24576 | bytes 295168 | tf_op jit(solution)/shard_map/while/body/eval_jaxpr/scatter-add | solution.py:36
  77.7 0.7 gather_fusion
  78.4 0.1 select_bitcast_fusion.10
  78.6 0.7 gather_fusion.1
  79.2 0.1 select_bitcast_fusion.11
  79.4 4.1 %fusion.34 = f32[64,128,128]{2,1,0:T(8,128)S(1)} fusion(f32[3,64,128]{2,1,0:T(8,128)S(1)} %copy.137, f32[3,64,128]{2,1,0:T(8,128)S(1)} %copy.138), kind=kLoop, calls=%fused_computation.11.clone.1 | loop fusion | flops 8388608 | bytes 4390912 | tf_op jit(solution)/shard_map/while/body/eval_jaxpr/reduce_sum | solution.py:18
  83.6 0.9 multiply_multiply_fusion.4
  84.5 7.6 %fusion.35 = f32[3,64,128]{2,1,0:T(8,128)S(1)} fusion(f32[64,128,128]{2,1,0:T(8,128)S(1)} %multiply_multiply_fusion.4, f32[3,64,128]{2,1,0:T(8,128)S(1)} %copy.137, f32[3,64,128]{2,1,0:T(8,128)S(1)} %copy.138), kind=kLoop, calls=%fused_computation.12.clone.1 | loop fusion | flops 9412608 | bytes 4489216 | tf_op jit(solution)/shard_map/while/body/eval_jaxpr/reduce_sum | solution.py:21
  92.2 2.7 %scatter_fusion = f32[3,80,128]{2,0,1:T(4,128)S(1)} fusion(f32[3,80,128]{2,0,1:T(4,128)S(1)} %get-tuple-element.513, s32[64]{0:T(128)S(1)} %get-tuple-element.454, f32[64,3,128]{2,1,0:T(4,128)S(1)} %copy.139), kind=kCustom, calls=%fused_computation.6.clone.1 | custom fusion | flops 24576 | bytes 295168 | tf_op jit(solution)/shard_map/while/body/eval_jaxpr/scatter-add | solution.py:36
  95.0 0.7 gather_fusion
  95.9 0.7 gather_fusion.1
  96.7 4.1 %fusion.34 = f32[64,128,128]{2,1,0:T(8,128)S(1)} fusion(f32[3,64,128]{2,1,0:T(8,128)S(1)} %copy.137, f32[3,64,128]{2,1,0:T(8,128)S(1)} %copy.138), kind=kLoop, calls=%fused_computation.11.clone.1 | loop fusion | flops 8388608 | bytes 4390912 | tf_op jit(solution)/shard_map/while/body/eval_jaxpr/reduce_sum | solution.py:18
  100.9 0.9 multiply_multiply_fusion.4
  101.8 7.6 %fusion.35 = f32[3,64,128]{2,1,0:T(8,128)S(1)} fusion(f32[64,128,128]{2,1,0:T(8,128)S(1)} %multiply_multiply_fusion.4, f32[3,64,128]{2,1,0:T(8,128)S(1)} %copy.137, f32[3,64,128]{2,1,0:T(8,128)S(1)} %copy.138), kind=kLoop, calls=%fused_computation.12.clone.1 | loop fusion | flops 9412608 | bytes 4489216 | tf_op jit(solution)/shard_map/while/body/eval_jaxpr/reduce_sum | solution.py:21
  109.5 2.7 %scatter_fusion = f32[3,80,128]{2,0,1:T(4,128)S(1)} fusion(f32[3,80,128]{2,0,1:T(4,128)S(1)} %get-tuple-element.513, s32[64]{0:T(128)S(1)} %get-tuple-element.454, f32[64,3,128]{2,1,0:T(4,128)S(1)} %copy.139), kind=kCustom, calls=%fused_computation.6.clone.1 | custom fusion | flops 24576 | bytes 295168 | tf_op jit(solution)/shard_map/while/body/eval_jaxpr/scatter-add | solution.py:36
  112.3 0.1 compare_reduce_fusion
  112.6 52.4 %while.29 = (s32[]{:T(128)}, f32[3,80,128]{2,0,1:T(4,128)S(1)}, s32[192]{0:T(256)S(1)}, s32[192]{0:T(256)S(1)}, f32[4,128,128]{2,0,1:T(4,128)S(1)}, /*index=5*/f...) while((s32[]{:T(128)}, f32[3,80,128]{2,0,1:T(4,128)S(1)}, ...), condition=%wide.region_15.17_spmd, body=%wide.region_11.16_spmd.sunk | while | flops 22104836 | bytes 19377580 | solution.py:39
  112.7 0.7 gather_fusion.2
  113.5 0.7 gather_fusion.3
  114.3 4.1 %fusion.36 = f32[64,128,128]{2,1,0:T(8,128)S(1)} fusion(f32[3,64,128]{2,1,0:T(8,128)S(1)} %copy.140, f32[3,64,128]{2,1,0:T(8,128)S(1)} %copy.141), kind=kLoop, calls=%fused_computation.24.clone.1 | loop fusion | flops 8388608 | bytes 4390912 | tf_op jit(solution)/shard_map/while/body/eval_jaxpr/reduce_sum | solution.py:18
  118.5 0.9 multiply_multiply_fusion.5
  119.4 7.6 %fusion.37 = f32[3,64,128]{2,1,0:T(8,128)S(1)} fusion(f32[64,128,128]{2,1,0:T(8,128)S(1)} %multiply_multiply_fusion.5, f32[3,64,128]{2,1,0:T(8,128)S(1)} %copy.140, f32[3,64,128]{2,1,0:T(8,128)S(1)} %copy.141), kind=kLoop, calls=%fused_computation.25.clone.1 | loop fusion | flops 9412608 | bytes 4489216 | tf_op jit(solution)/shard_map/while/body/eval_jaxpr/reduce_sum | solution.py:21
  127.3 2.8 %scatter_fusion.1 = f32[3,80,128]{2,0,1:T(4,128)S(1)} fusion(f32[3,80,128]{2,0,1:T(4,128)S(1)} %get-tuple-element.481, s32[64]{0:T(128)S(1)} %get-tuple-element.465, f32[64,3,128]{2,1,0:T(4,128)S(1)} %copy.142), kind=kCustom, calls=%fused_computation.7.clone.1 | custom fusion | flops 24576 | bytes 295168 | tf_op jit(solution)/shard_map/while/body/eval_jaxpr/scatter-add | solution.py:36
  130.2 0.7 gather_fusion.2
  131.0 0.7 gather_fusion.3
  131.8 4.1 %fusion.36 = f32[64,128,128]{2,1,0:T(8,128)S(1)} fusion(f32[3,64,128]{2,1,0:T(8,128)S(1)} %copy.140, f32[3,64,128]{2,1,0:T(8,128)S(1)} %copy.141), kind=kLoop, calls=%fused_computation.24.clone.1 | loop fusion | flops 8388608 | bytes 4390912 | tf_op jit(solution)/shard_map/while/body/eval_jaxpr/reduce_sum | solution.py:18
  136.0 0.9 multiply_multiply_fusion.5
  136.9 7.6 %fusion.37 = f32[3,64,128]{2,1,0:T(8,128)S(1)} fusion(f32[64,128,128]{2,1,0:T(8,128)S(1)} %multiply_multiply_fusion.5, f32[3,64,128]{2,1,0:T(8,128)S(1)} %copy.140, f32[3,64,128]{2,1,0:T(8,128)S(1)} %copy.141), kind=kLoop, calls=%fused_computation.25.clone.1 | loop fusion | flops 9412608 | bytes 4489216 | tf_op jit(solution)/shard_map/while/body/eval_jaxpr/reduce_sum | solution.py:21
  144.8 2.8 %scatter_fusion.1 = f32[3,80,128]{2,0,1:T(4,128)S(1)} fusion(f32[3,80,128]{2,0,1:T(4,128)S(1)} %get-tuple-element.481, s32[64]{0:T(128)S(1)} %get-tuple-element.465, f32[64,3,128]{2,1,0:T(4,128)S(1)} %copy.142), kind=kCustom, calls=%fused_computation.7.clone.1 | custom fusion | flops 24576 | bytes 295168 | tf_op jit(solution)/shard_map/while/body/eval_jaxpr/scatter-add | solution.py:36
  147.7 0.7 gather_fusion.2
  148.5 0.7 gather_fusion.3
  149.3 4.1 %fusion.36 = f32[64,128,128]{2,1,0:T(8,128)S(1)} fusion(f32[3,64,128]{2,1,0:T(8,128)S(1)} %copy.140, f32[3,64,128]{2,1,0:T(8,128)S(1)} %copy.141), kind=kLoop, calls=%fused_computation.24.clone.1 | loop fusion | flops 8388608 | bytes 4390912 | tf_op jit(solution)/shard_map/while/body/eval_jaxpr/reduce_sum | solution.py:18
  153.5 0.9 multiply_multiply_fusion.5
  154.4 7.6 %fusion.37 = f32[3,64,128]{2,1,0:T(8,128)S(1)} fusion(f32[64,128,128]{2,1,0:T(8,128)S(1)} %multiply_multiply_fusion.5, f32[3,64,128]{2,1,0:T(8,128)S(1)} %copy.140, f32[3,64,128]{2,1,0:T(8,128)S(1)} %copy.141), kind=kLoop, calls=%fused_computation.25.clone.1 | loop fusion | flops 9412608 | bytes 4489216 | tf_op jit(solution)/shard_map/while/body/eval_jaxpr/reduce_sum | solution.py:21
  162.3 2.7 %scatter_fusion.1 = f32[3,80,128]{2,0,1:T(4,128)S(1)} fusion(f32[3,80,128]{2,0,1:T(4,128)S(1)} %get-tuple-element.481, s32[64]{0:T(128)S(1)} %get-tuple-element.465, f32[64,3,128]{2,1,0:T(4,128)S(1)} %copy.142), kind=kCustom, calls=%fused_computation.7.clone.1 | custom fusion | flops 24576 | bytes 295168 | tf_op jit(solution)/shard_map/while/body/eval_jaxpr/scatter-add | solution.py:36
  165.1 0.8 copy_bitcast_fusion
  (84 shorter events, 3.3 us)
Async XLA Ops:
  33.6 10.3 %copy-start.1 = (s32[3,192]{1,0:T(4,128)S(1)}, s32[3,192]{1,0:T(4,128)}, u32[]{:S(2)}) copy-start(s32[3,192]{1,0:T(4,128)} %param.19) | copy-start | bytes 6916
  33.6 10.4 %copy-start = (s32[4,4,1,80]{3,2,1,0:T(1,128)S(1)}, s32[4,4,1,80]{3,2,1,0:T(1,128)}, u32[]{:S(2)}) copy-start(s32[4,4,1,80]{3,2,1,0:T(1,128)} %param.17) | copy-start | bytes 15364
  33.6 14.9 %copy-start.2 = (s32[2,192]{1,0:T(2,128)S(1)}, s32[2,192]{1,0:T(2,128)}, u32[]{:S(2)}) copy-start(s32[2,192]{1,0:T(2,128)} %param.18) | copy-start | bytes 4612
  37.6 17.5 %all-to-all-start = ((f32[7,8,1280]{2,0,1:T(8,128)}), f32[7,8,1280]{2,0,1:T(8,128)S(1)}, u32[]{:S(2)}, u32[]{:S(2)}) async-start(f32[7,8,1280]{2,0,1:T(8,128)} %copy.93), calls=%async_computation | async-start | bytes 655360 | tf_op jit(solution)/shard_map/all_to_all | solution.py:81
  56.5 56.1 %all-to-all-start.1 = ((f32[4,4,4096]{2,0,1:T(4,128)}), f32[4,4,4096]{2,0,1:T(4,128)S(1)}, u32[]{:S(2)}, u32[]{:S(2)}) async-start(f32[4,4,4096]{2,0,1:T(4,128)} %copy.101), calls=%async_computation.1 | async-start | bytes 524288 | tf_op jit(solution)/shard_map/all_to_all | solution.py:61
where the time goes:
time: 166 us
  other arithmetic  102 us (61%)
  local copies, waits for them, and re-layouts  45.4 us (27%)
  starting transfers between devices  10 us (6%)
  waiting for transfers between devices  6.58 us (4%)
    reduce_sum x6, other arithmetic, tile_forces(): return jnp.sum(weight[None] * delta, axis=-1)  45.7 us
    reduce_sum x6, other arithmetic, tile_forces(): dist_sq = jnp.sum(delta * delta, axis=0) + softening  24.8 us
    scatter x1, local copies, waits for them, and re-layouts, on_device(): jnp.zeros((7, n_sub * capacity), jnp.float32).at[:, slot].set(state)  23.5 us
    scatter-add x6, other arithmetic, step(): return total.at[:, tgt_block].add(near * wgt_block[None, :, None])  16.5 us
    all_to_all x1, waiting for transfers between devices, on_device(): lax.all_to_all(outgoing, 'sub', split_axis=1, concat_axis=1, tiled=True)  6.58 us
    all_to_all x1, starting transfers between devices, on_device(): lax.all_to_all(outgoing, 'sub', split_axis=1, concat_axis=1, tiled=True)  6.33 us
    mul x6, other arithmetic, tile_forces(): weight = sources[3][:, None, :] * inverse * inverse * inverse  5.41 us
    reshape x1, local copies, waits for them, and re-layouts, on_device(): outgoing = outgoing.reshape(7, n_sub, capacity)  4 us
  transfers between devices with their start and end apart: 2, of which 1 were waited for; matrix products, arithmetic and copies ran while one was open for 34% of the time, Pallas kernels for 0%

commit v1 on v0

v1 whole, which is shorter than its diff:
```python
import functools

import jax
import jax.numpy as jnp
from jax import lax
from jax.experimental import pallas as pl
from jax.experimental.pallas import tpu as pltpu
from jax.sharding import PartitionSpec as P

SLOTS = 32
LEAF = 128
COLS = 8

softening = 0.01
gravity = 4.0
kick_time = 0.5

VMEM_LIMIT = 48 << 20
F32 = jnp.float32
I32 = jnp.int32


def vmem():
    return pl.BlockSpec(memory_space=pltpu.VMEM)


def smem():
    return pl.BlockSpec(memory_space=pltpu.SMEM)


def lane_gather(tile, index):
    return jnp.take_along_axis(tile, index, axis=1, mode="promise_in_bounds")


def regroup_kernel(
    n_sub, leaves, pos_ref, mass_ref, vel_ref, dest_ref, near_ref, far_ref,
    tiles, table, off_ref, cnt_ref, start_ref, perm_ref, leaf_vec, leaf_idx, sem
):
    blocks = dest_ref.shape[0]
    dest = dest_ref[...]
    masks = [dest == e for e in range(n_sub)]
    ones_of = jnp.concatenate([m.astype(F32) for m in masks], axis=0).astype(jnp.bfloat16)
    row = lax.broadcasted_iota(I32, (LEAF, LEAF), 0)
    col = lax.broadcasted_iota(I32, (LEAF, LEAF), 1)
    upper = jnp.where(row <= col, 1.0, 0.0).astype(jnp.bfloat16)
    weights = jnp.concatenate([upper, jnp.ones((LEAF, LEAF), jnp.bfloat16)], axis=1)
    counts = jnp.dot(ones_of, weights, preferred_element_type=F32)
    brow = lax.broadcasted_iota(I32, (blocks, blocks), 0)
    bcol = lax.broadcasted_iota(I32, (blocks, blocks), 1)
    earlier = jnp.where(bcol < brow, 1.0, 0.0).astype(jnp.bfloat16)
    start = jnp.zeros((blocks, LEAF), F32)
    place = jnp.zeros((blocks, LEAF), F32)
    lane64 = lax.broadcasted_iota(I32, (blocks, LEAF), 1)
    leaf_of = jnp.zeros((blocks, LEAF), I32)
    for e in range(n_sub):
        inside = counts[e * blocks:(e + 1) * blocks, :LEAF]
        total = counts[e * blocks:(e + 1) * blocks, LEAF:]
        place = jnp.where(masks[e], inside - 1.0 + start, place)
        offset = jnp.dot(earlier, total.astype(jnp.bfloat16), preferred_element_type=F32).astype(I32)
        off_ref[e] = offset
        cnt_ref[e] = total.astype(I32)
        start_ref[e] = start.astype(I32)
        base = e * (leaves + 1)
        leaf_of = jnp.where(lane64 == e, base + (offset >> 7), leaf_of)
        ends = (offset + total.astype(I32)) >> 7
        leaf_of = jnp.where(lane64 == n_sub + e, base + ends, leaf_of)
        start = start + total
    leaf_vec[...] = leaf_of
    copy = pltpu.make_async_copy(leaf_vec, leaf_idx, sem)
    copy.start()
    perm_ref[...] = place.astype(I32)
    table[...] = jnp.zeros_like(table)
    tiles[...] = jnp.zeros_like(tiles)
    for b in range(blocks):
        lanes = slice(b * LEAF, (b + 1) * LEAF)
        table[b, 0:3, :] = pos_ref[:, lanes]
        table[b, 3:4, :] = mass_ref[b:b + 1, :]
        table[b, 4:7, :] = vel_ref[:, lanes]
    lane = lax.broadcasted_iota(I32, (8, LEAF), 1)
    lane_rows = lax.broadcasted_iota(I32, (16, LEAF), 1).astype(F32).astype(jnp.bfloat16)
    copy.wait()

    def step(b, tails):
        place_row = perm_ref[pl.ds(b, 1), :]
        onehot = jnp.where(row == place_row, 1.0, 0.0).astype(jnp.bfloat16)
        inverse = lax.dot_general(
            lane_rows, onehot, (((1,), (1,)), ((), ())), preferred_element_type=F32
        )[:8].astype(I32)
        ordered = lane_gather(table[b], inverse)
        new = []
        for e in range(n_sub):
            offset = jnp.broadcast_to(off_ref[e, pl.ds(b, 1), :], (8, LEAF))
            count = jnp.broadcast_to(cnt_ref[e, pl.ds(b, 1), :], (8, LEAF))
            first = jnp.broadcast_to(start_ref[e, pl.ds(b, 1), :], (8, LEAF))
            turned = (lane - offset) & (LEAF - 1)
            moved = lane_gather(ordered, (turned + first) & (LEAF - 1))
            low = offset & (LEAF - 1)
            taken = turned < count
            tail = jnp.where(taken & (lane >= low), moved, tails[e])
            tiles[leaf_idx[b, e]] = tail
            fresh = jnp.where(taken & (lane < low), moved, 0.0)
            new.append(jnp.where(low + count >= LEAF, fresh, tail))
        return tuple(new)

    tails = lax.fori_loop(0, blocks, step, (jnp.zeros((8, LEAF), F32),) * n_sub)
    for e in range(n_sub):
        tiles[leaf_idx[blocks - 1, n_sub + e]] = tails[e]
        for l in range(leaves):
            tile = tiles[e * (leaves + 1) + l]
            near_ref[e, 4 * l:4 * l + 4, :] = tile[0:4]
            far_ref[e, 4 * l:4 * l + 4, :] = tile[4:8]


def regroup(positions, masses, velocities, destinations, n_sub, leaves):
    count = positions.shape[1]
    blocks = count // LEAF
    out = jax.ShapeDtypeStruct((n_sub, leaves * 4, LEAF), F32)
    return pl.pallas_call(
        functools.partial(regroup_kernel, n_sub, leaves),
        out_shape=(out, out),
        in_specs=[vmem()] * 4,
        out_specs=(vmem(), vmem()),
        scratch_shapes=[
            pltpu.VMEM((n_sub * (leaves + 1), 8, LEAF), F32),
            pltpu.VMEM((blocks, 8, LEAF), F32),
            pltpu.VMEM((n_sub, blocks, LEAF), I32),
            pltpu.VMEM((n_sub, blocks, LEAF), I32),
            pltpu.VMEM((n_sub, blocks, LEAF), I32),
            pltpu.VMEM((blocks, LEAF), I32),
            pltpu.VMEM((blocks, LEAF), I32),
            pltpu.SMEM((blocks, LEAF), I32),
            pltpu.SemaphoreType.DMA,
        ],
        compiler_params=pltpu.CompilerParams(vmem_limit_bytes=VMEM_LIMIT),
        name="regroup",
    )(positions, masses.reshape(blocks, LEAF), velocities, destinations.reshape(blocks, LEAF))


def plan_kernel(n_dom, leaves, reads_ref, far_ref, me_ref, list_ref, source_ref, valid_ref, lookup):
    me = me_ref[0]
    pairs = far_ref.shape[1]

    def wanted(p, _):
        for k in range(SLOTS):
            list_ref[p, k] = 0

        def leaf(l, taken):
            flag = reads_ref[p, me, l]

            @pl.when(flag > 0)
            def _():
                list_ref[p, taken] = l

            return taken + flag

        def seen(l, before):
            lookup[p, l] = jnp.minimum(before, SLOTS - 1)
            return before + reads_ref[me, p, l]

        lax.fori_loop(0, leaves, leaf, jnp.int32(0))
        lax.fori_loop(0, leaves, seen, jnp.int32(0))
        return 0

    lax.fori_loop(0, n_dom, wanted, 0)

    def pair(i, _):
        q = far_ref[1, i]
        l = far_ref[2, i]
        source_ref[i] = q * SLOTS + lookup[q, l]
        valid_ref[i] = reads_ref[me, q, l].astype(F32)
        return 0

    lax.fori_loop(0, pairs, pair, 0)


def plan(readers, near_remote, my_dom):
    n_dom, leaves = readers.shape[0], readers.shape[3]
    pairs = near_remote.shape[1]
    return pl.pallas_call(
        functools.partial(plan_kernel, n_dom, leaves),
        out_shape=(
            jax.ShapeDtypeStruct((n_dom, SLOTS), I32),
            jax.ShapeDtypeStruct((pairs,), I32),
            jax.ShapeDtypeStruct((pairs,), F32),
        ),
        in_specs=[smem()] * 3,
        out_specs=(smem(), smem(), smem()),
        scratch_shapes=[pltpu.SMEM((n_dom, leaves), I32)],
        name="plan",
    )(readers.reshape(n_dom, n_dom, leaves), near_remote, my_dom.reshape(1))


def bundle_kernel(list_ref, leaf_ref, out_ref):
    n_dom = out_ref.shape[0]

    def step(k, _):
        for p in range(n_dom):
            out_ref[p, k] = leaf_ref[list_ref[p, k]]
        return 0

    lax.fori_loop(0, SLOTS, step, 0, unroll=4)


def bundle(lists, near):
    n_dom = lists.shape[0]
    return pl.pallas_call(
        bundle_kernel,
        out_shape=jax.ShapeDtypeStruct((n_dom, SLOTS, 4, LEAF), F32),
        in_specs=[smem(), vmem()],
        out_specs=vmem(),
        compiler_params=pltpu.CompilerParams(vmem_limit_bytes=VMEM_LIMIT),
        name="bundle",
    )(lists, near.reshape(-1, 4, LEAF))


def columns_of(src_ref, cols_ref):
    rows = src_ref.shape[0]
    for k in range(cols_ref.shape[0]):
        size = min(LEAF, rows - k * LEAF)
        part = src_ref[k * LEAF:k * LEAF + size, :]
        if size < LEAF:
            part = jnp.concatenate([part, jnp.zeros((LEAF - size, LEAF), F32)], axis=0)
        cols_ref[k] = part.T


def pair_loop(pairs, target_of, source_of, weight_of, tgt_ref, cols_ref, acc_ref):
    def step(i, _):
        t = target_of(i)
        s = source_of(i)
        block, first = s >> 5, (s & 31) * 4
        index = [jnp.full((8, LEAF), first + c, I32) for c in range(4)]
        here = [jnp.broadcast_to(tgt_ref[pl.ds(4 * t + c, 1), :], (8, LEAF)) for c in range(3)]
        sums = [jnp.zeros((8, LEAF), F32) for _ in range(3)]
        for g in range(LEAF // 8):
            cols = cols_ref[block, 8 * g:8 * g + 8, :]
            delta = [lane_gather(cols, index[c]) - here[c] for c in range(3)]
            mass = lane_gather(cols, index[3])
            dist = delta[0] * delta[0] + delta[1] * delta[1] + (delta[2] * delta[2] + softening)
            inv = lax.rsqrt(dist)
            weight = (mass * inv) * (inv * inv)
            sums = [sums[c] + weight * delta[c] for c in range(3)]
        scale = weight_of(i)
        for c in range(3):
            part = sums[c] if scale is None else sums[c] * scale
            acc_ref[t, c] += part
        return 0

    lax.fori_loop(0, pairs, step, 0, unroll=2)


def local_kernel(ids_ref, src_ref, out_ref, cols_ref, acc_ref):
    columns_of(src_ref, cols_ref)
    acc_ref[...] = jnp.zeros_like(acc_ref)
    pair_loop(
        ids_ref.shape[1], lambda i: ids_ref[0, i], lambda i: ids_ref[1, i], lambda i: None,
        src_ref, cols_ref, acc_ref,
    )
    for t in range(acc_ref.shape[0]):
        for c in range(3):
            out_ref[4 * t + c:4 * t + c + 1, :] = jnp.sum(acc_ref[t, c], axis=0, keepdims=True)


def local_forces(near_local, near):
    rows = near.shape[0]
    pairs = near_local.shape[1]
    work = pairs * LEAF * LEAF
    return pl.pallas_call(
        local_kernel,
        out_shape=jax.ShapeDtypeStruct((rows, LEAF), F32),
        in_specs=[smem(), vmem()],
        out_specs=vmem(),
        scratch_shapes=[
            pltpu.VMEM((pl.cdiv(rows, LEAF), LEAF, LEAF), F32),
            pltpu.VMEM((rows // 4, 3, 8, LEAF), F32),
        ],
        compiler_params=pltpu.CompilerParams(vmem_limit_bytes=VMEM_LIMIT),
        cost_estimate=pl.CostEstimate(flops=18 * work, transcendentals=work, bytes_accessed=8 * rows * LEAF),
        name="local_forces",
    )(near_local, near)


def remote_kernel(ids_ref, source_ref, valid_ref, tgt_ref, src_ref, local_ref, vel_ref,
                  accel_ref, kicked_ref, cols_ref, acc_ref):
    columns_of(src_ref, cols_ref)
    acc_ref[...] = jnp.zeros_like(acc_ref)
    pair_loop(
        ids_ref.shape[1], lambda i: ids_ref[0, i], lambda i: source_ref[i], lambda i: valid_ref[i],
        tgt_ref, cols_ref, acc_ref,
    )
    for t in range(acc_ref.shape[0]):
        used = tgt_ref[4 * t + 3:4 * t + 4, :] > 0.0
        lanes = slice(t * LEAF, (t + 1) * LEAF)
        for c in range(3):
            row = slice(4 * t + c, 4 * t + c + 1)
            total = local_ref[row, :] + jnp.sum(acc_ref[t, c], axis=0, keepdims=True)
            accel = jnp.where(used, gravity * total, 0.0)
            accel_ref[c:c + 1, lanes] = accel
            kicked_ref[c:c + 1, lanes] = vel_ref[row, :] + kick_time * accel


def remote_forces(near_remote, source, valid, near, arrived, local, vel):
    rows = near.shape[0]
    pairs = near_remote.shape[1]
    work = pairs * LEAF * LEAF
    out = jax.ShapeDtypeStruct((3, rows // 4 * LEAF), F32)
    return pl.pallas_call(
        remote_kernel,
        out_shape=(out, out),
        in_specs=[smem(), smem(), smem(), vmem(), vmem(), vmem(), vmem()],
        out_specs=(vmem(), vmem()),
        scratch_shapes=[
            pltpu.VMEM((pl.cdiv(arrived.shape[0], LEAF), LEAF, LEAF), F32),
            pltpu.VMEM((rows // 4, 3, 8, LEAF), F32),
        ],
        compiler_params=pltpu.CompilerParams(vmem_limit_bytes=VMEM_LIMIT),
        cost_estimate=pl.CostEstimate(flops=18 * work, transcendentals=work, bytes_accessed=24 * rows * LEAF),
        name="remote_forces",
    )(near_remote, source, valid, near, arrived, local, vel)


def on_device(positions, masses, velocities, destinations, readers, near_local, near_remote):
    n_sub = lax.axis_size("sub")
    n_dom = lax.axis_size("dom")
    count = positions.shape[1]
    capacity = 5 * count // (4 * n_sub)
    leaves = capacity // LEAF
    near, far = regroup(positions, masses, velocities, destinations, n_sub, leaves)
    near = lax.all_to_all(near, "sub", split_axis=0, concat_axis=0, tiled=True)
    lists, source, valid = plan(readers, near_remote, lax.axis_index("dom").astype(I32))
    near = near.reshape(n_sub * leaves * 4, LEAF)
    packed = bundle(lists, near)
    arrived = lax.all_to_all(packed, "dom", split_axis=0, concat_axis=0, tiled=True)
    far = lax.all_to_all(far, "sub", split_axis=0, concat_axis=0, tiled=True)
    local = local_forces(near_local, near)
    return remote_forces(
        near_remote, source, valid, near, arrived.reshape(n_dom * SLOTS * 4, LEAF), local,
        far.reshape(n_sub * leaves * 4, LEAF),
    )


def solution(mesh):
    in_specs = (
        P(None, ("dom", "sub")),
        P(("dom", "sub")),
        P(None, ("dom", "sub")),
        P(("dom", "sub"), None),
        P(None, None, "sub", None),
        P(None, ("dom", "sub")),
        P(None, ("dom", "sub")),
    )
    out_specs = (P(None, ("dom", "sub")), P(None, ("dom", "sub")))
    return jax.shard_map(
        on_device, mesh=mesh, in_specs=in_specs, out_specs=out_specs, check_vma=False
    )
```

time: 166 us -> 144 us (0.87)
  Pallas kernels: 0 us -> 117 us
  other arithmetic: 102 us -> 0 us
  local copies, waits for them, and re-layouts: 45.4 us -> 4.66 us
  blocking collectives: 0 us -> 13.3 us
  waiting for transfers between devices: 6.58 us -> 0.01 us
  starting transfers between devices: 10 us -> 7.23 us
    pallas_call x0 -> x5, Pallas kernels: none -> 117 us  [the longest x1 41.7 us: remote_forces(): pl.pallas_call(remote_kernel, out_shape=(out, out), in_specs=[smem(), sme...]
    reduce_sum x13 -> x0, other arithmetic: 71.5 us -> none  [the longest x6 45.7 us: tile_forces(): return jnp.sum(weight[None] * delta, axis=-1)]
    scatter x1 -> x0, local copies, waits for them, and re-layouts: 23.5 us -> none  [on_device(): jnp.zeros((7, n_sub * capacity), jnp.float32).at[:, slot].set(state)]
    scatter-add x6 -> x0, other arithmetic: 16.5 us -> none  [step(): return total.at[:, tgt_block].add(near * wgt_block[None, :, None])]
    all_to_all x0 -> x1, blocking collectives: none -> 13.3 us  [on_device(): near = lax.all_to_all(near, 'sub', split_axis=0, concat_axis=0, tiled=True)]
    gather x14 -> x0, local copies, waits for them, and re-layouts: 11.8 us -> none  [the longest x6 3.94 us: step(): jnp.take(targets, tgt_block, axis=1)]
    all_to_all x2, waiting for transfers between devices: 6.58 us -> 0.01 us  [the longest x1 0.01 us: on_device(): far = lax.all_to_all(far, 'sub', split_axis=0, concat_axis=0, tiled=True)]
    reshape x4 -> x0, local copies, waits for them, and re-layouts: 5.8 us -> none  [the longest x1 4 us: on_device(): outgoing = outgoing.reshape(7, n_sub, capacity)]
  transfers between devices with their start and end apart: 2 -> 2, of which waited for: 1 -> 0; matrix products, arithmetic and copies ran while one was open for 34% -> 0% of each run, Pallas kernels for 0% -> 37%
where the time goes in v1:
time: 144 us; the launch traced here: 143 us
  Pallas kernels  117 us (81%)
  blocking collectives  13.3 us (9%)
  starting transfers between devices  7.23 us (5%)
  local copies, waits for them, and re-layouts  4.66 us (3%)
    pallas_call x1, Pallas kernels, remote_forces(): pl.pallas_call(remote_kernel, out_shape=(out, out), in_specs=[smem(), sme...  41.7 us
    pallas_call x1, Pallas kernels, local_forces(): pl.pallas_call(local_kernel, out_shape=jax.ShapeDtypeStruct((rows, LEAF),...  40.7 us
    pallas_call x1, Pallas kernels, regroup(): pl.pallas_call(functools.partial(regroup_kernel, n_sub, leaves), out_shap...  22.1 us
    all_to_all x1, blocking collectives, on_device(): near = lax.all_to_all(near, 'sub', split_axis=0, concat_axis=0, tiled=True)  13.3 us
    pallas_call x1, Pallas kernels, plan(): pl.pallas_call(functools.partial(plan_kernel, n_dom, leaves), out_shape=(...  11.1 us
    unnamed x18, local copies, waits for them, and re-layouts  4.66 us
    all_to_all x1, starting transfers between devices, on_device(): lax.all_to_all(packed, 'dom', split_axis=0, concat_axis=0, tiled=True)  3.85 us
    all_to_all x1, starting transfers between devices, on_device(): far = lax.all_to_all(far, 'sub', split_axis=0, concat_axis=0, tiled=True)  3.38 us
  transfers between devices with their start and end apart: 2, of which 0 were waited for; matrix products, arithmetic and copies ran while one was open for 0% of the time, Pallas kernels for 37%

profile of v1, /device:TPU:0, one launch (start us, length us, event | category | flops | bytes accessed | tf_op | source)
XLA Modules:
  0.0 143.1 jit_solution(16232495869812140121)
XLA Ops:
  0.6 0.0 copy-start
  0.6 0.9 copy-done
  1.5 0.0 copy-start.1
  1.5 0.9 copy-done.1
  2.4 0.0 copy-start.2
  2.4 0.8 copy-done.2
  3.2 0.0 copy-start.3
  3.2 0.8 copy-done.3
  4.0 22.1 %regroup.1 = (f32[8,40,128]{2,1,0:T(8,128)S(1)}, f32[8,40,128]{2,1,0:T(8,128)}) custom-call(f32[3,8192]{1,0:T(4,128)S(1)} %copy-done, f32[64,128]{1,0:T(8,128)S(1)} %bitcast.13, f32[3,8192]{1,0:T(4,128)S(1)} %copy-done.1, s32[64,128]{1,0:T(8,128)S(1)} %bitcast.14), custom_call_target="tpu_custom_call" | custom-call | tf_op jit(solution)/shard_map/regroup/pallas_call | solution.py:118
  26.0 13.3 %all_to_all.15 = f32[8,40,128]{2,1,0:T(8,128)S(1)} all-to-all(f32[8,40,128]{2,1,0:T(8,128)S(1)} %get-tuple-element.9), channel_id=1, replica_groups=mesh['dom'=4,'sub'=8] {'sub'}, dimensions={0} | all-to-all | bytes 327680 | tf_op jit(solution)/shard_map/all_to_all | solution.py:328
  39.4 3.4 %all-to-all-start.2 = ((f32[8,40,128]{2,1,0:T(8,128)}), f32[8,40,128]{2,1,0:T(8,128)S(1)}, u32[]{:S(2)}, u32[]{:S(2)}) async-start(f32[8,40,128]{2,1,0:T(8,128)} %get-tuple-element.11), calls=%async_computation.2 | async-start | bytes 327680 | tf_op jit(solution)/shard_map/all_to_all | solution.py:333
  42.8 11.1 %plan.1 = (s32[4,32]{1,0:T(4,128)}, s32[192]{0:T(256)}, f32[192]{0:T(256)}) custom-call(s32[4,4,80]{2,1,0:T(4,128)} %bitcast.15, s32[3,192]{1,0:T(4,128)} %ids_ref.3, s32[1]{0:T(128)} %bitcast.1.me_ref), custom_call_target="tpu_custom_call" | custom-call | tf_op jit(solution)/shard_map/plan/pallas_call | solution.py:179
  53.9 0.0 copy-start.5
  53.9 0.7 copy-done.5
  54.6 1.5 %bundle.1 = f32[4,32,4,128]{3,2,1,0:T(4,128)} custom-call(s32[4,32]{1,0:T(4,128)S(1)} %copy-done.5, f32[80,4,128]{2,1,0:T(4,128)S(1)} %bitcast.8), custom_call_target="tpu_custom_call" | custom-call | tf_op jit(solution)/shard_map/bundle/pallas_call | solution.py:206
  56.1 0.0 copy-start.6
  56.1 0.0 all-to-all-done.2
  56.1 3.9 %all-to-all-start.1 = ((f32[4,32,4,128]{3,2,1,0:T(4,128)}), f32[4,32,4,128]{3,2,1,0:T(4,128)S(1)}, u32[]{:S(2)}, u32[]{:S(2)}) async-start(f32[4,32,4,128]{3,2,1,0:T(4,128)} %bundle.1), calls=%async_computation.1 | async-start | bytes 524288 | tf_op jit(solution)/shard_map/all_to_all | solution.py:332
  60.0 0.0 copy-done.6
  60.0 0.0 copy-start.8
  60.0 40.7 %local_forces.1.local_ref = f32[320,128]{1,0:T(8,128)S(1)} custom-call(s32[2,192]{1,0:T(2,128)S(1)} %copy-done.6, f32[320,128]{1,0:T(8,128)S(1)} %bitcast.9), custom_call_target="tpu_custom_call" | custom-call | flops 56623104 | bytes 327680 | tf_op jit(solution)/shard_map/local_forces/pallas_call | solution.py:267
  100.7 0.0 copy-start.4
  100.7 0.0 all-to-all-done.1
  100.7 0.0 copy-start.7
  100.7 0.0 copy-done.8
  100.7 0.6 copy-done.4
  101.4 0.0 copy-done.7
  101.4 41.7 %remote_forces.1 = (f32[3,10240]{1,0:T(4,128)}, f32[3,10240]{1,0:T(4,128)}) custom-call(s32[3,192]{1,0:T(4,128)S(1)} %copy-done.4, s32[192]{0:T(256)S(1)} %copy-done.7, f32[192]{0:T(256)S(1)} %copy-done.8, f32[320,128]{1,0:T(8,128)S(1)} %bitcast.10, f32[512,128]{1,0:T(8,128)S(1)} %bitcast.11, f32[320,128]{1,0:T(8,128)S(1)} %local_forces.1.local_ref, ...), custom_call_target="tpu_custom_call" | custom-call | flops 56623104 | bytes 983040 | tf_op jit(solution)/shard_map/remote_forces/pallas_call | solution.py:306
Async XLA Ops:
  0.6 0.9 copy-start
  1.5 0.9 copy-start.1
  2.4 0.8 copy-start.2
  3.2 0.8 copy-start.3
  39.4 16.7 %all-to-all-start.2 = ((f32[8,40,128]{2,1,0:T(8,128)}), f32[8,40,128]{2,1,0:T(8,128)S(1)}, u32[]{:S(2)}, u32[]{:S(2)}) async-start(f32[8,40,128]{2,1,0:T(8,128)} %get-tuple-element.11), calls=%async_computation.2 | async-start | bytes 327680 | tf_op jit(solution)/shard_map/all_to_all | solution.py:333
  53.9 0.7 copy-start.5
  56.1 3.9 %copy-start.6 = (s32[2,192]{1,0:T(2,128)S(1)}, s32[2,192]{1,0:T(2,128)}, u32[]{:S(2)}) copy-start(s32[2,192]{1,0:T(2,128)} %ids_ref.2) | copy-start | bytes 4612
  56.1 44.6 %all-to-all-start.1 = ((f32[4,32,4,128]{3,2,1,0:T(4,128)}), f32[4,32,4,128]{3,2,1,0:T(4,128)S(1)}, u32[]{:S(2)}, u32[]{:S(2)}) async-start(f32[4,32,4,128]{3,2,1,0:T(4,128)} %bundle.1), calls=%async_computation.1 | async-start | bytes 524288 | tf_op jit(solution)/shard_map/all_to_all | solution.py:332
  60.0 40.8 %copy-start.8 = (f32[192]{0:T(256)S(1)}, f32[192]{0:T(256)}, u32[]{:S(2)}) copy-start(f32[192]{0:T(256)} %get-tuple-element.8.valid_ref) | copy-start | bytes 2308
  100.7 0.7 copy-start.4
  100.7 0.7 copy-start.7

commit v2 on v1

v2 whole, which is shorter than its diff:
```python
import functools

import jax
import jax.numpy as jnp
from jax import lax
from jax.experimental import pallas as pl
from jax.experimental.pallas import tpu as pltpu
from jax.sharding import PartitionSpec as P

SLOTS = 32
LEAF = 128
ROWS = 4 * SLOTS

softening = 0.01
gravity = 4.0
kick_time = 0.5

VMEM_LIMIT = 48 << 20
F32 = jnp.float32
I32 = jnp.int32
BF16 = jnp.bfloat16


def vmem():
    return pl.BlockSpec(memory_space=pltpu.VMEM)


def smem():
    return pl.BlockSpec(memory_space=pltpu.SMEM)


def anywhere():
    return pl.BlockSpec(memory_space=pl.ANY)


def params():
    return pltpu.CompilerParams(vmem_limit_bytes=VMEM_LIMIT)


def lane_gather(tile, index):
    return jnp.take_along_axis(tile, index, axis=1, mode="promise_in_bounds")


def iota(shape, dim):
    return lax.broadcasted_iota(I32, shape, dim)


def as_bf16(condition):
    return jnp.where(condition, 1.0, 0.0).astype(BF16)


def plan_reads(n_dom, reads_ref, list_ref, lookup_ref):
    me = lax.axis_index("dom")
    leaves = reads_ref.shape[2]
    lower = as_bf16(iota((leaves, leaves), 0) < iota((leaves, leaves), 1))
    wanted = jnp.concatenate([reads_ref[p, pl.ds(me, 1), :] for p in range(n_dom)], axis=0)
    flags = jnp.concatenate([wanted, reads_ref[me]], axis=0).astype(F32)
    place = jnp.dot(flags.astype(BF16), lower, preferred_element_type=F32).astype(I32)
    lookup_ref[...] = jnp.minimum(place[n_dom:], SLOTS - 1)
    slot = iota((SLOTS, leaves), 0)
    leaf = iota((SLOTS, leaves), 1)
    lane = iota((SLOTS, LEAF), 1)
    lists = jnp.zeros((SLOTS, LEAF), I32)
    for p in range(n_dom):
        hit = (place[p:p + 1] == slot) & (wanted[p:p + 1] > 0)
        lists = jnp.where(lane == p, jnp.sum(jnp.where(hit, leaf, 0), axis=1, keepdims=True), lists)
    list_ref[...] = lists


def regroup_kernel(
    n_sub, n_dom, leaves, pos_hbm, mass_hbm, vel_hbm, dest_hbm, reads_ref,
    near_ref, far_ref, list_ref, lookup_ref,
    pos_ref, mass_ref, vel_ref, dest_ref, tiles, table, ordered,
    off_ref, cnt_ref, start_ref, perm_ref, leaf_vec, leaf_idx, sems
):
    blocks = dest_ref.shape[0]
    loads = [
        pltpu.make_async_copy(source, target, sems.at[n])
        for n, (source, target) in enumerate(
            [(dest_hbm, dest_ref), (pos_hbm, pos_ref), (mass_hbm, mass_ref), (vel_hbm, vel_ref)]
        )
    ]
    for load in loads:
        load.start()
    plan_reads(n_dom, reads_ref, list_ref, lookup_ref)
    tiles[...] = jnp.zeros_like(tiles)
    row = iota((LEAF, LEAF), 0)
    weights = jnp.concatenate([as_bf16(row <= iota((LEAF, LEAF), 1)), jnp.ones((LEAF, LEAF), BF16)], axis=1)
    earlier = as_bf16(iota((blocks, blocks), 1) < iota((blocks, blocks), 0))
    lane64 = iota((blocks, LEAF), 1)
    loads[0].wait()
    dest = dest_ref[...]
    masks = [dest == e for e in range(n_sub)]
    ones_of = jnp.concatenate([as_bf16(m) for m in masks], axis=0)
    counts = jnp.dot(ones_of, weights, preferred_element_type=F32)
    start = jnp.zeros((blocks, LEAF), F32)
    place = jnp.zeros((blocks, LEAF), F32)
    leaf_of = jnp.zeros((blocks, LEAF), I32)
    for e in range(n_sub):
        inside = counts[e * blocks:(e + 1) * blocks, :LEAF]
        total = counts[e * blocks:(e + 1) * blocks, LEAF:]
        place = jnp.where(masks[e], inside - 1.0 + start, place)
        offset = jnp.dot(earlier, total.astype(BF16), preferred_element_type=F32).astype(I32)
        count = total.astype(I32)
        off_ref[e] = offset
        cnt_ref[e] = count
        start_ref[e] = start.astype(I32)
        base = e * (leaves + 1)
        leaf_of = jnp.where(lane64 == e, base + (offset >> 7), leaf_of)
        leaf_of = jnp.where(lane64 == n_sub + e, base + ((offset + count) >> 7), leaf_of)
        start = start + total
    leaf_vec[...] = leaf_of
    copy = pltpu.make_async_copy(leaf_vec, leaf_idx, sems.at[4])
    copy.start()
    perm_ref[...] = place.astype(I32)
    for load in loads[1:]:
        load.wait()
    table[:, 7:8, :] = jnp.zeros((blocks, 1, LEAF), F32)
    for b in range(blocks):
        lanes = slice(b * LEAF, (b + 1) * LEAF)
        table[b, 0:3, :] = pos_ref[:, lanes]
        table[b, 3:4, :] = mass_ref[b:b + 1, :]
        table[b, 4:7, :] = vel_ref[:, lanes]
    lane = iota((8, LEAF), 1)
    lane_rows = iota((16, LEAF), 1).astype(F32).astype(BF16)

    def order(b, _):
        onehot = as_bf16(row == perm_ref[pl.ds(b, 1), :])
        inverse = lax.dot_general(
            lane_rows, onehot, (((1,), (1,)), ((), ())), preferred_element_type=F32
        )[:8].astype(I32)
        ordered[b] = lane_gather(table[b], inverse)
        return 0

    lax.fori_loop(0, blocks, order, 0, unroll=8)
    copy.wait()

    def step(b, tails):
        block = ordered[b]
        new = []
        for e in range(n_sub):
            offset = jnp.broadcast_to(off_ref[e, pl.ds(b, 1), :], (8, LEAF))
            count = jnp.broadcast_to(cnt_ref[e, pl.ds(b, 1), :], (8, LEAF))
            first = jnp.broadcast_to(start_ref[e, pl.ds(b, 1), :], (8, LEAF))
            turned = (lane - offset) & (LEAF - 1)
            moved = lane_gather(block, (turned + first) & (LEAF - 1))
            low = offset & (LEAF - 1)
            taken = turned < count
            tail = jnp.where(taken & (lane >= low), moved, tails[e])
            tiles[leaf_idx[b, e]] = tail
            fresh = jnp.where(taken & (lane < low), moved, 0.0)
            new.append(jnp.where(low + count >= LEAF, fresh, tail))
        return tuple(new)

    tails = lax.fori_loop(0, blocks, step, (jnp.zeros((8, LEAF), F32),) * n_sub, unroll=4)
    for e in range(n_sub):
        tiles[leaf_idx[blocks - 1, n_sub + e]] = tails[e]
        for l in range(leaves):
            tile = tiles[e * (leaves + 1) + l]
            near_ref[e, 4 * l:4 * l + 4, :] = tile[0:4]
            far_ref[e, 4 * l:4 * l + 4, :] = tile[4:8]


def regroup(positions, masses, velocities, destinations, reads, n_sub, leaves):
    count = positions.shape[1]
    blocks = count // LEAF
    n_dom = reads.shape[0]
    out = jax.ShapeDtypeStruct((n_sub, leaves * 4, LEAF), F32)
    return pl.pallas_call(
        functools.partial(regroup_kernel, n_sub, n_dom, leaves),
        out_shape=(
            out,
            out,
            jax.ShapeDtypeStruct((SLOTS, LEAF), I32),
            jax.ShapeDtypeStruct((n_dom, reads.shape[2]), I32),
        ),
        in_specs=[anywhere()] * 4 + [vmem()],
        out_specs=(vmem(),) * 4,
        scratch_shapes=[
            pltpu.VMEM((3, count), F32),
            pltpu.VMEM((blocks, LEAF), F32),
            pltpu.VMEM((3, count), F32),
            pltpu.VMEM((blocks, LEAF), I32),
            pltpu.VMEM((n_sub * (leaves + 1), 8, LEAF), F32),
            pltpu.VMEM((blocks, 8, LEAF), F32),
            pltpu.VMEM((blocks, 8, LEAF), F32),
            pltpu.VMEM((n_sub, blocks, LEAF), I32),
            pltpu.VMEM((n_sub, blocks, LEAF), I32),
            pltpu.VMEM((n_sub, blocks, LEAF), I32),
            pltpu.VMEM((blocks, LEAF), I32),
            pltpu.VMEM((blocks, LEAF), I32),
            pltpu.SMEM((blocks, LEAF), I32),
            pltpu.SemaphoreType.DMA((5,)),
        ],
        compiler_params=params(),
        name="regroup",
    )(positions, masses.reshape(blocks, LEAF), velocities, destinations.reshape(blocks, LEAF), reads)


def bundle_kernel(n_dom, list_ref, leaf_hbm, *rest):
    outs, sems = rest[:n_dom - 1], rest[n_dom - 1]
    me = lax.axis_index("dom")
    for k in range(1, n_dom):
        for slot in range(SLOTS):
            leaf = list_ref[slot, me ^ k]
            pltpu.make_async_copy(leaf_hbm.at[leaf], outs[k - 1].at[slot], sems.at[k - 1]).start()
    for k in range(1, n_dom):
        pltpu.make_async_copy(outs[k - 1], outs[k - 1], sems.at[k - 1]).wait()


def bundle(lists, near, n_dom):
    return pl.pallas_call(
        functools.partial(bundle_kernel, n_dom),
        out_shape=(jax.ShapeDtypeStruct((SLOTS, 4, LEAF), F32),) * (n_dom - 1),
        in_specs=[smem(), anywhere()],
        out_specs=(anywhere(),) * (n_dom - 1),
        scratch_shapes=[pltpu.SemaphoreType.DMA((n_dom - 1,))],
        compiler_params=params(),
        name="bundle",
    )(lists, near)


def spread_sources(src_refs, wide_ref):
    group = iota((8, LEAF), 1) & ~15

    def spread(k, _):
        h = 0
        for src_ref in src_refs:
            for r in range(0, src_ref.shape[0], 8):
                wide_ref[k, h] = lane_gather(src_ref[r:r + 8, :], group + k)
                h += 1
        return 0

    lax.fori_loop(0, 16, spread, 0)


def pair_loop(pairs, target_of, source_of, weight_of, here_ref, wide_ref, acc_ref):
    def step(i, _):
        t = target_of(i)
        s = source_of(i)
        h, first = s >> 1, (s & 1) * 4
        here = [here_ref[t, c] for c in range(3)]
        sums = None
        for k in range(16):
            there = [jnp.broadcast_to(wide_ref[k, h, pl.ds(first + c, 1), :], (8, LEAF)) for c in range(4)]
            delta = [there[c] - here[c] for c in range(3)]
            dist = delta[0] * delta[0] + delta[1] * delta[1] + (delta[2] * delta[2] + softening)
            inv = lax.rsqrt(dist)
            weight = (there[3] * inv) * (inv * inv)
            terms = [weight * delta[c] for c in range(3)]
            sums = terms if sums is None else [sums[c] + terms[c] for c in range(3)]
        scale = weight_of(i)
        for c in range(3):
            acc_ref[t, c] += sums[c] if scale is None else sums[c] * scale
        return 0

    lax.fori_loop(0, pairs, step, 0, unroll=4)


def local_kernel(ids_ref, src_ref, acc_ref, here_ref, wide_ref):
    spread_sources([src_ref], wide_ref)
    leaves = acc_ref.shape[0]
    fold = iota((8, LEAF), 0) * 16 + (iota((8, LEAF), 1) & 15)
    batch = 8 if leaves % 8 == 0 else 1

    def pack(j, _):
        for u in range(batch):
            for c in range(3):
                line = src_ref[pl.ds(4 * (j * batch + u) + c, 1), :]
                here_ref[j * batch + u, c] = lane_gather(jnp.broadcast_to(line, (8, LEAF)), fold)
        return 0

    lax.fori_loop(0, leaves // batch, pack, 0)
    acc_ref[...] = jnp.zeros_like(acc_ref)
    pair_loop(
        ids_ref.shape[1], lambda i: ids_ref[0, i], lambda i: ids_ref[1, i], lambda i: None,
        here_ref, wide_ref, acc_ref,
    )


def local_forces(near_local, near):
    rows = near.shape[0]
    leaves = rows // 4
    work = near_local.shape[1] * LEAF * LEAF
    return pl.pallas_call(
        local_kernel,
        out_shape=(
            jax.ShapeDtypeStruct((leaves, 4, 8, LEAF), F32),
            jax.ShapeDtypeStruct((leaves, 3, 8, LEAF), F32),
        ),
        in_specs=[smem(), vmem()],
        out_specs=(vmem(), vmem()),
        scratch_shapes=[pltpu.VMEM((16, rows // 8, 8, LEAF), F32)],
        compiler_params=params(),
        cost_estimate=pl.CostEstimate(flops=18 * work, transcendentals=work, bytes_accessed=8 * rows * LEAF),
        name="local_forces",
    )(near_local, near)


def three_parts(x):
    high = x.astype(BF16)
    rest = x - high.astype(F32)
    middle = rest.astype(BF16)
    return [high, middle, (rest - middle.astype(F32)).astype(BF16)]


def unpack_sums(acc_refs, leaves):
    source, target = iota((LEAF, LEAF), 0), iota((LEAF, LEAF), 1)
    parts, picks = [], []
    for s in range(8):
        lines = [ref.reshape(leaves * 32, LEAF)[pl.ds(s, leaves * 4, stride=8), :] for ref in acc_refs]
        pick = as_bf16(((source & 15) == (target & 15)) & ((target >> 4) == s))
        parts += three_parts(sum(lines[1:], lines[0]))
        picks += [pick] * 3
    return jnp.dot(
        jnp.concatenate(parts, axis=1), jnp.concatenate(picks, axis=0), preferred_element_type=F32
    )


def remote_kernel(n_dom, ids_ref, lookup_ref, reads_ref, tgt_ref, vel_ref, local_ref, here_ref, *rest):
    src_refs = rest[:n_dom - 1]
    accel_ref, kicked_ref, wide_ref, acc_ref = rest[n_dom - 1:]
    me = lax.axis_index("dom")
    spread_sources(src_refs, wide_ref)
    acc_ref[...] = jnp.zeros_like(acc_ref)

    def source_of(i):
        q = ids_ref[1, i]
        return jnp.maximum((q ^ me) - 1, 0) * SLOTS + lookup_ref[q, ids_ref[2, i]]

    def weight_of(i):
        return reads_ref[me, ids_ref[1, i], ids_ref[2, i]].astype(F32)

    pair_loop(ids_ref.shape[1], lambda i: ids_ref[0, i], source_of, weight_of, here_ref, wide_ref, acc_ref)
    leaves = acc_ref.shape[0]
    total = gravity * unpack_sums([local_ref, acc_ref], leaves)
    first = iota((8, LEAF), 0) < 4
    for h in range(leaves // 2):
        rows = slice(8 * h, 8 * h + 8)
        mass = [jnp.broadcast_to(tgt_ref[8 * h + r:8 * h + r + 1, :], (8, LEAF)) for r in (3, 7)]
        accel = jnp.where(jnp.where(first, mass[0], mass[1]) > 0.0, total[rows], 0.0)
        kicked = vel_ref[rows, :] + kick_time * accel
        for u in range(2):
            lanes = slice((2 * h + u) * LEAF, (2 * h + u + 1) * LEAF)
            accel_ref[:, lanes] = accel[4 * u:4 * u + 3]
            kicked_ref[:, lanes] = kicked[4 * u:4 * u + 3]


def remote_forces(near_remote, lookup, reads, near, vel, local, here, arrived):
    n_dom = reads.shape[0]
    rows = near.shape[0]
    leaves = rows // 4
    work = near_remote.shape[1] * LEAF * LEAF
    out = jax.ShapeDtypeStruct((3, leaves * LEAF), F32)
    return pl.pallas_call(
        functools.partial(remote_kernel, n_dom),
        out_shape=(out, out),
        in_specs=[smem()] * 3 + [vmem()] * (3 + n_dom),
        out_specs=(vmem(), vmem()),
        scratch_shapes=[
            pltpu.VMEM((16, (n_dom - 1) * ROWS // 8, 8, LEAF), F32),
            pltpu.VMEM((leaves, 4, 8, LEAF), F32),
        ],
        compiler_params=params(),
        cost_estimate=pl.CostEstimate(flops=18 * work, transcendentals=work, bytes_accessed=24 * rows * LEAF),
        name="remote_forces",
    )(near_remote, lookup, reads, near, vel, local, here, *arrived)


def on_device(positions, masses, velocities, destinations, readers, near_local, near_remote):
    n_sub = lax.axis_size("sub")
    n_dom = lax.axis_size("dom")
    count = positions.shape[1]
    capacity = 5 * count // (4 * n_sub)
    leaves = capacity // LEAF
    reads = readers.reshape(n_dom, n_dom, readers.shape[3])
    near, far, lists, lookup = regroup(positions, masses, velocities, destinations, reads, n_sub, leaves)
    near = lax.all_to_all(near, "sub", split_axis=0, concat_axis=0, tiled=True)
    packed = bundle(lists, near.reshape(n_sub * leaves, 4, LEAF), n_dom)
    arrived = [
        lax.ppermute(packed[k - 1], "dom", [(i, i ^ k) for i in range(n_dom)]).reshape(ROWS, LEAF)
        for k in range(1, n_dom)
    ]
    far = lax.all_to_all(far, "sub", split_axis=0, concat_axis=0, tiled=True)
    near = near.reshape(n_sub * leaves * 4, LEAF)
    local, here = local_forces(near_local, near)
    return remote_forces(
        near_remote, lookup, reads, near, far.reshape(n_sub * leaves * 4, LEAF), local, here, arrived
    )


def solution(mesh):
    in_specs = (
        P(None, ("dom", "sub")),
        P(("dom", "sub")),
        P(None, ("dom", "sub")),
        P(("dom", "sub"), None),
        P(None, None, "sub", None),
        P(None, ("dom", "sub")),
        P(None, ("dom", "sub")),
    )
    out_specs = (P(None, ("dom", "sub")), P(None, ("dom", "sub")))
    return jax.shard_map(
        on_device, mesh=mesh, in_specs=in_specs, out_specs=out_specs, check_vma=False
    )
```

time: 144 us -> 59.7 us (0.41)
  Pallas kernels: 117 us -> 33.5 us
    pallas_call x5 -> x4, Pallas kernels: 117 us -> 33.5 us  [the longest x1 13.1 us: remote_forces(): pl.pallas_call(functools.partial(remote_kernel, n_dom), out_shape=(out, o...]
    all_to_all x1 -> x0, starting transfers between devices: 3.85 us -> none  [on_device(): lax.all_to_all(packed, 'dom', split_axis=0, concat_axis=0, tiled=True)]
    ppermute x0 -> x3, starting transfers between devices: none -> 3.55 us  [on_device(): lax.ppermute(packed[k - 1], 'dom', [(i, i ^ k) for i in range(n_dom)])]
    unnamed x18 -> x16, local copies, waits for them, and re-layouts: 4.66 us -> 4.7 us
  transfers between devices with their start and end apart: 2 -> 4, of which waited for: 0 -> 0; matrix products, arithmetic and copies ran while one was open for 0% -> 0% of each run, Pallas kernels for 37% -> 22%
where the time goes in v2:
time: 59.7 us; the launch traced here: 59.2 us
  Pallas kernels  33.5 us (56%)
  blocking collectives  13.3 us (22%)
  starting transfers between devices  6.94 us (12%)
  local copies, waits for them, and re-layouts  4.7 us (8%)
  between operations  0.72 us (1%)
    all_to_all x1, blocking collectives, on_device(): near = lax.all_to_all(near, 'sub', split_axis=0, concat_axis=0, tiled=True)  13.3 us
    pallas_call x1, Pallas kernels, remote_forces(): pl.pallas_call(functools.partial(remote_kernel, n_dom), out_shape=(out, o...  13.1 us
    pallas_call x1, Pallas kernels, local_forces(): pl.pallas_call(local_kernel, out_shape=(jax.ShapeDtypeStruct((leaves, 4,...  11.8 us
    pallas_call x1, Pallas kernels, regroup(): pl.pallas_call(functools.partial(regroup_kernel, n_sub, n_dom, leaves), o...  7.15 us
    unnamed x16, local copies, waits for them, and re-layouts  4.7 us
    ppermute x3, starting transfers between devices, on_device(): lax.ppermute(packed[k - 1], 'dom', [(i, i ^ k) for i in range(n_dom)])  3.55 us
    all_to_all x1, starting transfers between devices, on_device(): far = lax.all_to_all(far, 'sub', split_axis=0, concat_axis=0, tiled=True)  3.38 us
    pallas_call x1, Pallas kernels, bundle(): pl.pallas_call(functools.partial(bundle_kernel, n_dom), out_shape=(jax.Sh...  1.45 us
  transfers between devices with their start and end apart: 4, of which 0 were waited for; matrix products, arithmetic and copies ran while one was open for 0% of the time, Pallas kernels for 22%

profile of v2, /device:TPU:0, one launch (start us, length us, event | category | flops | bytes accessed | tf_op | source)
XLA Modules:
  0.0 59.2 jit_solution(16379900422252750117)
XLA Ops:
  0.6 0.0 copy-start
  0.6 0.9 %copy-done = f32[3,8192]{1,0:T(4,128)S(1)} copy-done((f32[3,8192]{1,0:T(4,128)S(1)}, f32[3,8192]{1,0:T(4,128)}, u32[]{:S(2)}) %copy-start) | copy-done | bytes 98328
  1.5 0.0 copy-start.1
  1.5 0.9 %copy-done.1 = f32[3,8192]{1,0:T(4,128)S(1)} copy-done((f32[3,8192]{1,0:T(4,128)S(1)}, f32[3,8192]{1,0:T(4,128)}, u32[]{:S(2)}) %copy-start.1) | copy-done | bytes 98328
  2.4 0.0 copy-start.2
  2.4 0.8 %copy-done.2 = f32[8192]{0:T(1024)S(1)} copy-done((f32[8192]{0:T(1024)S(1)}, f32[8192]{0:T(1024)}, u32[]{:S(2)}) %copy-start.2) | copy-done | bytes 32792
  3.2 0.0 copy-start.3
  3.2 0.8 %copy-done.3 = s32[8192,1]{0,1:T(1,128)S(1)} copy-done((s32[8192,1]{0,1:T(1,128)S(1)}, s32[8192,1]{0,1:T(1,128)}, u32[]{:S(2)}) %copy-start.3) | copy-done | bytes 32792
  4.0 0.0 copy-start.4
  4.0 0.7 %copy-done.4 = s32[4,4,1,80]{3,2,1,0:T(1,128)S(1)} copy-done((s32[4,4,1,80]{3,2,1,0:T(1,128)S(1)}, s32[4,4,1,80]{3,2,1,0:T(1,128)}, u32[]{:S(2)}) %copy-start.4) | copy-done | bytes 5144
  4.7 7.2 %regroup.1 = (f32[8,40,128]{2,1,0:T(8,128)S(1)}, f32[8,40,128]{2,1,0:T(8,128)}, s32[32,128]{1,0:T(8,128)S(1)}, s32[4,80]{1,0:T(4,128)S(1)}) custom-call(f32[3,8192]{1,0:T(4,128)S(1)} %copy-done, f32[64,128]{1,0:T(8,128)S(1)} %bitcast.13, f32[3,8192]{1,0:T(4,128)S(1)} %copy-done.1, s32[64,128]{1,0:T(8,128)S(1)} %bitcast.14, s32[4,4,80]{2,1,0:T(4,128)S(1)} %bitcast.15), custom_call_target="tpu_custom_call" | custom-call | tf_op jit(solution)/shard_map/regroup/pallas_call | solution.py:169
  11.8 13.3 %all_to_all.10 = f32[8,40,128]{2,1,0:T(8,128)S(1)} all-to-all(f32[8,40,128]{2,1,0:T(8,128)S(1)} %get-tuple-element.12), channel_id=1, replica_groups=mesh['dom'=4,'sub'=8] {'sub'}, dimensions={0} | all-to-all | bytes 327680 | tf_op jit(solution)/shard_map/all_to_all | solution.py:378
  25.2 3.4 %all-to-all-start.1 = ((f32[8,40,128]{2,1,0:T(8,128)}), f32[8,40,128]{2,1,0:T(8,128)S(1)}, u32[]{:S(2)}, u32[]{:S(2)}) async-start(f32[8,40,128]{2,1,0:T(8,128)} %get-tuple-element.13), calls=%async_computation.1 | async-start | bytes 327680 | tf_op jit(solution)/shard_map/all_to_all | solution.py:384
  28.5 1.5 %bundle.1 = (f32[32,4,128]{2,1,0:T(4,128)S(1)}, f32[32,4,128]{2,1,0:T(4,128)S(1)}, f32[32,4,128]{2,1,0:T(4,128)S(1)}) custom-call(s32[32,128]{1,0:T(8,128)S(1)} %get-tuple-element.16.list_ref, f32[80,4,128]{2,1,0:T(4,128)S(1)} %bitcast.9), custom_call_target="tpu_custom_call" | custom-call | tf_op jit(solution)/shard_map/bundle/pallas_call | solution.py:212
  30.0 1.6 %collective-permute-start = (f32[32,4,128]{2,1,0:T(4,128)S(1)}, f32[32,4,128]{2,1,0:T(4,128)S(1)}, u32[]{:S(2)}, u32[]{:S(2)}) collective-permute-start(f32[32,4,128]{2,1,0:T(4,128)S(1)} %get-tuple-element.17), channel_id=1, source_target_pairs={{0,8},{8,0},{16,24},{24,16},{1,9},{9,1},{17,25},{25,17},{2,10},{10... | collective-permute-start | bytes 196616 | tf_op jit(solution)/shard_map/ppermute | solution.py:381
  31.6 1.5 %collective-permute-start.1 = (f32[32,4,128]{2,1,0:T(4,128)S(1)}, f32[32,4,128]{2,1,0:T(4,128)S(1)}, u32[]{:S(2)}, u32[]{:S(2)}) collective-permute-start(f32[32,4,128]{2,1,0:T(4,128)S(1)} %get-tuple-element.18), channel_id=1, source_target_pairs={{0,16},{8,24},{16,0},{24,8},{1,17},{9,25},{17,1},{25,9},{2,18},{10... | collective-permute-start | bytes 196616 | tf_op jit(solution)/shard_map/ppermute | solution.py:381
  33.1 0.5 collective-permute-start.2
  33.6 0.0 copy-start.7
  33.6 0.7 %copy-done.7 = s32[2,192]{1,0:T(2,128)S(1)} copy-done((s32[2,192]{1,0:T(2,128)S(1)}, s32[2,192]{1,0:T(2,128)}, u32[]{:S(2)}) %copy-start.7) | copy-done | bytes 1560
  34.2 0.0 copy-start.5
  34.2 0.0 copy-start.6
  34.2 11.8 %local_forces.1 = (f32[80,4,8,128]{3,2,1,0:T(8,128)S(1)}, f32[80,3,8,128]{3,2,1,0:T(8,128)S(1)}) custom-call(s32[2,192]{1,0:T(2,128)S(1)} %copy-done.7, f32[320,128]{1,0:T(8,128)S(1)} %bitcast.10), custom_call_target="tpu_custom_call" | custom-call | flops 56623104 | bytes 327680 | tf_op jit(solution)/shard_map/local_forces/pallas_call | solution.py:285
  46.0 0.0 all-to-all-done.1
  46.1 0.0 collective-permute-done
  46.1 0.0 collective-permute-done.1
  46.1 0.0 collective-permute-done.2
  46.1 0.0 copy-done.5
  46.1 0.0 copy-done.6
  46.1 13.1 %remote_forces.1 = (f32[3,10240]{1,0:T(4,128)}, f32[3,10240]{1,0:T(4,128)}) custom-call(s32[3,192]{1,0:T(4,128)S(1)} %copy-done.6, s32[4,80]{1,0:T(4,128)S(1)} %get-tuple-element.11.lookup_ref, s32[4,4,80]{2,1,0:T(4,128)S(1)} %bitcast.16, f32[320,128]{1,0:T(8,128)S(1)} %bitcast.11, f32[320,128]{1,0:T(8,128)S(1)} %bitcast.12, ...), custom_call_target="tpu_custom_call" | custom-call | flops 56623104 | bytes 983040 | tf_op jit(solution)/shard_map/remote_forces/pallas_call | solution.py:355
Async XLA Ops:
  0.6 0.9 %copy-start = (f32[3,8192]{1,0:T(4,128)S(1)}, f32[3,8192]{1,0:T(4,128)}, u32[]{:S(2)}) copy-start(f32[3,8192]{1,0:T(4,128)} %pos_hbm.1) | copy-start | bytes 294916
  1.5 0.9 %copy-start.1 = (f32[3,8192]{1,0:T(4,128)S(1)}, f32[3,8192]{1,0:T(4,128)}, u32[]{:S(2)}) copy-start(f32[3,8192]{1,0:T(4,128)} %vel_hbm.1) | copy-start | bytes 294916
  2.4 0.8 %copy-start.2 = (f32[8192]{0:T(1024)S(1)}, f32[8192]{0:T(1024)}, u32[]{:S(2)}) copy-start(f32[8192]{0:T(1024)} %param.8) | copy-start | bytes 98308
  3.2 0.8 %copy-start.3 = (s32[8192,1]{0,1:T(1,128)S(1)}, s32[8192,1]{0,1:T(1,128)}, u32[]{:S(2)}) copy-start(s32[8192,1]{0,1:T(1,128)} %param.10) | copy-start | bytes 98308
  4.0 0.7 %copy-start.4 = (s32[4,4,1,80]{3,2,1,0:T(1,128)S(1)}, s32[4,4,1,80]{3,2,1,0:T(1,128)}, u32[]{:S(2)}) copy-start(s32[4,4,1,80]{3,2,1,0:T(1,128)} %param.11) | copy-start | bytes 15364
  25.2 20.9 %all-to-all-start.1 = ((f32[8,40,128]{2,1,0:T(8,128)}), f32[8,40,128]{2,1,0:T(8,128)S(1)}, u32[]{:S(2)}, u32[]{:S(2)}) async-start(f32[8,40,128]{2,1,0:T(8,128)} %get-tuple-element.13), calls=%async_computation.1 | async-start | bytes 327680 | tf_op jit(solution)/shard_map/all_to_all | solution.py:384
  30.0 16.0 %collective-permute-start = (f32[32,4,128]{2,1,0:T(4,128)S(1)}, f32[32,4,128]{2,1,0:T(4,128)S(1)}, u32[]{:S(2)}, u32[]{:S(2)}) collective-permute-start(f32[32,4,128]{2,1,0:T(4,128)S(1)} %get-tuple-element.17), channel_id=1, source_target_pairs={{0,8},{8,0},{16,24},{24,16},{1,9},{9,1},{17,25},{25,17},{2,10},{10... | collective-permute-start | bytes 196616 | tf_op jit(solution)/shard_map/ppermute | solution.py:381
  31.6 14.5 %collective-permute-start.1 = (f32[32,4,128]{2,1,0:T(4,128)S(1)}, f32[32,4,128]{2,1,0:T(4,128)S(1)}, u32[]{:S(2)}, u32[]{:S(2)}) collective-permute-start(f32[32,4,128]{2,1,0:T(4,128)S(1)} %get-tuple-element.18), channel_id=1, source_target_pairs={{0,16},{8,24},{16,0},{24,8},{1,17},{9,25},{17,1},{25,9},{2,18},{10... | collective-permute-start | bytes 196616 | tf_op jit(solution)/shard_map/ppermute | solution.py:381
  33.1 13.0 %collective-permute-start.2 = (f32[32,4,128]{2,1,0:T(4,128)S(1)}, f32[32,4,128]{2,1,0:T(4,128)S(1)}, u32[]{:S(2)}, u32[]{:S(2)}) collective-permute-start(f32[32,4,128]{2,1,0:T(4,128)S(1)} %get-tuple-element.19), channel_id=1, source_target_pairs={{0,24},{8,16},{16,8},{24,0},{1,25},{9,17},{17,9},{25,1},{2,26},{10... | collective-permute-start | bytes 196616 | tf_op jit(solution)/shard_map/ppermute | solution.py:381
  33.6 0.7 %copy-start.7 = (s32[2,192]{1,0:T(2,128)S(1)}, s32[2,192]{1,0:T(2,128)}, u32[]{:S(2)}) copy-start(s32[2,192]{1,0:T(2,128)} %ids_ref.2) | copy-start | bytes 4612
  34.2 11.8 %copy-start.5 = (s32[4,4,1,80]{3,2,1,0:T(1,128)S(1)}, s32[4,4,1,80]{3,2,1,0:T(1,128)}, u32[]{:S(2)}) copy-start(s32[4,4,1,80]{3,2,1,0:T(1,128)} %param.11) | copy-start | bytes 15364
  34.2 11.9 %copy-start.6 = (s32[3,192]{1,0:T(4,128)S(1)}, s32[3,192]{1,0:T(4,128)}, u32[]{:S(2)}) copy-start(s32[3,192]{1,0:T(4,128)} %ids_ref.3) | copy-start | bytes 6916

commit v3 on v2

--- a/solution.py
+++ b/solution.py
@@ -9,7 +9,6 @@
 
 SLOTS = 32
 LEAF = 128
-ROWS = 4 * SLOTS
 
 softening = 0.01
 gravity = 4.0
@@ -29,8 +28,12 @@
     return pl.BlockSpec(memory_space=pltpu.SMEM)
 
 
-def anywhere():
-    return pl.BlockSpec(memory_space=pl.ANY)
+def hbm():
+    return pl.BlockSpec(memory_space=pltpu.HBM)
+
+
+def in_hbm(*arrays):
+    return [pltpu.with_memory_space_constraint(x, pltpu.MemorySpace.HBM) for x in arrays]
 
 
 def params():
@@ -50,39 +53,37 @@
 
 
 def plan_reads(n_dom, reads_ref, list_ref, lookup_ref):
-    me = lax.axis_index("dom")
     leaves = reads_ref.shape[2]
     lower = as_bf16(iota((leaves, leaves), 0) < iota((leaves, leaves), 1))
-    wanted = jnp.concatenate([reads_ref[p, pl.ds(me, 1), :] for p in range(n_dom)], axis=0)
-    flags = jnp.concatenate([wanted, reads_ref[me]], axis=0).astype(F32)
-    place = jnp.dot(flags.astype(BF16), lower, preferred_element_type=F32).astype(I32)
-    lookup_ref[...] = jnp.minimum(place[n_dom:], SLOTS - 1)
+    wanted = reads_ref[lax.axis_index("dom")]
+    flags = wanted.astype(F32).astype(BF16)
+    place = jnp.dot(flags, lower, preferred_element_type=F32).astype(I32)
+    lookup_ref[...] = jnp.minimum(place, SLOTS - 1)
     slot = iota((SLOTS, leaves), 0)
     leaf = iota((SLOTS, leaves), 1)
     lane = iota((SLOTS, LEAF), 1)
     lists = jnp.zeros((SLOTS, LEAF), I32)
-    for p in range(n_dom):
-        hit = (place[p:p + 1] == slot) & (wanted[p:p + 1] > 0)
-        lists = jnp.where(lane == p, jnp.sum(jnp.where(hit, leaf, 0), axis=1, keepdims=True), lists)
+    for q in range(n_dom):
+        hit = (place[q:q + 1] == slot) & (wanted[q:q + 1] > 0)
+        lists = jnp.where(lane == q, jnp.sum(jnp.where(hit, leaf, 0), axis=1, keepdims=True), lists)
     list_ref[...] = lists
 
 
 def regroup_kernel(
-    n_sub, n_dom, leaves, pos_hbm, mass_hbm, vel_hbm, dest_hbm, reads_ref,
+    n_sub, n_dom, leaves, pos_hbm, mass_hbm, vel_hbm, dest_hbm, reads_hbm,
     near_ref, far_ref, list_ref, lookup_ref,
-    pos_ref, mass_ref, vel_ref, dest_ref, tiles, table, ordered,
+    pos_ref, mass_ref, vel_ref, dest_ref, reads_ref, tiles, table, ordered,
     off_ref, cnt_ref, start_ref, perm_ref, leaf_vec, leaf_idx, sems
 ):
     blocks = dest_ref.shape[0]
     loads = [
         pltpu.make_async_copy(source, target, sems.at[n])
         for n, (source, target) in enumerate(
-            [(dest_hbm, dest_ref), (pos_hbm, pos_ref), (mass_hbm, mass_ref), (vel_hbm, vel_ref)]
+            [(dest_hbm, dest_ref), (reads_hbm, reads_ref), (pos_hbm, pos_ref), (mass_hbm, mass_ref), (vel_hbm, vel_ref)]
         )
     ]
     for load in loads:
         load.start()
-    plan_reads(n_dom, reads_ref, list_ref, lookup_ref)
     tiles[...] = jnp.zeros_like(tiles)
     row = iota((LEAF, LEAF), 0)
     weights = jnp.concatenate([as_bf16(row <= iota((LEAF, LEAF), 1)), jnp.ones((LEAF, LEAF), BF16)], axis=1)
@@ -110,11 +111,12 @@
         leaf_of = jnp.where(lane64 == n_sub + e, base + ((offset + count) >> 7), leaf_of)
         start = start + total
     leaf_vec[...] = leaf_of
-    copy = pltpu.make_async_copy(leaf_vec, leaf_idx, sems.at[4])
+    copy = pltpu.make_async_copy(leaf_vec, leaf_idx, sems.at[5])
     copy.start()
     perm_ref[...] = place.astype(I32)
     for load in loads[1:]:
         load.wait()
+    plan_reads(n_dom, reads_ref, list_ref, lookup_ref)
     table[:, 7:8, :] = jnp.zeros((blocks, 1, LEAF), F32)
     for b in range(blocks):
         lanes = slice(b * LEAF, (b + 1) * LEAF)
@@ -132,7 +134,7 @@
         ordered[b] = lane_gather(table[b], inverse)
         return 0
 
-    lax.fori_loop(0, blocks, order, 0, unroll=8)
+    lax.fori_loop(0, blocks, order, 0, unroll=32)
     copy.wait()
 
     def step(b, tails):
@@ -152,7 +154,7 @@
             new.append(jnp.where(low + count >= LEAF, fresh, tail))
         return tuple(new)
 
-    tails = lax.fori_loop(0, blocks, step, (jnp.zeros((8, LEAF), F32),) * n_sub, unroll=4)
+    tails = lax.fori_loop(0, blocks, step, (jnp.zeros((8, LEAF), F32),) * n_sub, unroll=8)
     for e in range(n_sub):
         tiles[leaf_idx[blocks - 1, n_sub + e]] = tails[e]
         for l in range(leaves):
@@ -174,13 +176,14 @@
             jax.ShapeDtypeStruct((SLOTS, LEAF), I32),
             jax.ShapeDtypeStruct((n_dom, reads.shape[2]), I32),
         ),
-        in_specs=[anywhere()] * 4 + [vmem()],
+        in_specs=[hbm()] * 5,
         out_specs=(vmem(),) * 4,
         scratch_shapes=[
             pltpu.VMEM((3, count), F32),
             pltpu.VMEM((blocks, LEAF), F32),
             pltpu.VMEM((3, count), F32),
             pltpu.VMEM((blocks, LEAF), I32),
+            pltpu.VMEM(reads.shape, I32),
             pltpu.VMEM((n_sub * (leaves + 1), 8, LEAF), F32),
             pltpu.VMEM((blocks, 8, LEAF), F32),
             pltpu.VMEM((blocks, 8, LEAF), F32),
@@ -190,48 +193,18 @@
             pltpu.VMEM((blocks, LEAF), I32),
             pltpu.VMEM((blocks, LEAF), I32),
             pltpu.SMEM((blocks, LEAF), I32),
-            pltpu.SemaphoreType.DMA((5,)),
+            pltpu.SemaphoreType.DMA((6,)),
         ],
         compiler_params=params(),
         name="regroup",
-    )(positions, masses.reshape(blocks, LEAF), velocities, destinations.reshape(blocks, LEAF), reads)
-
-
-def bundle_kernel(n_dom, list_ref, leaf_hbm, *rest):
-    outs, sems = rest[:n_dom - 1], rest[n_dom - 1]
-    me = lax.axis_index("dom")
-    for k in range(1, n_dom):
-        for slot in range(SLOTS):
-            leaf = list_ref[slot, me ^ k]
-            pltpu.make_async_copy(leaf_hbm.at[leaf], outs[k - 1].at[slot], sems.at[k - 1]).start()
-    for k in range(1, n_dom):
-        pltpu.make_async_copy(outs[k - 1], outs[k - 1], sems.at[k - 1]).wait()
-
-
-def bundle(lists, near, n_dom):
-    return pl.pallas_call(
-        functools.partial(bundle_kernel, n_dom),
-        out_shape=(jax.ShapeDtypeStruct((SLOTS, 4, LEAF), F32),) * (n_dom - 1),
-        in_specs=[smem(), anywhere()],
-        out_specs=(anywhere(),) * (n_dom - 1),
-        scratch_shapes=[pltpu.SemaphoreType.DMA((n_dom - 1,))],
-        compiler_params=params(),
-        name="bundle",
-    )(lists, near)
-
-
-def spread_sources(src_refs, wide_ref):
+    )(*in_hbm(positions, masses.reshape(blocks, LEAF), velocities, destinations.reshape(blocks, LEAF), reads))
+
+
+def spread_tiles(tiles, wide_ref):
     group = iota((8, LEAF), 1) & ~15
-
-    def spread(k, _):
-        h = 0
-        for src_ref in src_refs:
-            for r in range(0, src_ref.shape[0], 8):
-                wide_ref[k, h] = lane_gather(src_ref[r:r + 8, :], group + k)
-                h += 1
-        return 0
-
-    lax.fori_loop(0, 16, spread, 0)
+    for k in range(16):
+        for h, tile in enumerate(tiles):
+            wide_ref[k, h] = lane_gather(tile(), group + k)
 
 
 def pair_loop(pairs, target_of, source_of, weight_of, here_ref, wide_ref, acc_ref):
@@ -257,21 +230,18 @@
     lax.fori_loop(0, pairs, step, 0, unroll=4)
 
 
-def local_kernel(ids_ref, src_ref, acc_ref, here_ref, wide_ref):
-    spread_sources([src_ref], wide_ref)
+def local_kernel(ids_hbm, src_ref, acc_ref, here_ref, ids_ref, wide_ref, sem):
+    load = pltpu.make_async_copy(ids_hbm, ids_ref, sem)
+    load.start()
     leaves = acc_ref.shape[0]
+    spread_tiles([functools.partial(src_ref.__getitem__, pl.ds(8 * h, 8)) for h in range(leaves // 2)], wide_ref)
     fold = iota((8, LEAF), 0) * 16 + (iota((8, LEAF), 1) & 15)
-    batch = 8 if leaves % 8 == 0 else 1
-
-    def pack(j, _):
-        for u in range(batch):
-            for c in range(3):
-                line = src_ref[pl.ds(4 * (j * batch + u) + c, 1), :]
-                here_ref[j * batch + u, c] = lane_gather(jnp.broadcast_to(line, (8, LEAF)), fold)
-        return 0
-
-    lax.fori_loop(0, leaves // batch, pack, 0)
+    for t in range(leaves):
+        for c in range(3):
+            line = src_ref[4 * t + c:4 * t + c + 1, :]
+            here_ref[t, c] = lane_gather(jnp.broadcast_to(line, (8, LEAF)), fold)
     acc_ref[...] = jnp.zeros_like(acc_ref)
+    load.wait()
     pair_loop(
         ids_ref.shape[1], lambda i: ids_ref[0, i], lambda i: ids_ref[1, i], lambda i: None,
         here_ref, wide_ref, acc_ref,
@@ -288,13 +258,17 @@
             jax.ShapeDtypeStruct((leaves, 4, 8, LEAF), F32),
             jax.ShapeDtypeStruct((leaves, 3, 8, LEAF), F32),
         ),
-        in_specs=[smem(), vmem()],
+        in_specs=[hbm(), vmem()],
         out_specs=(vmem(), vmem()),
-        scratch_shapes=[pltpu.VMEM((16, rows // 8, 8, LEAF), F32)],
+        scratch_shapes=[
+            pltpu.SMEM(near_local.shape, I32),
+            pltpu.VMEM((16, rows // 8, 8, LEAF), F32),
+            pltpu.SemaphoreType.DMA,
+        ],
         compiler_params=params(),
         cost_estimate=pl.CostEstimate(flops=18 * work, transcendentals=work, bytes_accessed=8 * rows * LEAF),
         name="local_forces",
-    )(near_local, near)
+    )(*in_hbm(near_local), near)
 
 
 def three_parts(x):
@@ -317,12 +291,32 @@
     )
 
 
-def remote_kernel(n_dom, ids_ref, lookup_ref, reads_ref, tgt_ref, vel_ref, local_ref, here_ref, *rest):
+def remote_kernel(
+    n_dom, ids_hbm, lookup_hbm, list_hbm, reads_hbm, tgt_ref, vel_ref, local_ref, here_ref, *rest
+):
     src_refs = rest[:n_dom - 1]
-    accel_ref, kicked_ref, wide_ref, acc_ref = rest[n_dom - 1:]
+    (accel_ref, kicked_ref, ids_ref, lookup_ref, list_ref, reads_ref, wide_ref, acc_ref, sems) = rest[n_dom - 1:]
     me = lax.axis_index("dom")
-    spread_sources(src_refs, wide_ref)
+    loads = [
+        pltpu.make_async_copy(source, target, sems.at[n])
+        for n, (source, target) in enumerate([
+            (list_hbm, list_ref), (ids_hbm, ids_ref), (lookup_hbm, lookup_ref), (reads_hbm, reads_ref),
+        ])
+    ]
+    for load in loads:
+        load.start()
     acc_ref[...] = jnp.zeros_like(acc_ref)
+    loads[0].wait()
+
+    def two_leaves(k, j):
+        pair = [src_refs[k - 1][list_ref[2 * j + u, me ^ k]] for u in range(2)]
+        return jnp.concatenate(pair, axis=0)
+
+    spread_tiles(
+        [functools.partial(two_leaves, k, j) for k in range(1, n_dom) for j in range(SLOTS // 2)], wide_ref
+    )
+    for load in loads[1:]:
+        load.wait()
 
     def source_of(i):
         q = ids_ref[1, i]
@@ -339,14 +333,17 @@
         rows = slice(8 * h, 8 * h + 8)
         mass = [jnp.broadcast_to(tgt_ref[8 * h + r:8 * h + r + 1, :], (8, LEAF)) for r in (3, 7)]
         accel = jnp.where(jnp.where(first, mass[0], mass[1]) > 0.0, total[rows], 0.0)
-        kicked = vel_ref[rows, :] + kick_time * accel
+        per = vel_ref.shape[1]
+        kicked = jnp.concatenate(
+            [vel_ref[r // per, r % per:r % per + 4, :] for r in (8 * h, 8 * h + 4)], axis=0
+        ) + kick_time * accel
         for u in range(2):
             lanes = slice((2 * h + u) * LEAF, (2 * h + u + 1) * LEAF)
             accel_ref[:, lanes] = accel[4 * u:4 * u + 3]
             kicked_ref[:, lanes] = kicked[4 * u:4 * u + 3]
 
 
-def remote_forces(near_remote, lookup, reads, near, vel, local, here, arrived):
+def remote_forces(near_remote, lookup, lists, reads, near, vel, local, here, arrived):
     n_dom = reads.shape[0]
     rows = near.shape[0]
     leaves = rows // 4
@@ -355,16 +352,21 @@
     return pl.pallas_call(
         functools.partial(remote_kernel, n_dom),
         out_shape=(out, out),
-        in_specs=[smem()] * 3 + [vmem()] * (3 + n_dom),
+        in_specs=[hbm()] * 4 + [vmem()] * (3 + n_dom),
         out_specs=(vmem(), vmem()),
         scratch_shapes=[
-            pltpu.VMEM((16, (n_dom - 1) * ROWS // 8, 8, LEAF), F32),
+            pltpu.SMEM(near_remote.shape, I32),
+            pltpu.SMEM(lookup.shape, I32),
+            pltpu.SMEM(lists.shape, I32),
+            pltpu.SMEM(reads.shape, I32),
+            pltpu.VMEM((16, (n_dom - 1) * SLOTS // 2, 8, LEAF), F32),
             pltpu.VMEM((leaves, 4, 8, LEAF), F32),
+            pltpu.SemaphoreType.DMA((4,)),
         ],
         compiler_params=params(),
         cost_estimate=pl.CostEstimate(flops=18 * work, transcendentals=work, bytes_accessed=24 * rows * LEAF),
         name="remote_forces",
-    )(near_remote, lookup, reads, near, vel, local, here, *arrived)
+    )(*in_hbm(near_remote), lookup, lists, *in_hbm(reads), near, vel, local, here, *arrived)
 
 
 def on_device(positions, masses, velocities, destinations, readers, near_local, near_remote):
@@ -376,17 +378,12 @@
     reads = readers.reshape(n_dom, n_dom, readers.shape[3])
     near, far, lists, lookup = regroup(positions, masses, velocities, destinations, reads, n_sub, leaves)
     near = lax.all_to_all(near, "sub", split_axis=0, concat_axis=0, tiled=True)
-    packed = bundle(lists, near.reshape(n_sub * leaves, 4, LEAF), n_dom)
-    arrived = [
-        lax.ppermute(packed[k - 1], "dom", [(i, i ^ k) for i in range(n_dom)]).reshape(ROWS, LEAF)
-        for k in range(1, n_dom)
-    ]
+    whole = near.reshape(n_sub * leaves, 4, LEAF)
+    arrived = [lax.ppermute(whole, "dom", [(i, i ^ k) for i in range(n_dom)]) for k in range(1, n_dom)]
     far = lax.all_to_all(far, "sub", split_axis=0, concat_axis=0, tiled=True)
     near = near.reshape(n_sub * leaves * 4, LEAF)
     local, here = local_forces(near_local, near)
-    return remote_forces(
-        near_remote, lookup, reads, near, far.reshape(n_sub * leaves * 4, LEAF), local, here, arrived
-    )
+    return remote_forces(near_remote, lookup, lists, reads, near, far, local, here, arrived)
 
 
 def solution(mesh):

time: 59.7 us -> 49.7 us (0.83)
  Pallas kernels: 33.5 us -> 28.5 us
  local copies, waits for them, and re-layouts: 4.7 us -> 0 us
    unnamed x16 -> x0, local copies, waits for them, and re-layouts: 4.7 us -> none
    pallas_call x1, Pallas kernels: 11.8 us -> 9.53 us  [local_forces(): pl.pallas_call(local_kernel, out_shape=(jax.ShapeDtypeStruct((leaves, 4,...]
    pallas_call x1 -> x0, Pallas kernels: 1.45 us -> none  [bundle(): pl.pallas_call(functools.partial(bundle_kernel, n_dom), out_shape=(jax.Sh...]
    pallas_call x1, Pallas kernels: 7.15 us -> 5.77 us  [regroup(): pl.pallas_call(functools.partial(regroup_kernel, n_sub, n_dom, leaves), o...]
  transfers between devices with their start and end apart: 4 -> 4, of which waited for: 0 -> 0; matrix products, arithmetic and copies ran while one was open for 0% -> 0% of each run, Pallas kernels for 22% -> 19%
where the time goes in v3:
time: 49.7 us; the launch traced here: 49.4 us
  Pallas kernels  28.5 us (57%)
  blocking collectives  13.3 us (27%)
  starting transfers between devices  6.94 us (14%)
  between operations  0.69 us (1%)
    all_to_all x1, blocking collectives, on_device(): near = lax.all_to_all(near, 'sub', split_axis=0, concat_axis=0, tiled=True)  13.3 us
    pallas_call x1, Pallas kernels, remote_forces(): pl.pallas_call(functools.partial(remote_kernel, n_dom), out_shape=(out, o...  13.2 us
    pallas_call x1, Pallas kernels, local_forces(): pl.pallas_call(local_kernel, out_shape=(jax.ShapeDtypeStruct((leaves, 4,...  9.53 us
    pallas_call x1, Pallas kernels, regroup(): pl.pallas_call(functools.partial(regroup_kernel, n_sub, n_dom, leaves), o...  5.77 us
    ppermute x3, starting transfers between devices, on_device(): lax.ppermute(whole, 'dom', [(i, i ^ k) for i in range(n_dom)])  3.55 us
    all_to_all x1, starting transfers between devices, on_device(): far = lax.all_to_all(far, 'sub', split_axis=0, concat_axis=0, tiled=True)  3.38 us
  transfers between devices with their start and end apart: 4, of which 0 were waited for; matrix products, arithmetic and copies ran while one was open for 0% of the time, Pallas kernels for 19%

profile of v3, /device:TPU:0, one launch (start us, length us, event | category | flops | bytes accessed | tf_op | source)
XLA Modules:
  0.0 49.4 jit_solution(16724306829456232838)
XLA Ops:
  0.6 5.8 %regroup.1 = (f32[8,40,128]{2,1,0:T(8,128)S(1)}, f32[8,40,128]{2,1,0:T(8,128)}, s32[32,128]{1,0:T(8,128)S(1)}, s32[4,80]{1,0:T(4,128)S(1)}) custom-call(f32[3,8192]{1,0:T(4,128)} %pos_hbm.1, f32[64,128]{1,0:T(8,128)} %bitcast.10, f32[3,8192]{1,0:T(4,128)} %vel_hbm.1, s32[64,128]{1,0:T(8,128)} %bitcast.11, s32[4,4,80]{2,1,0:T(4,128)} %bitcast.12), custom_call_target="tpu_custom_call" | custom-call | tf_op jit(solution)/shard_map/regroup/pallas_call | solution.py:171
  6.4 13.3 %all_to_all.10 = f32[8,40,128]{2,1,0:T(8,128)S(1)} all-to-all(f32[8,40,128]{2,1,0:T(8,128)S(1)} %get-tuple-element.10), channel_id=1, replica_groups=mesh['dom'=4,'sub'=8] {'sub'}, dimensions={0} | all-to-all | bytes 327680 | tf_op jit(solution)/shard_map/all_to_all | solution.py:380
  19.8 3.4 %all-to-all-start.1 = ((f32[8,40,128]{2,1,0:T(8,128)}), f32[8,40,128]{2,1,0:T(8,128)S(1)}, u32[]{:S(2)}, u32[]{:S(2)}) async-start(f32[8,40,128]{2,1,0:T(8,128)} %get-tuple-element.11), calls=%async_computation.1 | async-start | bytes 327680 | tf_op jit(solution)/shard_map/all_to_all | solution.py:383
  23.2 2.5 %collective-permute-start.2 = (f32[80,4,128]{2,1,0:T(4,128)S(1)}, f32[80,4,128]{2,1,0:T(4,128)S(1)}, u32[]{:S(2)}, u32[]{:S(2)}) collective-permute-start(f32[80,4,128]{2,1,0:T(4,128)S(1)} %bitcast.5), channel_id=1, source_target_pairs={{0,24},{8,16},{16,8},{24,0},{1,25},{9,17},{17,9},{25,1},{2,26},{10... | collective-permute-start | bytes 491528 | tf_op jit(solution)/shard_map/ppermute | solution.py:382
  25.7 0.5 %collective-permute-start.1 = (f32[80,4,128]{2,1,0:T(4,128)S(1)}, f32[80,4,128]{2,1,0:T(4,128)S(1)}, u32[]{:S(2)}, u32[]{:S(2)}) collective-permute-start(f32[80,4,128]{2,1,0:T(4,128)S(1)} %bitcast.6), channel_id=1, source_target_pairs={{0,16},{8,24},{16,0},{24,8},{1,17},{9,25},{17,1},{25,9},{2,18},{10... | collective-permute-start | bytes 491528 | tf_op jit(solution)/shard_map/ppermute | solution.py:382
  26.2 0.5 %collective-permute-start = (f32[80,4,128]{2,1,0:T(4,128)S(1)}, f32[80,4,128]{2,1,0:T(4,128)S(1)}, u32[]{:S(2)}, u32[]{:S(2)}) collective-permute-start(f32[80,4,128]{2,1,0:T(4,128)S(1)} %bitcast.7), channel_id=1, source_target_pairs={{0,8},{8,0},{16,24},{24,16},{1,9},{9,1},{17,25},{25,17},{2,10},{10... | collective-permute-start | bytes 491528 | tf_op jit(solution)/shard_map/ppermute | solution.py:382
  26.7 9.5 %local_forces.1 = (f32[80,4,8,128]{3,2,1,0:T(8,128)S(1)}, f32[80,3,8,128]{3,2,1,0:T(8,128)S(1)}) custom-call(s32[2,192]{1,0:T(2,128)} %ids_hbm.2, f32[320,128]{1,0:T(8,128)S(1)} %bitcast.8), custom_call_target="tpu_custom_call" | custom-call | flops 56623104 | bytes 327680 | tf_op jit(solution)/shard_map/local_forces/pallas_call | solution.py:255
  36.2 0.0 all-to-all-done.1.vel_ref
  36.3 0.0 collective-permute-done.2.rest_2_
  36.3 0.0 collective-permute-done.1.rest_1_
  36.3 0.0 collective-permute-done.rest_0_
  36.3 13.2 %remote_forces.1 = (f32[3,10240]{1,0:T(4,128)}, f32[3,10240]{1,0:T(4,128)}) custom-call(s32[3,192]{1,0:T(4,128)} %ids_hbm.3, s32[4,80]{1,0:T(4,128)S(1)} %get-tuple-element.8.lookup_hbm, s32[32,128]{1,0:T(8,128)S(1)} %get-tuple-element.9.list_hbm, s32[4,4,80]{2,1,0:T(4,128)} %bitcast.13, f32[320,128]{1,0:T(8,128)S(1)} %bitcast.9, ...), custom_call_target="tpu_custom_call" | custom-call | flops 56623104 | bytes 983040 | tf_op jit(solution)/shard_map/remote_forces/pallas_call | solution.py:352
Async XLA Ops:
  19.8 16.5 %all-to-all-start.1 = ((f32[8,40,128]{2,1,0:T(8,128)}), f32[8,40,128]{2,1,0:T(8,128)S(1)}, u32[]{:S(2)}, u32[]{:S(2)}) async-start(f32[8,40,128]{2,1,0:T(8,128)} %get-tuple-element.11), calls=%async_computation.1 | async-start | bytes 327680 | tf_op jit(solution)/shard_map/all_to_all | solution.py:383
  23.2 13.1 %collective-permute-start.2 = (f32[80,4,128]{2,1,0:T(4,128)S(1)}, f32[80,4,128]{2,1,0:T(4,128)S(1)}, u32[]{:S(2)}, u32[]{:S(2)}) collective-permute-start(f32[80,4,128]{2,1,0:T(4,128)S(1)} %bitcast.5), channel_id=1, source_target_pairs={{0,24},{8,16},{16,8},{24,0},{1,25},{9,17},{17,9},{25,1},{2,26},{10... | collective-permute-start | bytes 491528 | tf_op jit(solution)/shard_map/ppermute | solution.py:382
  25.7 10.6 %collective-permute-start.1 = (f32[80,4,128]{2,1,0:T(4,128)S(1)}, f32[80,4,128]{2,1,0:T(4,128)S(1)}, u32[]{:S(2)}, u32[]{:S(2)}) collective-permute-start(f32[80,4,128]{2,1,0:T(4,128)S(1)} %bitcast.6), channel_id=1, source_target_pairs={{0,16},{8,24},{16,0},{24,8},{1,17},{9,25},{17,1},{25,9},{2,18},{10... | collective-permute-start | bytes 491528 | tf_op jit(solution)/shard_map/ppermute | solution.py:382
  26.2 10.1 %collective-permute-start = (f32[80,4,128]{2,1,0:T(4,128)S(1)}, f32[80,4,128]{2,1,0:T(4,128)S(1)}, u32[]{:S(2)}, u32[]{:S(2)}) collective-permute-start(f32[80,4,128]{2,1,0:T(4,128)S(1)} %bitcast.7), channel_id=1, source_target_pairs={{0,8},{8,0},{16,24},{24,16},{1,9},{9,1},{17,25},{25,17},{2,10},{10... | collective-permute-start | bytes 491528 | tf_op jit(solution)/shard_map/ppermute | solution.py:382

commit v4 on v3

--- a/solution.py
+++ b/solution.py
@@ -52,34 +52,49 @@
     return jnp.where(condition, 1.0, 0.0).astype(BF16)
 
 
-def plan_reads(n_dom, reads_ref, list_ref, lookup_ref):
+def plan_reads(n_dom, reads_ref, ids_ref, local_ref, list_ref, pairs_ref):
+    me = lax.axis_index("dom")
     leaves = reads_ref.shape[2]
+    pairs = ids_ref.shape[1]
     lower = as_bf16(iota((leaves, leaves), 0) < iota((leaves, leaves), 1))
-    wanted = reads_ref[lax.axis_index("dom")]
+    wanted = reads_ref[me]
     flags = wanted.astype(F32).astype(BF16)
-    place = jnp.dot(flags, lower, preferred_element_type=F32).astype(I32)
-    lookup_ref[...] = jnp.minimum(place, SLOTS - 1)
-    slot = iota((SLOTS, leaves), 0)
+    place = jnp.minimum(jnp.dot(flags, lower, preferred_element_type=F32), SLOTS - 1.0)
+    slot = iota((SLOTS, leaves), 0).astype(F32)
     leaf = iota((SLOTS, leaves), 1)
     lane = iota((SLOTS, LEAF), 1)
     lists = jnp.zeros((SLOTS, LEAF), I32)
+    source_dom, source_leaf = ids_ref[1:2, :], ids_ref[2:3, :]
+    line = iota((8, leaves), 0)
+    looked = jnp.zeros((8, pairs), F32)
     for q in range(n_dom):
-        hit = (place[q:q + 1] == slot) & (wanted[q:q + 1] > 0)
+        mine = wanted[q:q + 1]
+        hit = (place[q:q + 1] == slot) & (mine > 0)
         lists = jnp.where(lane == q, jnp.sum(jnp.where(hit, leaf, 0), axis=1, keepdims=True), lists)
+        rows = jnp.where(line == 0, place[q:q + 1], jnp.where(line == 1, mine.astype(F32), 0.0))
+        here = as_bf16((iota((leaves, pairs), 0) == source_leaf) & (source_dom == q))
+        looked += jnp.dot(rows.astype(BF16), here, preferred_element_type=F32)
     list_ref[...] = lists
+    looked = looked.astype(I32)
+    pairs_ref[0:1, :] = ids_ref[0:1, :]
+    pairs_ref[1:2, :] = jnp.maximum((source_dom ^ me) - 1, 0) * SLOTS + looked[0:1]
+    pairs_ref[2:3, :] = looked[1:2]
+    pairs_ref[3:5, :] = local_ref[...]
+    pairs_ref[5:8, :] = jnp.zeros((3, pairs), I32)
 
 
 def regroup_kernel(
-    n_sub, n_dom, leaves, pos_hbm, mass_hbm, vel_hbm, dest_hbm, reads_hbm,
-    near_ref, far_ref, list_ref, lookup_ref,
-    pos_ref, mass_ref, vel_ref, dest_ref, reads_ref, tiles, table, ordered,
+    n_sub, n_dom, leaves, pos_hbm, mass_hbm, vel_hbm, dest_hbm, reads_hbm, ids_hbm, local_hbm,
+    near_ref, far_ref, list_ref, pairs_ref,
+    pos_ref, mass_ref, vel_ref, dest_ref, reads_ref, ids_ref, local_ref, tiles, table, ordered,
     off_ref, cnt_ref, start_ref, perm_ref, leaf_vec, leaf_idx, sems
 ):
     blocks = dest_ref.shape[0]
     loads = [
         pltpu.make_async_copy(source, target, sems.at[n])
         for n, (source, target) in enumerate(
-            [(dest_hbm, dest_ref), (reads_hbm, reads_ref), (pos_hbm, pos_ref), (mass_hbm, mass_ref), (vel_hbm, vel_ref)]
+            [(dest_hbm, dest_ref), (reads_hbm, reads_ref), (ids_hbm, ids_ref), (local_hbm, local_ref),
+             (pos_hbm, pos_ref), (mass_hbm, mass_ref), (vel_hbm, vel_ref)]
         )
     ]
     for load in loads:
@@ -111,12 +126,12 @@
         leaf_of = jnp.where(lane64 == n_sub + e, base + ((offset + count) >> 7), leaf_of)
         start = start + total
     leaf_vec[...] = leaf_of
-    copy = pltpu.make_async_copy(leaf_vec, leaf_idx, sems.at[5])
+    copy = pltpu.make_async_copy(leaf_vec, leaf_idx, sems.at[7])
     copy.start()
     perm_ref[...] = place.astype(I32)
     for load in loads[1:]:
         load.wait()
-    plan_reads(n_dom, reads_ref, list_ref, lookup_ref)
+    plan_reads(n_dom, reads_ref, ids_ref, local_ref, list_ref, pairs_ref)
     table[:, 7:8, :] = jnp.zeros((blocks, 1, LEAF), F32)
     for b in range(blocks):
         lanes = slice(b * LEAF, (b + 1) * LEAF)
@@ -163,7 +178,7 @@
             far_ref[e, 4 * l:4 * l + 4, :] = tile[4:8]
 
 
-def regroup(positions, masses, velocities, destinations, reads, n_sub, leaves):
+def regroup(positions, masses, velocities, destinations, reads, near_local, near_remote, n_sub, leaves):
     count = positions.shape[1]
     blocks = count // LEAF
     n_dom = reads.shape[0]
@@ -174,9 +189,9 @@
             out,
             out,
             jax.ShapeDtypeStruct((SLOTS, LEAF), I32),
-            jax.ShapeDtypeStruct((n_dom, reads.shape[2]), I32),
+            jax.ShapeDtypeStruct((8, near_remote.shape[1]), I32),
         ),
-        in_specs=[hbm()] * 5,
+        in_specs=[hbm()] * 7,
         out_specs=(vmem(),) * 4,
         scratch_shapes=[
             pltpu.VMEM((3, count), F32),
@@ -184,6 +199,8 @@
             pltpu.VMEM((3, count), F32),
             pltpu.VMEM((blocks, LEAF), I32),
             pltpu.VMEM(reads.shape, I32),
+            pltpu.VMEM(near_remote.shape, I32),
+            pltpu.VMEM(near_local.shape, I32),
             pltpu.VMEM((n_sub * (leaves + 1), 8, LEAF), F32),
             pltpu.VMEM((blocks, 8, LEAF), F32),
             pltpu.VMEM((blocks, 8, LEAF), F32),
@@ -193,24 +210,55 @@
             pltpu.VMEM((blocks, LEAF), I32),
             pltpu.VMEM((blocks, LEAF), I32),
             pltpu.SMEM((blocks, LEAF), I32),
-            pltpu.SemaphoreType.DMA((6,)),
+            pltpu.SemaphoreType.DMA((8,)),
         ],
         compiler_params=params(),
         name="regroup",
-    )(*in_hbm(positions, masses.reshape(blocks, LEAF), velocities, destinations.reshape(blocks, LEAF), reads))
-
-
-def spread_tiles(tiles, wide_ref):
+    )(*in_hbm(
+        positions, masses.reshape(blocks, LEAF), velocities, destinations.reshape(blocks, LEAF), reads,
+        near_remote, near_local,
+    ))
+
+
+UNROLL = 8
+
+
+def spread_tiles(tile_of, count, wide_ref):
     group = iota((8, LEAF), 1) & ~15
     for k in range(16):
-        for h, tile in enumerate(tiles):
-            wide_ref[k, h] = lane_gather(tile(), group + k)
-
-
-def pair_loop(pairs, target_of, source_of, weight_of, here_ref, wide_ref, acc_ref):
-    def step(i, _):
-        t = target_of(i)
-        s = source_of(i)
+        for h in range(count):
+            wide_ref[k, h] = lane_gather(tile_of(h), group + k)
+
+
+def live_pairs(targets, sources, flags, target_mass, source_mass, list_ref):
+    pairs = targets.shape[1]
+    spare = target_mass.shape[0]
+
+    def filled(ids, mass):
+        some = jnp.broadcast_to(mass[:, :1] > 0.0, (mass.shape[0], pairs))
+        pick = as_bf16((iota((mass.shape[0], pairs), 0) == ids) & some)
+        return jnp.dot(jnp.ones((8, mass.shape[0]), BF16), pick, preferred_element_type=F32)
+
+    live = filled(targets, target_mass) * filled(sources, source_mass)
+    if flags is not None:
+        live = live * flags.astype(F32)
+    row, col = iota((pairs, pairs), 0), iota((pairs, pairs), 1)
+    place = jnp.dot(live.astype(BF16), as_bf16(row < col), preferred_element_type=F32).astype(I32)
+    move = as_bf16((place[:1] == row) & (live[:1] > 0.0))
+    line = iota((8, pairs), 0)
+    rows = jnp.where(line == 0, targets.astype(F32), jnp.where(line == 1, sources.astype(F32), 1.0))
+    moved = lax.dot_general(
+        rows.astype(BF16), move, (((1,), (1,)), ((), ())), preferred_element_type=F32
+    ).astype(I32)
+    count = jnp.sum(live, axis=1, keepdims=True).astype(I32)
+    moved = jnp.where((line == 0) & (moved[2:3] == 0), spare, moved)
+    list_ref[...] = jnp.where(line == 2, count, moved)
+
+
+def pair_loop(list_ref, here_ref, wide_ref, acc_ref):
+    def pair(i):
+        t = list_ref[0, i]
+        s = list_ref[1, i]
         h, first = s >> 1, (s & 1) * 4
         here = [here_ref[t, c] for c in range(3)]
         sums = None
@@ -222,53 +270,59 @@
             weight = (there[3] * inv) * (inv * inv)
             terms = [weight * delta[c] for c in range(3)]
             sums = terms if sums is None else [sums[c] + terms[c] for c in range(3)]
-        scale = weight_of(i)
         for c in range(3):
-            acc_ref[t, c] += sums[c] if scale is None else sums[c] * scale
+            acc_ref[t, c] += sums[c]
+
+    def step(j, _):
+        for u in range(UNROLL):
+            pair(j * UNROLL + u)
         return 0
 
-    lax.fori_loop(0, pairs, step, 0, unroll=4)
-
-
-def local_kernel(ids_hbm, src_ref, acc_ref, here_ref, ids_ref, wide_ref, sem):
-    load = pltpu.make_async_copy(ids_hbm, ids_ref, sem)
-    load.start()
-    leaves = acc_ref.shape[0]
-    spread_tiles([functools.partial(src_ref.__getitem__, pl.ds(8 * h, 8)) for h in range(leaves // 2)], wide_ref)
+    lax.fori_loop(0, (list_ref[2, 0] + UNROLL - 1) // UNROLL, step, 0)
+
+
+def local_kernel(ids_ref, src_ref, acc_ref, here_ref, wide_ref, list_vec, list_ref, sem):
+    leaves = acc_ref.shape[0] - 1
+    mass = src_ref[pl.ds(3, leaves, stride=4), :]
+    live_pairs(ids_ref[3:4, :], ids_ref[4:5, :], None, mass, mass, list_vec)
+    copy = pltpu.make_async_copy(list_vec, list_ref, sem)
+    copy.start()
+    spread_tiles(lambda h: src_ref[8 * h:8 * h + 8, :], leaves // 2, wide_ref)
     fold = iota((8, LEAF), 0) * 16 + (iota((8, LEAF), 1) & 15)
     for t in range(leaves):
         for c in range(3):
             line = src_ref[4 * t + c:4 * t + c + 1, :]
             here_ref[t, c] = lane_gather(jnp.broadcast_to(line, (8, LEAF)), fold)
+    here_ref[leaves] = jnp.zeros((3, 8, LEAF), F32)
     acc_ref[...] = jnp.zeros_like(acc_ref)
-    load.wait()
-    pair_loop(
-        ids_ref.shape[1], lambda i: ids_ref[0, i], lambda i: ids_ref[1, i], lambda i: None,
-        here_ref, wide_ref, acc_ref,
-    )
-
-
-def local_forces(near_local, near):
+    copy.wait()
+    pair_loop(list_ref, here_ref, wide_ref, acc_ref)
+
+
+def local_forces(ids, near):
     rows = near.shape[0]
     leaves = rows // 4
-    work = near_local.shape[1] * LEAF * LEAF
+    pairs = ids.shape[1]
+    assert pairs % UNROLL == 0
+    work = pairs * LEAF * LEAF
     return pl.pallas_call(
         local_kernel,
         out_shape=(
-            jax.ShapeDtypeStruct((leaves, 4, 8, LEAF), F32),
-            jax.ShapeDtypeStruct((leaves, 3, 8, LEAF), F32),
+            jax.ShapeDtypeStruct((leaves + 1, 4, 8, LEAF), F32),
+            jax.ShapeDtypeStruct((leaves + 1, 3, 8, LEAF), F32),
         ),
-        in_specs=[hbm(), vmem()],
+        in_specs=[vmem(), vmem()],
         out_specs=(vmem(), vmem()),
         scratch_shapes=[
-            pltpu.SMEM(near_local.shape, I32),
             pltpu.VMEM((16, rows // 8, 8, LEAF), F32),
+            pltpu.VMEM((8, pairs), I32),
+            pltpu.SMEM((8, pairs), I32),
             pltpu.SemaphoreType.DMA,
         ],
         compiler_params=params(),
         cost_estimate=pl.CostEstimate(flops=18 * work, transcendentals=work, bytes_accessed=8 * rows * LEAF),
         name="local_forces",
-    )(*in_hbm(near_local), near)
+    )(ids, near)
 
 
 def three_parts(x):
@@ -282,7 +336,7 @@
     source, target = iota((LEAF, LEAF), 0), iota((LEAF, LEAF), 1)
     parts, picks = [], []
     for s in range(8):
-        lines = [ref.reshape(leaves * 32, LEAF)[pl.ds(s, leaves * 4, stride=8), :] for ref in acc_refs]
+        lines = [ref.reshape((leaves + 1) * 32, LEAF)[pl.ds(s, leaves * 4, stride=8), :] for ref in acc_refs]
         pick = as_bf16(((source & 15) == (target & 15)) & ((target >> 4) == s))
         parts += three_parts(sum(lines[1:], lines[0]))
         picks += [pick] * 3
@@ -291,49 +345,37 @@
     )
 
 
-def remote_kernel(
-    n_dom, ids_hbm, lookup_hbm, list_hbm, reads_hbm, tgt_ref, vel_ref, local_ref, here_ref, *rest
-):
+def remote_kernel(n_dom, leaf_list, pairs_ref, tgt_ref, vel_ref, local_ref, here_ref, *rest):
     src_refs = rest[:n_dom - 1]
-    (accel_ref, kicked_ref, ids_ref, lookup_ref, list_ref, reads_ref, wide_ref, acc_ref, sems) = rest[n_dom - 1:]
+    (accel_ref, kicked_ref, leaf_ref, chosen_ref, wide_ref, acc_ref, list_vec, list_ref,
+     sems) = rest[n_dom - 1:]
     me = lax.axis_index("dom")
-    loads = [
-        pltpu.make_async_copy(source, target, sems.at[n])
-        for n, (source, target) in enumerate([
-            (list_hbm, list_ref), (ids_hbm, ids_ref), (lookup_hbm, lookup_ref), (reads_hbm, reads_ref),
-        ])
-    ]
-    for load in loads:
-        load.start()
+    load = pltpu.make_async_copy(leaf_list, leaf_ref, sems.at[0])
+    load.start()
+    leaves = acc_ref.shape[0] - 1
     acc_ref[...] = jnp.zeros_like(acc_ref)
-    loads[0].wait()
-
-    def two_leaves(k, j):
-        pair = [src_refs[k - 1][list_ref[2 * j + u, me ^ k]] for u in range(2)]
-        return jnp.concatenate(pair, axis=0)
-
-    spread_tiles(
-        [functools.partial(two_leaves, k, j) for k in range(1, n_dom) for j in range(SLOTS // 2)], wide_ref
+    slots = (n_dom - 1) * SLOTS
+    load.wait()
+    for k in range(1, n_dom):
+        for j in range(SLOTS):
+            at = 4 * ((k - 1) * SLOTS + j)
+            chosen_ref[at:at + 4, :] = src_refs[k - 1][leaf_ref[j, me ^ k]]
+    live_pairs(
+        pairs_ref[0:1, :], pairs_ref[1:2, :], pairs_ref[2:3, :],
+        tgt_ref[pl.ds(3, leaves, stride=4), :], chosen_ref[pl.ds(3, slots, stride=4), :], list_vec,
     )
-    for load in loads[1:]:
-        load.wait()
-
-    def source_of(i):
-        q = ids_ref[1, i]
-        return jnp.maximum((q ^ me) - 1, 0) * SLOTS + lookup_ref[q, ids_ref[2, i]]
-
-    def weight_of(i):
-        return reads_ref[me, ids_ref[1, i], ids_ref[2, i]].astype(F32)
-
-    pair_loop(ids_ref.shape[1], lambda i: ids_ref[0, i], source_of, weight_of, here_ref, wide_ref, acc_ref)
-    leaves = acc_ref.shape[0]
+    copy = pltpu.make_async_copy(list_vec, list_ref, sems.at[1])
+    copy.start()
+    spread_tiles(lambda h: chosen_ref[8 * h:8 * h + 8, :], slots // 2, wide_ref)
+    copy.wait()
+    pair_loop(list_ref, here_ref, wide_ref, acc_ref)
     total = gravity * unpack_sums([local_ref, acc_ref], leaves)
     first = iota((8, LEAF), 0) < 4
+    per = vel_ref.shape[1]
     for h in range(leaves // 2):
         rows = slice(8 * h, 8 * h + 8)
         mass = [jnp.broadcast_to(tgt_ref[8 * h + r:8 * h + r + 1, :], (8, LEAF)) for r in (3, 7)]
         accel = jnp.where(jnp.where(first, mass[0], mass[1]) > 0.0, total[rows], 0.0)
-        per = vel_ref.shape[1]
         kicked = jnp.concatenate(
             [vel_ref[r // per, r % per:r % per + 4, :] for r in (8 * h, 8 * h + 4)], axis=0
         ) + kick_time * accel
@@ -343,30 +385,32 @@
             kicked_ref[:, lanes] = kicked[4 * u:4 * u + 3]
 
 
-def remote_forces(near_remote, lookup, lists, reads, near, vel, local, here, arrived):
-    n_dom = reads.shape[0]
+def remote_forces(lists, pairs, near, vel, local, here, arrived):
+    n_dom = len(arrived) + 1
     rows = near.shape[0]
     leaves = rows // 4
-    work = near_remote.shape[1] * LEAF * LEAF
+    slots = (n_dom - 1) * SLOTS
+    work = pairs.shape[1] * LEAF * LEAF
+    assert pairs.shape[1] % UNROLL == 0
     out = jax.ShapeDtypeStruct((3, leaves * LEAF), F32)
     return pl.pallas_call(
         functools.partial(remote_kernel, n_dom),
         out_shape=(out, out),
-        in_specs=[hbm()] * 4 + [vmem()] * (3 + n_dom),
+        in_specs=[vmem()] * (5 + n_dom),
         out_specs=(vmem(), vmem()),
         scratch_shapes=[
-            pltpu.SMEM(near_remote.shape, I32),
-            pltpu.SMEM(lookup.shape, I32),
             pltpu.SMEM(lists.shape, I32),
-            pltpu.SMEM(reads.shape, I32),
-            pltpu.VMEM((16, (n_dom - 1) * SLOTS // 2, 8, LEAF), F32),
-            pltpu.VMEM((leaves, 4, 8, LEAF), F32),
-            pltpu.SemaphoreType.DMA((4,)),
+            pltpu.VMEM((slots * 4, LEAF), F32),
+            pltpu.VMEM((16, slots // 2, 8, LEAF), F32),
+            pltpu.VMEM((leaves + 1, 4, 8, LEAF), F32),
+            pltpu.VMEM(pairs.shape, I32),
+            pltpu.SMEM(pairs.shape, I32),
+            pltpu.SemaphoreType.DMA((2,)),
         ],
         compiler_params=params(),
         cost_estimate=pl.CostEstimate(flops=18 * work, transcendentals=work, bytes_accessed=24 * rows * LEAF),
         name="remote_forces",
-    )(*in_hbm(near_remote), lookup, lists, *in_hbm(reads), near, vel, local, here, *arrived)
+    )(lists, pairs, near, vel, local, here, *arrived)
 
 
 def on_device(positions, masses, velocities, destinations, readers, near_local, near_remote):
@@ -376,14 +420,16 @@
     capacity = 5 * count // (4 * n_sub)
     leaves = capacity // LEAF
     reads = readers.reshape(n_dom, n_dom, readers.shape[3])
-    near, far, lists, lookup = regroup(positions, masses, velocities, destinations, reads, n_sub, leaves)
+    near, far, lists, pairs = regroup(
+        positions, masses, velocities, destinations, reads, near_local, near_remote, n_sub, leaves
+    )
     near = lax.all_to_all(near, "sub", split_axis=0, concat_axis=0, tiled=True)
     whole = near.reshape(n_sub * leaves, 4, LEAF)
     arrived = [lax.ppermute(whole, "dom", [(i, i ^ k) for i in range(n_dom)]) for k in range(1, n_dom)]
     far = lax.all_to_all(far, "sub", split_axis=0, concat_axis=0, tiled=True)
     near = near.reshape(n_sub * leaves * 4, LEAF)
-    local, here = local_forces(near_local, near)
-    return remote_forces(near_remote, lookup, lists, reads, near, far, local, here, arrived)
+    local, here = local_forces(pairs, near)
+    return remote_forces(lists, pairs, near, far, local, here, arrived)
 
 
 def solution(mesh):

time: 49.7 us -> 44.4 us (0.89)
  Pallas kernels: 28.5 us -> 23.2 us
    pallas_call x1, Pallas kernels: 13.2 us -> 10.1 us  [remote_forces(): pl.pallas_call(functools.partial(remote_kernel, n_dom), out_shape=(out, o...]
    pallas_call x1, Pallas kernels: 9.53 us -> 7.28 us  [local_forces(): pl.pallas_call(local_kernel, out_shape=(jax.ShapeDtypeStruct((leaves + 1,...]
  transfers between devices with their start and end apart: 4 -> 4, of which waited for: 0 -> 2; matrix products, arithmetic and copies ran while one was open for 0% -> 0% of each run, Pallas kernels for 19% -> 16%
where the time goes in v4:
time: 44.4 us; the launch traced here: 44.3 us
  Pallas kernels  23.2 us (52%)
  blocking collectives  13.3 us (30%)
  starting transfers between devices  6.94 us (16%)
  between operations  0.67 us (2%)
    all_to_all x1, blocking collectives, on_device(): near = lax.all_to_all(near, 'sub', split_axis=0, concat_axis=0, tiled=True)  13.3 us
    pallas_call x1, Pallas kernels, remote_forces(): pl.pallas_call(functools.partial(remote_kernel, n_dom), out_shape=(out, o...  10.1 us
    pallas_call x1, Pallas kernels, local_forces(): pl.pallas_call(local_kernel, out_shape=(jax.ShapeDtypeStruct((leaves + 1,...  7.28 us
    pallas_call x1, Pallas kernels, regroup(): pl.pallas_call(functools.partial(regroup_kernel, n_sub, n_dom, leaves), o...  5.83 us
    ppermute x3, starting transfers between devices, on_device(): lax.ppermute(whole, 'dom', [(i, i ^ k) for i in range(n_dom)])  3.55 us
    all_to_all x1, starting transfers between devices, on_device(): far = lax.all_to_all(far, 'sub', split_axis=0, concat_axis=0, tiled=True)  3.38 us
  transfers between devices with their start and end apart: 4, of which 2 were waited for; matrix products, arithmetic and copies ran while one was open for 0% of the time, Pallas kernels for 16%

profile of v4, /device:TPU:0, one launch (start us, length us, event | category | flops | bytes accessed | tf_op | source)
XLA Modules:
  0.0 44.3 jit_solution(5278223084584969210)
XLA Ops:
  0.6 5.8 %regroup.1 = (f32[8,40,128]{2,1,0:T(8,128)S(1)}, f32[8,40,128]{2,1,0:T(8,128)}, s32[32,128]{1,0:T(8,128)S(1)}, s32[8,192]{1,0:T(8,128)S(1)}) custom-call(f32[3,8192]{1,0:T(4,128)} %pos_hbm.1, f32[64,128]{1,0:T(8,128)} %bitcast.10, f32[3,8192]{1,0:T(4,128)} %vel_hbm.1, s32[64,128]{1,0:T(8,128)} %bitcast.11, s32[4,4,80]{2,1,0:T(4,128)} %bitcast.12, ...), custom_call_target="tpu_custom_call" | custom-call | tf_op jit(solution)/shard_map/regroup/pallas_call | solution.py:186
  6.5 13.3 %all_to_all.10 = f32[8,40,128]{2,1,0:T(8,128)S(1)} all-to-all(f32[8,40,128]{2,1,0:T(8,128)S(1)} %get-tuple-element.10), channel_id=1, replica_groups=mesh['dom'=4,'sub'=8] {'sub'}, dimensions={0} | all-to-all | bytes 327680 | tf_op jit(solution)/shard_map/all_to_all | solution.py:426
  19.8 3.4 %all-to-all-start.1 = ((f32[8,40,128]{2,1,0:T(8,128)}), f32[8,40,128]{2,1,0:T(8,128)S(1)}, u32[]{:S(2)}, u32[]{:S(2)}) async-start(f32[8,40,128]{2,1,0:T(8,128)} %get-tuple-element.11), calls=%async_computation.1 | async-start | bytes 327680 | tf_op jit(solution)/shard_map/all_to_all | solution.py:429
  23.2 2.5 %collective-permute-start.2 = (f32[80,4,128]{2,1,0:T(4,128)S(1)}, f32[80,4,128]{2,1,0:T(4,128)S(1)}, u32[]{:S(2)}, u32[]{:S(2)}) collective-permute-start(f32[80,4,128]{2,1,0:T(4,128)S(1)} %bitcast.5), channel_id=1, source_target_pairs={{0,24},{8,16},{16,8},{24,0},{1,25},{9,17},{17,9},{25,1},{2,26},{10... | collective-permute-start | bytes 491528 | tf_op jit(solution)/shard_map/ppermute | solution.py:428
  25.7 0.5 %collective-permute-start.1 = (f32[80,4,128]{2,1,0:T(4,128)S(1)}, f32[80,4,128]{2,1,0:T(4,128)S(1)}, u32[]{:S(2)}, u32[]{:S(2)}) collective-permute-start(f32[80,4,128]{2,1,0:T(4,128)S(1)} %bitcast.6), channel_id=1, source_target_pairs={{0,16},{8,24},{16,0},{24,8},{1,17},{9,25},{17,1},{25,9},{2,18},{10... | collective-permute-start | bytes 491528 | tf_op jit(solution)/shard_map/ppermute | solution.py:428
  26.2 0.5 %collective-permute-start = (f32[80,4,128]{2,1,0:T(4,128)S(1)}, f32[80,4,128]{2,1,0:T(4,128)S(1)}, u32[]{:S(2)}, u32[]{:S(2)}) collective-permute-start(f32[80,4,128]{2,1,0:T(4,128)S(1)} %bitcast.7), channel_id=1, source_target_pairs={{0,8},{8,0},{16,24},{24,16},{1,9},{9,1},{17,25},{25,17},{2,10},{10... | collective-permute-start | bytes 491528 | tf_op jit(solution)/shard_map/ppermute | solution.py:428
  26.8 7.3 %local_forces.1 = (f32[81,4,8,128]{3,2,1,0:T(8,128)S(1)}, f32[81,3,8,128]{3,2,1,0:T(8,128)S(1)}) custom-call(s32[8,192]{1,0:T(8,128)S(1)} %get-tuple-element.9.ids_ref.pairs_ref, f32[320,128]{1,0:T(8,128)S(1)} %bitcast.8), custom_call_target="tpu_custom_call" | custom-call | flops 56623104 | bytes 327680 | tf_op jit(solution)/shard_map/local_forces/pallas_call | solution.py:308
  34.0 0.0 all-to-all-done.1.vel_ref
  34.1 0.0 collective-permute-done.2.rest_2_
  34.1 0.1 collective-permute-done.1.rest_1_
  34.1 0.1 collective-permute-done.rest_0_
  34.2 10.1 %remote_forces.1 = (f32[3,10240]{1,0:T(4,128)}, f32[3,10240]{1,0:T(4,128)}) custom-call(s32[32,128]{1,0:T(8,128)S(1)} %get-tuple-element.8.leaf_list, s32[8,192]{1,0:T(8,128)S(1)} %get-tuple-element.9.ids_ref.pairs_ref, f32[320,128]{1,0:T(8,128)S(1)} %bitcast.9, f32[8,40,128]{2,1,0:T(8,128)S(1)} %all-to-all-done.1.vel_ref, ...), custom_call_target="tpu_custom_call" | custom-call | flops 56623104 | bytes 983040 | tf_op jit(solution)/shard_map/remote_forces/pallas_call | solution.py:396
Async XLA Ops:
  19.8 14.2 %all-to-all-start.1 = ((f32[8,40,128]{2,1,0:T(8,128)}), f32[8,40,128]{2,1,0:T(8,128)S(1)}, u32[]{:S(2)}, u32[]{:S(2)}) async-start(f32[8,40,128]{2,1,0:T(8,128)} %get-tuple-element.11), calls=%async_computation.1 | async-start | bytes 327680 | tf_op jit(solution)/shard_map/all_to_all | solution.py:429
  23.2 10.9 %collective-permute-start.2 = (f32[80,4,128]{2,1,0:T(4,128)S(1)}, f32[80,4,128]{2,1,0:T(4,128)S(1)}, u32[]{:S(2)}, u32[]{:S(2)}) collective-permute-start(f32[80,4,128]{2,1,0:T(4,128)S(1)} %bitcast.5), channel_id=1, source_target_pairs={{0,24},{8,16},{16,8},{24,0},{1,25},{9,17},{17,9},{25,1},{2,26},{10... | collective-permute-start | bytes 491528 | tf_op jit(solution)/shard_map/ppermute | solution.py:428
  25.7 8.4 %collective-permute-start.1 = (f32[80,4,128]{2,1,0:T(4,128)S(1)}, f32[80,4,128]{2,1,0:T(4,128)S(1)}, u32[]{:S(2)}, u32[]{:S(2)}) collective-permute-start(f32[80,4,128]{2,1,0:T(4,128)S(1)} %bitcast.6), channel_id=1, source_target_pairs={{0,16},{8,24},{16,0},{24,8},{1,17},{9,25},{17,1},{25,9},{2,18},{10... | collective-permute-start | bytes 491528 | tf_op jit(solution)/shard_map/ppermute | solution.py:428
  26.2 8.0 %collective-permute-start = (f32[80,4,128]{2,1,0:T(4,128)S(1)}, f32[80,4,128]{2,1,0:T(4,128)S(1)}, u32[]{:S(2)}, u32[]{:S(2)}) collective-permute-start(f32[80,4,128]{2,1,0:T(4,128)S(1)} %bitcast.7), channel_id=1, source_target_pairs={{0,8},{8,0},{16,24},{24,16},{1,9},{9,1},{17,25},{25,17},{2,10},{10... | collective-permute-start | bytes 491528 | tf_op jit(solution)/shard_map/ppermute | solution.py:428

commit v5 on v4

--- a/solution.py
+++ b/solution.py
@@ -83,22 +83,57 @@
     pairs_ref[5:8, :] = jnp.zeros((3, pairs), I32)
 
 
+def start_copies(sems, *pairs):
+    loads = [pltpu.make_async_copy(source, target, sems.at[n]) for n, (source, target) in enumerate(pairs)]
+    for load in loads:
+        load.start()
+    return loads
+
+
+def by_half(ref, b, half):
+    rows = [jnp.broadcast_to(ref[pl.ds(b + at, 1), :], (8, LEAF)) for at in (0, half)]
+    return jnp.where(iota((8, LEAF), 0) < 4, rows[0], rows[1])
+
+
+def place_particles(n_sub, leaves, ordered, spans, leaf_idx, tiles, out_ref):
+    off_ref, cnt_ref, start_ref = spans
+    half = ordered.shape[0]
+    lane = iota((8, LEAF), 1)
+
+    def step(b, tails):
+        block = ordered[b]
+        new = []
+        for e in range(n_sub):
+            offset = by_half(off_ref.at[e], b, half)
+            count = by_half(cnt_ref.at[e], b, half)
+            first = by_half(start_ref.at[e], b, half)
+            turned = (lane - offset) & (LEAF - 1)
+            moved = lane_gather(block, (turned + first) & (LEAF - 1))
+            low = offset & (LEAF - 1)
+            taken = turned < count
+            tail = jnp.where(taken & (lane >= low), moved, tails[e])
+            tiles[leaf_idx[b, e], 0:4, :] = tail[0:4]
+            tiles[leaf_idx[b + half, e], 4:8, :] = tail[4:8]
+            fresh = jnp.where(taken & (lane < low), moved, 0.0)
+            new.append(jnp.where(low + count >= LEAF, fresh, tail))
+        return tuple(new)
+
+    tails = lax.fori_loop(0, half, step, (jnp.zeros((8, LEAF), F32),) * n_sub, unroll=8)
+    for e in range(n_sub):
+        tiles[leaf_idx[half - 1, n_sub + e], 0:4, :] = tails[e][0:4]
+        tiles[leaf_idx[2 * half - 1, n_sub + e], 4:8, :] = tails[e][4:8]
+        for l in range(leaves):
+            tile = tiles[e * (leaves + 1) + l]
+            out_ref[e, 4 * l:4 * l + 4, :] = tile[0:4] + tile[4:8]
+
+
 def regroup_kernel(
-    n_sub, n_dom, leaves, pos_hbm, mass_hbm, vel_hbm, dest_hbm, reads_hbm, ids_hbm, local_hbm,
-    near_ref, far_ref, list_ref, pairs_ref,
-    pos_ref, mass_ref, vel_ref, dest_ref, reads_ref, ids_ref, local_ref, tiles, table, ordered,
-    off_ref, cnt_ref, start_ref, perm_ref, leaf_vec, leaf_idx, sems
+    n_sub, leaves, pos_hbm, mass_hbm, dest_hbm, near_ref, off_ref, cnt_ref, start_ref, inv_ref, leaf_vec,
+    pos_ref, mass_ref, dest_ref, tiles, table, ordered, perm_ref, leaf_idx, sems
 ):
     blocks = dest_ref.shape[0]
-    loads = [
-        pltpu.make_async_copy(source, target, sems.at[n])
-        for n, (source, target) in enumerate(
-            [(dest_hbm, dest_ref), (reads_hbm, reads_ref), (ids_hbm, ids_ref), (local_hbm, local_ref),
-             (pos_hbm, pos_ref), (mass_hbm, mass_ref), (vel_hbm, vel_ref)]
-        )
-    ]
-    for load in loads:
-        load.start()
+    half = blocks // 2
+    loads = start_copies(sems, (dest_hbm, dest_ref), (pos_hbm, pos_ref), (mass_hbm, mass_ref))
     tiles[...] = jnp.zeros_like(tiles)
     row = iota((LEAF, LEAF), 0)
     weights = jnp.concatenate([as_bf16(row <= iota((LEAF, LEAF), 1)), jnp.ones((LEAF, LEAF), BF16)], axis=1)
@@ -126,98 +161,115 @@
         leaf_of = jnp.where(lane64 == n_sub + e, base + ((offset + count) >> 7), leaf_of)
         start = start + total
     leaf_vec[...] = leaf_of
-    copy = pltpu.make_async_copy(leaf_vec, leaf_idx, sems.at[7])
+    copy = pltpu.make_async_copy(leaf_vec, leaf_idx, sems.at[3])
     copy.start()
     perm_ref[...] = place.astype(I32)
     for load in loads[1:]:
         load.wait()
-    plan_reads(n_dom, reads_ref, ids_ref, local_ref, list_ref, pairs_ref)
-    table[:, 7:8, :] = jnp.zeros((blocks, 1, LEAF), F32)
     for b in range(blocks):
-        lanes = slice(b * LEAF, (b + 1) * LEAF)
-        table[b, 0:3, :] = pos_ref[:, lanes]
-        table[b, 3:4, :] = mass_ref[b:b + 1, :]
-        table[b, 4:7, :] = vel_ref[:, lanes]
-    lane = iota((8, LEAF), 1)
+        at = b // half * 4
+        table[b % half, at:at + 3, :] = pos_ref[:, b * LEAF:(b + 1) * LEAF]
+        table[b % half, at + 3:at + 4, :] = mass_ref[b:b + 1, :]
     lane_rows = iota((16, LEAF), 1).astype(F32).astype(BF16)
+    upper_half = iota((8, LEAF), 0) < 4
 
     def order(b, _):
-        onehot = as_bf16(row == perm_ref[pl.ds(b, 1), :])
-        inverse = lax.dot_general(
-            lane_rows, onehot, (((1,), (1,)), ((), ())), preferred_element_type=F32
-        )[:8].astype(I32)
-        ordered[b] = lane_gather(table[b], inverse)
+        inverse = []
+        for at in (b, b + half):
+            onehot = as_bf16(row == perm_ref[pl.ds(at, 1), :])
+            found = lax.dot_general(
+                lane_rows, onehot, (((1,), (1,)), ((), ())), preferred_element_type=F32
+            )[:8].astype(I32)
+            inv_ref[pl.ds(at, 1), :] = found[:1]
+            inverse.append(found)
+        ordered[b] = lane_gather(table[b], jnp.where(upper_half, inverse[0], inverse[1]))
         return 0
 
-    lax.fori_loop(0, blocks, order, 0, unroll=32)
+    lax.fori_loop(0, half, order, 0, unroll=16)
     copy.wait()
-
-    def step(b, tails):
-        block = ordered[b]
-        new = []
-        for e in range(n_sub):
-            offset = jnp.broadcast_to(off_ref[e, pl.ds(b, 1), :], (8, LEAF))
-            count = jnp.broadcast_to(cnt_ref[e, pl.ds(b, 1), :], (8, LEAF))
-            first = jnp.broadcast_to(start_ref[e, pl.ds(b, 1), :], (8, LEAF))
-            turned = (lane - offset) & (LEAF - 1)
-            moved = lane_gather(block, (turned + first) & (LEAF - 1))
-            low = offset & (LEAF - 1)
-            taken = turned < count
-            tail = jnp.where(taken & (lane >= low), moved, tails[e])
-            tiles[leaf_idx[b, e]] = tail
-            fresh = jnp.where(taken & (lane < low), moved, 0.0)
-            new.append(jnp.where(low + count >= LEAF, fresh, tail))
-        return tuple(new)
-
-    tails = lax.fori_loop(0, blocks, step, (jnp.zeros((8, LEAF), F32),) * n_sub, unroll=8)
-    for e in range(n_sub):
-        tiles[leaf_idx[blocks - 1, n_sub + e]] = tails[e]
-        for l in range(leaves):
-            tile = tiles[e * (leaves + 1) + l]
-            near_ref[e, 4 * l:4 * l + 4, :] = tile[0:4]
-            far_ref[e, 4 * l:4 * l + 4, :] = tile[4:8]
-
-
-def regroup(positions, masses, velocities, destinations, reads, near_local, near_remote, n_sub, leaves):
+    place_particles(n_sub, leaves, ordered, (off_ref, cnt_ref, start_ref), leaf_idx, tiles, near_ref)
+
+
+def regroup(positions, masses, destinations, n_sub, leaves):
     count = positions.shape[1]
     blocks = count // LEAF
+    spans = jax.ShapeDtypeStruct((n_sub, blocks, LEAF), I32)
+    rows = jax.ShapeDtypeStruct((blocks, LEAF), I32)
+    return pl.pallas_call(
+        functools.partial(regroup_kernel, n_sub, leaves),
+        out_shape=(jax.ShapeDtypeStruct((n_sub, leaves * 4, LEAF), F32), spans, spans, spans, rows, rows),
+        in_specs=[hbm()] * 3,
+        out_specs=(vmem(),) * 6,
+        scratch_shapes=[
+            pltpu.VMEM((3, count), F32),
+            pltpu.VMEM((blocks, LEAF), F32),
+            pltpu.VMEM((blocks, LEAF), I32),
+            pltpu.VMEM((n_sub * (leaves + 1), 8, LEAF), F32),
+            pltpu.VMEM((blocks // 2, 8, LEAF), F32),
+            pltpu.VMEM((blocks // 2, 8, LEAF), F32),
+            pltpu.VMEM((blocks, LEAF), I32),
+            pltpu.SMEM((blocks, LEAF), I32),
+            pltpu.SemaphoreType.DMA((4,)),
+        ],
+        compiler_params=params(),
+        name="regroup",
+    )(*in_hbm(positions, masses.reshape(blocks, LEAF), destinations.reshape(blocks, LEAF)))
+
+
+def velocity_kernel(
+    n_sub, n_dom, leaves, vel_hbm, reads_hbm, ids_hbm, local_hbm, off_ref, cnt_ref, start_ref, inv_ref, leaf_vec,
+    far_ref, list_ref, pairs_ref, vel_ref, reads_ref, ids_ref, local_ref, tiles, table, ordered, leaf_idx, sems
+):
+    half = ordered.shape[0]
+    loads = start_copies(
+        sems, (vel_hbm, vel_ref), (leaf_vec, leaf_idx), (reads_hbm, reads_ref), (ids_hbm, ids_ref),
+        (local_hbm, local_ref),
+    )
+    tiles[...] = jnp.zeros_like(tiles)
+    table[...] = jnp.zeros_like(table)
+    for load in loads:
+        load.wait()
+    plan_reads(n_dom, reads_ref, ids_ref, local_ref, list_ref, pairs_ref)
+    for b in range(2 * half):
+        at = b // half * 4
+        table[b % half, at:at + 3, :] = vel_ref[:, b * LEAF:(b + 1) * LEAF]
+
+    def order(b, _):
+        ordered[b] = lane_gather(table[b], by_half(inv_ref, b, half))
+        return 0
+
+    lax.fori_loop(0, half, order, 0, unroll=8)
+    place_particles(n_sub, leaves, ordered, (off_ref, cnt_ref, start_ref), leaf_idx, tiles, far_ref)
+
+
+def regroup_velocities(velocities, reads, near_local, near_remote, tables, n_sub, leaves):
+    count = velocities.shape[1]
+    blocks = count // LEAF
     n_dom = reads.shape[0]
-    out = jax.ShapeDtypeStruct((n_sub, leaves * 4, LEAF), F32)
     return pl.pallas_call(
-        functools.partial(regroup_kernel, n_sub, n_dom, leaves),
+        functools.partial(velocity_kernel, n_sub, n_dom, leaves),
         out_shape=(
-            out,
-            out,
+            jax.ShapeDtypeStruct((n_sub, leaves * 4, LEAF), F32),
             jax.ShapeDtypeStruct((SLOTS, LEAF), I32),
             jax.ShapeDtypeStruct((8, near_remote.shape[1]), I32),
         ),
-        in_specs=[hbm()] * 7,
-        out_specs=(vmem(),) * 4,
+        in_specs=[hbm()] * 4 + [vmem()] * 5,
+        out_specs=(vmem(),) * 3,
         scratch_shapes=[
             pltpu.VMEM((3, count), F32),
-            pltpu.VMEM((blocks, LEAF), F32),
-            pltpu.VMEM((3, count), F32),
-            pltpu.VMEM((blocks, LEAF), I32),
             pltpu.VMEM(reads.shape, I32),
             pltpu.VMEM(near_remote.shape, I32),
             pltpu.VMEM(near_local.shape, I32),
             pltpu.VMEM((n_sub * (leaves + 1), 8, LEAF), F32),
-            pltpu.VMEM((blocks, 8, LEAF), F32),
-            pltpu.VMEM((blocks, 8, LEAF), F32),
-            pltpu.VMEM((n_sub, blocks, LEAF), I32),
-            pltpu.VMEM((n_sub, blocks, LEAF), I32),
-            pltpu.VMEM((n_sub, blocks, LEAF), I32),
-            pltpu.VMEM((blocks, LEAF), I32),
-            pltpu.VMEM((blocks, LEAF), I32),
+            pltpu.VMEM((blocks // 2, 8, LEAF), F32),
+            pltpu.VMEM((blocks // 2, 8, LEAF), F32),
             pltpu.SMEM((blocks, LEAF), I32),
-            pltpu.SemaphoreType.DMA((8,)),
+            pltpu.SemaphoreType.DMA((5,)),
         ],
         compiler_params=params(),
-        name="regroup",
-    )(*in_hbm(
-        positions, masses.reshape(blocks, LEAF), velocities, destinations.reshape(blocks, LEAF), reads,
-        near_remote, near_local,
-    ))
+        cost_estimate=pl.CostEstimate(flops=200 * n_sub * count, transcendentals=0, bytes_accessed=400 * count),
+        name="regroup_velocities",
+    )(*in_hbm(velocities, reads, near_remote, near_local), *tables)
 
 
 UNROLL = 8
@@ -420,10 +472,10 @@
     capacity = 5 * count // (4 * n_sub)
     leaves = capacity // LEAF
     reads = readers.reshape(n_dom, n_dom, readers.shape[3])
-    near, far, lists, pairs = regroup(
-        positions, masses, velocities, destinations, reads, near_local, near_remote, n_sub, leaves
-    )
+    near, *tables = regroup(positions, masses, destinations, n_sub, leaves)
     near = lax.all_to_all(near, "sub", split_axis=0, concat_axis=0, tiled=True)
+    far, lists, pairs = regroup_velocities(velocities, reads, near_local, near_remote, tables, n_sub, leaves)
+    near, far, lists, pairs = lax.optimization_barrier((near, far, lists, pairs))
     whole = near.reshape(n_sub * leaves, 4, LEAF)
     arrived = [lax.ppermute(whole, "dom", [(i, i ^ k) for i in range(n_dom)]) for k in range(1, n_dom)]
     far = lax.all_to_all(far, "sub", split_axis=0, concat_axis=0, tiled=True)

time: 44.4 us -> 42.8 us (0.964)
  blocking collectives: 13.3 us -> 0 us
  starting transfers between devices: 6.94 us -> 13.3 us
  waiting for transfers between devices: 0.16 us -> 4.45 us
  Pallas kernels: 23.2 us -> 24.1 us
    all_to_all x1 -> x0, blocking collectives: 13.3 us -> none  [on_device(): near = lax.all_to_all(near, 'sub', split_axis=0, concat_axis=0, tiled=True)]
    all_to_all x0 -> x1, starting transfers between devices: none -> 6.33 us  [on_device(): near = lax.all_to_all(near, 'sub', split_axis=0, concat_axis=0, tiled=True)]
    all_to_all x0 -> x1, waiting for transfers between devices: none -> 3.61 us  [on_device(): near = lax.all_to_all(near, 'sub', split_axis=0, concat_axis=0, tiled=True)]
    pallas_call x1 -> x2, Pallas kernels: 5.83 us -> 8.16 us  [the longest x1 4.56 us: regroup(): pl.pallas_call(functools.partial(regroup_kernel, n_sub, leaves), out_shap...]
    ppermute x3, waiting for transfers between devices: 0.16 us -> 0.84 us  [on_device(): lax.ppermute(whole, 'dom', [(i, i ^ k) for i in range(n_dom)])]
    pallas_call x1, Pallas kernels: 10.1 us -> 9.38 us  [remote_forces(): pl.pallas_call(functools.partial(remote_kernel, n_dom), out_shape=(out, o...]
    pallas_call x1, Pallas kernels: 7.28 us -> 6.61 us  [local_forces(): pl.pallas_call(local_kernel, out_shape=(jax.ShapeDtypeStruct((leaves + 1,...]
  transfers between devices with their start and end apart: 4 -> 5, of which waited for: 2 -> 3; matrix products, arithmetic and copies ran while one was open for 0% -> 0% of each run, Pallas kernels for 16% -> 24%
where the time goes in v5:
time: 42.8 us; the launch traced here: 42.5 us
  Pallas kernels  24.1 us (56%)
  starting transfers between devices  13.3 us (31%)
  waiting for transfers between devices  4.45 us (10%)
  between operations  0.67 us (2%)
    pallas_call x1, Pallas kernels, remote_forces(): pl.pallas_call(functools.partial(remote_kernel, n_dom), out_shape=(out, o...  9.38 us
    pallas_call x1, Pallas kernels, local_forces(): pl.pallas_call(local_kernel, out_shape=(jax.ShapeDtypeStruct((leaves + 1,...  6.61 us
    all_to_all x1, starting transfers between devices, on_device(): near = lax.all_to_all(near, 'sub', split_axis=0, concat_axis=0, tiled=True)  6.33 us
    pallas_call x1, Pallas kernels, regroup(): pl.pallas_call(functools.partial(regroup_kernel, n_sub, leaves), out_shap...  4.56 us
    all_to_all x1, waiting for transfers between devices, on_device(): near = lax.all_to_all(near, 'sub', split_axis=0, concat_axis=0, tiled=True)  3.61 us
    pallas_call x1, Pallas kernels, regroup_velocities(): pl.pallas_call(functools.partial(velocity_kernel, n_sub, n_dom, leaves),...  3.6 us
    ppermute x3, starting transfers between devices, on_device(): lax.ppermute(whole, 'dom', [(i, i ^ k) for i in range(n_dom)])  3.55 us
    all_to_all x1, starting transfers between devices, on_device(): far = lax.all_to_all(far, 'sub', split_axis=0, concat_axis=0, tiled=True)  3.38 us
  transfers between devices with their start and end apart: 5, of which 3 were waited for; matrix products, arithmetic and copies ran while one was open for 0% of the time, Pallas kernels for 24%

profile of v5, /device:TPU:0, one launch (start us, length us, event | category | flops | bytes accessed | tf_op | source)
XLA Modules:
  0.0 42.5 jit_solution(9227516388842783637)
XLA Ops:
  0.6 4.6 %regroup.1 = (f32[8,40,128]{2,1,0:T(8,128)}, s32[8,64,128]{2,1,0:T(8,128)S(1)}, s32[8,64,128]{2,1,0:T(8,128)S(1)}, s32[8,64,128]{2,1,0:T(8,128)S(1)}, s32[64,128]{1,0:T(8,128)S(1)}, /*index=5*/s32[64,128]{1,0:T(8,128)S(1)}) custom-call(f32[3,8192]{1,0:T(4,128)} %pos_hbm.1, f32[64,128]{1,0:T(8,128)} %bitcast.10, s32[64,128]{1,0:T(8,128)} %bitcast.11), custom_call_target="tpu_custom_call" | custom-call | tf_op jit(solution)/shard_map/regroup/pallas_call | solution.py:198
  5.2 6.3 %all-to-all-start = ((f32[8,40,128]{2,1,0:T(8,128)}), f32[8,40,128]{2,1,0:T(8,128)S(1)}, u32[]{:S(2)}, u32[]{:S(2)}) async-start(f32[8,40,128]{2,1,0:T(8,128)} %get-tuple-element.17), calls=%async_computation | async-start | bytes 327680 | tf_op jit(solution)/shard_map/all_to_all | solution.py:476
  11.5 3.6 %regroup_velocities.1 = (f32[8,40,128]{2,1,0:T(8,128)}, s32[32,128]{1,0:T(8,128)S(1)}, s32[8,192]{1,0:T(8,128)S(1)}) custom-call(f32[3,8192]{1,0:T(4,128)} %vel_hbm.1, s32[4,4,80]{2,1,0:T(4,128)} %bitcast.12, s32[3,192]{1,0:T(4,128)} %ids_hbm.1, s32[2,192]{1,0:T(2,128)} %local_hbm.1, s32[8,64,128]{2,1,0:T(8,128)S(1)} %get-tuple-element.18.off_ref, ...), custom_call_target="tpu_custom_call" | custom-call | flops 13107200 | bytes 3276800 | tf_op jit(solution)/shard_map/regroup_velocities/pallas_call | solution.py:249
  15.1 3.6 %all-to-all-done = f32[8,40,128]{2,1,0:T(8,128)S(1)} async-done(((f32[8,40,128]{2,1,0:T(8,128)}), f32[8,40,128]{2,1,0:T(8,128)S(1)}, u32[]{:S(2)}, u32[]{:S(2)}) %all-to-all-start) | async-done | bytes 163872 | tf_op jit(solution)/shard_map/all_to_all | solution.py:476
  18.8 3.4 %all-to-all-start.1 = ((f32[8,40,128]{2,1,0:T(8,128)}), f32[8,40,128]{2,1,0:T(8,128)S(1)}, u32[]{:S(2)}, u32[]{:S(2)}) async-start(f32[8,40,128]{2,1,0:T(8,128)} %get-tuple-element.29), calls=%async_computation.1 | async-start | bytes 327680 | tf_op jit(solution)/shard_map/all_to_all | solution.py:481
  22.1 2.5 %collective-permute-start.2 = (f32[80,4,128]{2,1,0:T(4,128)S(1)}, f32[80,4,128]{2,1,0:T(4,128)S(1)}, u32[]{:S(2)}, u32[]{:S(2)}) collective-permute-start(f32[80,4,128]{2,1,0:T(4,128)S(1)} %bitcast.5), channel_id=1, source_target_pairs={{0,24},{8,16},{16,8},{24,0},{1,25},{9,17},{17,9},{25,1},{2,26},{10... | collective-permute-start | bytes 491528 | tf_op jit(solution)/shard_map/ppermute | solution.py:480
  24.7 0.5 %collective-permute-start.1 = (f32[80,4,128]{2,1,0:T(4,128)S(1)}, f32[80,4,128]{2,1,0:T(4,128)S(1)}, u32[]{:S(2)}, u32[]{:S(2)}) collective-permute-start(f32[80,4,128]{2,1,0:T(4,128)S(1)} %bitcast.6), channel_id=1, source_target_pairs={{0,16},{8,24},{16,0},{24,8},{1,17},{9,25},{17,1},{25,9},{2,18},{10... | collective-permute-start | bytes 491528 | tf_op jit(solution)/shard_map/ppermute | solution.py:480
  25.2 0.5 %collective-permute-start = (f32[80,4,128]{2,1,0:T(4,128)S(1)}, f32[80,4,128]{2,1,0:T(4,128)S(1)}, u32[]{:S(2)}, u32[]{:S(2)}) collective-permute-start(f32[80,4,128]{2,1,0:T(4,128)S(1)} %bitcast.7), channel_id=1, source_target_pairs={{0,8},{8,0},{16,24},{24,16},{1,9},{9,1},{17,25},{25,17},{2,10},{10... | collective-permute-start | bytes 491528 | tf_op jit(solution)/shard_map/ppermute | solution.py:480
  25.7 6.6 %local_forces.1 = (f32[81,4,8,128]{3,2,1,0:T(8,128)S(1)}, f32[81,3,8,128]{3,2,1,0:T(8,128)S(1)}) custom-call(s32[8,192]{1,0:T(8,128)S(1)} %get-tuple-element.27.ids_ref.pairs_ref, f32[320,128]{1,0:T(8,128)S(1)} %bitcast.8), custom_call_target="tpu_custom_call" | custom-call | flops 56623104 | bytes 327680 | tf_op jit(solution)/shard_map/local_forces/pallas_call | solution.py:360
  32.3 0.0 collective-permute-done.2.rest_2_
  32.3 0.7 %collective-permute-done.1.rest_1_ = f32[80,4,128]{2,1,0:T(4,128)S(1)} collective-permute-done((f32[80,4,128]{2,1,0:T(4,128)S(1)}, f32[80,4,128]{2,1,0:T(4,128)S(1)}, u32[]{:S(2)}, u32[]{:S(2)}) %collective-permute-start.1) | collective-permute-done | bytes 163872 | tf_op jit(solution)/shard_map/ppermute | solution.py:480
  33.1 0.1 collective-permute-done.rest_0_
  33.2 0.0 all-to-all-done.1.vel_ref
  33.2 9.4 %remote_forces.1 = (f32[3,10240]{1,0:T(4,128)}, f32[3,10240]{1,0:T(4,128)}) custom-call(s32[32,128]{1,0:T(8,128)S(1)} %get-tuple-element.26.leaf_list, s32[8,192]{1,0:T(8,128)S(1)} %get-tuple-element.27.ids_ref.pairs_ref, f32[320,128]{1,0:T(8,128)S(1)} %bitcast.9, f32[8,40,128]{2,1,0:T(8,128)S(1)} %all-to-all-done.1.vel_ref, ...), custom_call_target="tpu_custom_call" | custom-call | flops 56623104 | bytes 983040 | tf_op jit(solution)/shard_map/remote_forces/pallas_call | solution.py:448
Async XLA Ops:
  5.2 13.6 %all-to-all-start = ((f32[8,40,128]{2,1,0:T(8,128)}), f32[8,40,128]{2,1,0:T(8,128)S(1)}, u32[]{:S(2)}, u32[]{:S(2)}) async-start(f32[8,40,128]{2,1,0:T(8,128)} %get-tuple-element.17), calls=%async_computation | async-start | bytes 327680 | tf_op jit(solution)/shard_map/all_to_all | solution.py:476
  18.8 14.4 %all-to-all-start.1 = ((f32[8,40,128]{2,1,0:T(8,128)}), f32[8,40,128]{2,1,0:T(8,128)S(1)}, u32[]{:S(2)}, u32[]{:S(2)}) async-start(f32[8,40,128]{2,1,0:T(8,128)} %get-tuple-element.29), calls=%async_computation.1 | async-start | bytes 327680 | tf_op jit(solution)/shard_map/all_to_all | solution.py:481
  22.1 10.2 %collective-permute-start.2 = (f32[80,4,128]{2,1,0:T(4,128)S(1)}, f32[80,4,128]{2,1,0:T(4,128)S(1)}, u32[]{:S(2)}, u32[]{:S(2)}) collective-permute-start(f32[80,4,128]{2,1,0:T(4,128)S(1)} %bitcast.5), channel_id=1, source_target_pairs={{0,24},{8,16},{16,8},{24,0},{1,25},{9,17},{17,9},{25,1},{2,26},{10... | collective-permute-start | bytes 491528 | tf_op jit(solution)/shard_map/ppermute | solution.py:480
  24.7 8.4 %collective-permute-start.1 = (f32[80,4,128]{2,1,0:T(4,128)S(1)}, f32[80,4,128]{2,1,0:T(4,128)S(1)}, u32[]{:S(2)}, u32[]{:S(2)}) collective-permute-start(f32[80,4,128]{2,1,0:T(4,128)S(1)} %bitcast.6), channel_id=1, source_target_pairs={{0,16},{8,24},{16,0},{24,8},{1,17},{9,25},{17,1},{25,9},{2,18},{10... | collective-permute-start | bytes 491528 | tf_op jit(solution)/shard_map/ppermute | solution.py:480
  25.2 8.0 %collective-permute-start = (f32[80,4,128]{2,1,0:T(4,128)S(1)}, f32[80,4,128]{2,1,0:T(4,128)S(1)}, u32[]{:S(2)}, u32[]{:S(2)}) collective-permute-start(f32[80,4,128]{2,1,0:T(4,128)S(1)} %bitcast.7), channel_id=1, source_target_pairs={{0,8},{8,0},{16,24},{24,16},{1,9},{9,1},{17,25},{25,17},{2,10},{10... | collective-permute-start | bytes 491528 | tf_op jit(solution)/shard_map/ppermute | solution.py:480

commit v6 on v5

--- a/solution.py
+++ b/solution.py
@@ -80,7 +80,8 @@
     pairs_ref[1:2, :] = jnp.maximum((source_dom ^ me) - 1, 0) * SLOTS + looked[0:1]
     pairs_ref[2:3, :] = looked[1:2]
     pairs_ref[3:5, :] = local_ref[...]
-    pairs_ref[5:8, :] = jnp.zeros((3, pairs), I32)
+    pairs_ref[5:6, :] = jnp.maximum((source_dom ^ me) - 1, 0) * leaves + source_leaf
+    pairs_ref[6:8, :] = jnp.zeros((2, pairs), I32)
 
 
 def start_copies(sems, *pairs):
@@ -118,7 +119,7 @@
             new.append(jnp.where(low + count >= LEAF, fresh, tail))
         return tuple(new)
 
-    tails = lax.fori_loop(0, half, step, (jnp.zeros((8, LEAF), F32),) * n_sub, unroll=8)
+    tails = lax.fori_loop(0, half, step, (jnp.zeros((8, LEAF), F32),) * n_sub, unroll=16)
     for e in range(n_sub):
         tiles[leaf_idx[half - 1, n_sub + e], 0:4, :] = tails[e][0:4]
         tiles[leaf_idx[2 * half - 1, n_sub + e], 4:8, :] = tails[e][4:8]
@@ -139,7 +140,8 @@
     weights = jnp.concatenate([as_bf16(row <= iota((LEAF, LEAF), 1)), jnp.ones((LEAF, LEAF), BF16)], axis=1)
     earlier = as_bf16(iota((blocks, blocks), 1) < iota((blocks, blocks), 0))
     lane64 = iota((blocks, LEAF), 1)
-    loads[0].wait()
+    for load in loads:
+        load.wait()
     dest = dest_ref[...]
     masks = [dest == e for e in range(n_sub)]
     ones_of = jnp.concatenate([as_bf16(m) for m in masks], axis=0)
@@ -164,8 +166,6 @@
     copy = pltpu.make_async_copy(leaf_vec, leaf_idx, sems.at[3])
     copy.start()
     perm_ref[...] = place.astype(I32)
-    for load in loads[1:]:
-        load.wait()
     for b in range(blocks):
         at = b // half * 4
         table[b % half, at:at + 3, :] = pos_ref[:, b * LEAF:(b + 1) * LEAF]
@@ -185,7 +185,7 @@
         ordered[b] = lane_gather(table[b], jnp.where(upper_half, inverse[0], inverse[1]))
         return 0
 
-    lax.fori_loop(0, half, order, 0, unroll=16)
+    lax.fori_loop(0, half, order, 0, unroll=half)
     copy.wait()
     place_particles(n_sub, leaves, ordered, (off_ref, cnt_ref, start_ref), leaf_idx, tiles, near_ref)
 
@@ -282,7 +282,7 @@
             wide_ref[k, h] = lane_gather(tile_of(h), group + k)
 
 
-def live_pairs(targets, sources, flags, target_mass, source_mass, list_ref):
+def live_pairs(targets, sources, flags, target_mass, keys, source_mass, list_ref):
     pairs = targets.shape[1]
     spare = target_mass.shape[0]
 
@@ -291,7 +291,7 @@
         pick = as_bf16((iota((mass.shape[0], pairs), 0) == ids) & some)
         return jnp.dot(jnp.ones((8, mass.shape[0]), BF16), pick, preferred_element_type=F32)
 
-    live = filled(targets, target_mass) * filled(sources, source_mass)
+    live = filled(targets, target_mass) * filled(keys, source_mass)
     if flags is not None:
         live = live * flags.astype(F32)
     row, col = iota((pairs, pairs), 0), iota((pairs, pairs), 1)
@@ -322,8 +322,10 @@
             weight = (there[3] * inv) * (inv * inv)
             terms = [weight * delta[c] for c in range(3)]
             sums = terms if sums is None else [sums[c] + terms[c] for c in range(3)]
+            if k == 7:
+                early, sums = sums, None
         for c in range(3):
-            acc_ref[t, c] += sums[c]
+            acc_ref[t, c] += sums[c] + early[c]
 
     def step(j, _):
         for u in range(UNROLL):
@@ -336,7 +338,7 @@
 def local_kernel(ids_ref, src_ref, acc_ref, here_ref, wide_ref, list_vec, list_ref, sem):
     leaves = acc_ref.shape[0] - 1
     mass = src_ref[pl.ds(3, leaves, stride=4), :]
-    live_pairs(ids_ref[3:4, :], ids_ref[4:5, :], None, mass, mass, list_vec)
+    live_pairs(ids_ref[3:4, :], ids_ref[4:5, :], None, mass, ids_ref[4:5, :], mass, list_vec)
     copy = pltpu.make_async_copy(list_vec, list_ref, sem)
     copy.start()
     spread_tiles(lambda h: src_ref[8 * h:8 * h + 8, :], leaves // 2, wide_ref)
@@ -407,17 +409,17 @@
     leaves = acc_ref.shape[0] - 1
     acc_ref[...] = jnp.zeros_like(acc_ref)
     slots = (n_dom - 1) * SLOTS
+    live_pairs(
+        pairs_ref[0:1, :], pairs_ref[1:2, :], pairs_ref[2:3, :], tgt_ref[pl.ds(3, leaves, stride=4), :],
+        pairs_ref[5:6, :], jnp.concatenate([ref[:, 3, :] for ref in src_refs], axis=0), list_vec,
+    )
+    copy = pltpu.make_async_copy(list_vec, list_ref, sems.at[1])
+    copy.start()
     load.wait()
     for k in range(1, n_dom):
         for j in range(SLOTS):
             at = 4 * ((k - 1) * SLOTS + j)
             chosen_ref[at:at + 4, :] = src_refs[k - 1][leaf_ref[j, me ^ k]]
-    live_pairs(
-        pairs_ref[0:1, :], pairs_ref[1:2, :], pairs_ref[2:3, :],
-        tgt_ref[pl.ds(3, leaves, stride=4), :], chosen_ref[pl.ds(3, slots, stride=4), :], list_vec,
-    )
-    copy = pltpu.make_async_copy(list_vec, list_ref, sems.at[1])
-    copy.start()
     spread_tiles(lambda h: chosen_ref[8 * h:8 * h + 8, :], slots // 2, wide_ref)
     copy.wait()
     pair_loop(list_ref, here_ref, wide_ref, acc_ref)

time: 42.8 us -> 42.8 us (level)
  Pallas kernels: 24.1 us -> 23.4 us
  waiting for transfers between devices: 4.45 us -> 4.91 us
  transfers between devices with their start and end apart: 5 -> 5, of which waited for: 3 -> 3; matrix products, arithmetic and copies ran while one was open for 0% -> 0% of each run, Pallas kernels for 24% -> 23%
where the time goes in v6:
time: 42.8 us; the launch traced here: 42.2 us
  Pallas kernels  23.4 us (55%)
  starting transfers between devices  13.3 us (31%)
  waiting for transfers between devices  4.91 us (11%)
  between operations  0.67 us (2%)
    pallas_call x1, Pallas kernels, remote_forces(): pl.pallas_call(functools.partial(remote_kernel, n_dom), out_shape=(out, o...  9.28 us
    all_to_all x1, starting transfers between devices, on_device(): near = lax.all_to_all(near, 'sub', split_axis=0, concat_axis=0, tiled=True)  6.34 us
    pallas_call x1, Pallas kernels, local_forces(): pl.pallas_call(local_kernel, out_shape=(jax.ShapeDtypeStruct((leaves + 1,...  6.23 us
    pallas_call x1, Pallas kernels, regroup(): pl.pallas_call(functools.partial(regroup_kernel, n_sub, leaves), out_shap...  4.33 us
    all_to_all x1, waiting for transfers between devices, on_device(): near = lax.all_to_all(near, 'sub', split_axis=0, concat_axis=0, tiled=True)  3.68 us
    ppermute x3, starting transfers between devices, on_device(): lax.ppermute(whole, 'dom', [(i, i ^ k) for i in range(n_dom)])  3.55 us
    pallas_call x1, Pallas kernels, regroup_velocities(): pl.pallas_call(functools.partial(velocity_kernel, n_sub, n_dom, leaves),...  3.53 us
    all_to_all x1, starting transfers between devices, on_device(): far = lax.all_to_all(far, 'sub', split_axis=0, concat_axis=0, tiled=True)  3.38 us
  transfers between devices with their start and end apart: 5, of which 3 were waited for; matrix products, arithmetic and copies ran while one was open for 0% of the time, Pallas kernels for 23%

profile of v6, /device:TPU:0, one launch (start us, length us, event | category | flops | bytes accessed | tf_op | source)
XLA Modules:
  0.0 42.2 jit_solution(6427276829915389031)
XLA Ops:
  0.6 4.3 %regroup.1 = (f32[8,40,128]{2,1,0:T(8,128)}, s32[8,64,128]{2,1,0:T(8,128)S(1)}, s32[8,64,128]{2,1,0:T(8,128)S(1)}, s32[8,64,128]{2,1,0:T(8,128)S(1)}, s32[64,128]{1,0:T(8,128)S(1)}, /*index=5*/s32[64,128]{1,0:T(8,128)S(1)}) custom-call(f32[3,8192]{1,0:T(4,128)} %pos_hbm.1, f32[64,128]{1,0:T(8,128)} %bitcast.10, s32[64,128]{1,0:T(8,128)} %bitcast.11), custom_call_target="tpu_custom_call" | custom-call | tf_op jit(solution)/shard_map/regroup/pallas_call | solution.py:198
  5.0 6.3 %all-to-all-start = ((f32[8,40,128]{2,1,0:T(8,128)}), f32[8,40,128]{2,1,0:T(8,128)S(1)}, u32[]{:S(2)}, u32[]{:S(2)}) async-start(f32[8,40,128]{2,1,0:T(8,128)} %get-tuple-element.17), calls=%async_computation | async-start | bytes 327680 | tf_op jit(solution)/shard_map/all_to_all | solution.py:478
  11.3 3.5 %regroup_velocities.1 = (f32[8,40,128]{2,1,0:T(8,128)}, s32[32,128]{1,0:T(8,128)S(1)}, s32[8,192]{1,0:T(8,128)S(1)}) custom-call(f32[3,8192]{1,0:T(4,128)} %vel_hbm.1, s32[4,4,80]{2,1,0:T(4,128)} %bitcast.12, s32[3,192]{1,0:T(4,128)} %ids_hbm.1, s32[2,192]{1,0:T(2,128)} %local_hbm.1, s32[8,64,128]{2,1,0:T(8,128)S(1)} %get-tuple-element.18.off_ref, ...), custom_call_target="tpu_custom_call" | custom-call | flops 13107200 | bytes 3276800 | tf_op jit(solution)/shard_map/regroup_velocities/pallas_call | solution.py:249
  14.8 3.7 %all-to-all-done = f32[8,40,128]{2,1,0:T(8,128)S(1)} async-done(((f32[8,40,128]{2,1,0:T(8,128)}), f32[8,40,128]{2,1,0:T(8,128)S(1)}, u32[]{:S(2)}, u32[]{:S(2)}) %all-to-all-start) | async-done | bytes 163872 | tf_op jit(solution)/shard_map/all_to_all | solution.py:478
  18.5 3.4 %all-to-all-start.1 = ((f32[8,40,128]{2,1,0:T(8,128)}), f32[8,40,128]{2,1,0:T(8,128)S(1)}, u32[]{:S(2)}, u32[]{:S(2)}) async-start(f32[8,40,128]{2,1,0:T(8,128)} %get-tuple-element.29), calls=%async_computation.1 | async-start | bytes 327680 | tf_op jit(solution)/shard_map/all_to_all | solution.py:483
  21.9 2.5 %collective-permute-start.2 = (f32[80,4,128]{2,1,0:T(4,128)S(1)}, f32[80,4,128]{2,1,0:T(4,128)S(1)}, u32[]{:S(2)}, u32[]{:S(2)}) collective-permute-start(f32[80,4,128]{2,1,0:T(4,128)S(1)} %bitcast.5), channel_id=1, source_target_pairs={{0,24},{8,16},{16,8},{24,0},{1,25},{9,17},{17,9},{25,1},{2,26},{10... | collective-permute-start | bytes 491528 | tf_op jit(solution)/shard_map/ppermute | solution.py:482
  24.4 0.5 %collective-permute-start.1 = (f32[80,4,128]{2,1,0:T(4,128)S(1)}, f32[80,4,128]{2,1,0:T(4,128)S(1)}, u32[]{:S(2)}, u32[]{:S(2)}) collective-permute-start(f32[80,4,128]{2,1,0:T(4,128)S(1)} %bitcast.6), channel_id=1, source_target_pairs={{0,16},{8,24},{16,0},{24,8},{1,17},{9,25},{17,1},{25,9},{2,18},{10... | collective-permute-start | bytes 491528 | tf_op jit(solution)/shard_map/ppermute | solution.py:482
  24.9 0.5 %collective-permute-start = (f32[80,4,128]{2,1,0:T(4,128)S(1)}, f32[80,4,128]{2,1,0:T(4,128)S(1)}, u32[]{:S(2)}, u32[]{:S(2)}) collective-permute-start(f32[80,4,128]{2,1,0:T(4,128)S(1)} %bitcast.7), channel_id=1, source_target_pairs={{0,8},{8,0},{16,24},{24,16},{1,9},{9,1},{17,25},{25,17},{2,10},{10... | collective-permute-start | bytes 491528 | tf_op jit(solution)/shard_map/ppermute | solution.py:482
  25.5 6.2 %local_forces.1 = (f32[81,4,8,128]{3,2,1,0:T(8,128)S(1)}, f32[81,3,8,128]{3,2,1,0:T(8,128)S(1)}) custom-call(s32[8,192]{1,0:T(8,128)S(1)} %get-tuple-element.27.ids_ref.pairs_ref, f32[320,128]{1,0:T(8,128)S(1)} %bitcast.8), custom_call_target="tpu_custom_call" | custom-call | flops 56623104 | bytes 327680 | tf_op jit(solution)/shard_map/local_forces/pallas_call | solution.py:362
  31.7 0.0 collective-permute-done.2.rest_2_
  31.7 1.1 %collective-permute-done.1.rest_1_ = f32[80,4,128]{2,1,0:T(4,128)S(1)} collective-permute-done((f32[80,4,128]{2,1,0:T(4,128)S(1)}, f32[80,4,128]{2,1,0:T(4,128)S(1)}, u32[]{:S(2)}, u32[]{:S(2)}) %collective-permute-start.1) | collective-permute-done | bytes 163872 | tf_op jit(solution)/shard_map/ppermute | solution.py:482
  32.8 0.1 collective-permute-done.rest_0_
  32.9 0.0 all-to-all-done.1.vel_ref
  32.9 9.3 %remote_forces.1 = (f32[3,10240]{1,0:T(4,128)}, f32[3,10240]{1,0:T(4,128)}) custom-call(s32[32,128]{1,0:T(8,128)S(1)} %get-tuple-element.26.leaf_list, s32[8,192]{1,0:T(8,128)S(1)} %get-tuple-element.27.ids_ref.pairs_ref, f32[320,128]{1,0:T(8,128)S(1)} %bitcast.9, f32[8,40,128]{2,1,0:T(8,128)S(1)} %all-to-all-done.1.vel_ref, ...), custom_call_target="tpu_custom_call" | custom-call | flops 56623104 | bytes 983040 | tf_op jit(solution)/shard_map/remote_forces/pallas_call | solution.py:450
Async XLA Ops:
  5.0 13.6 %all-to-all-start = ((f32[8,40,128]{2,1,0:T(8,128)}), f32[8,40,128]{2,1,0:T(8,128)S(1)}, u32[]{:S(2)}, u32[]{:S(2)}) async-start(f32[8,40,128]{2,1,0:T(8,128)} %get-tuple-element.17), calls=%async_computation | async-start | bytes 327680 | tf_op jit(solution)/shard_map/all_to_all | solution.py:478
  18.5 14.4 %all-to-all-start.1 = ((f32[8,40,128]{2,1,0:T(8,128)}), f32[8,40,128]{2,1,0:T(8,128)S(1)}, u32[]{:S(2)}, u32[]{:S(2)}) async-start(f32[8,40,128]{2,1,0:T(8,128)} %get-tuple-element.29), calls=%async_computation.1 | async-start | bytes 327680 | tf_op jit(solution)/shard_map/all_to_all | solution.py:483
  21.9 9.8 %collective-permute-start.2 = (f32[80,4,128]{2,1,0:T(4,128)S(1)}, f32[80,4,128]{2,1,0:T(4,128)S(1)}, u32[]{:S(2)}, u32[]{:S(2)}) collective-permute-start(f32[80,4,128]{2,1,0:T(4,128)S(1)} %bitcast.5), channel_id=1, source_target_pairs={{0,24},{8,16},{16,8},{24,0},{1,25},{9,17},{17,9},{25,1},{2,26},{10... | collective-permute-start | bytes 491528 | tf_op jit(solution)/shard_map/ppermute | solution.py:482
  24.4 8.4 %collective-permute-start.1 = (f32[80,4,128]{2,1,0:T(4,128)S(1)}, f32[80,4,128]{2,1,0:T(4,128)S(1)}, u32[]{:S(2)}, u32[]{:S(2)}) collective-permute-start(f32[80,4,128]{2,1,0:T(4,128)S(1)} %bitcast.6), channel_id=1, source_target_pairs={{0,16},{8,24},{16,0},{24,8},{1,17},{9,25},{17,1},{25,9},{2,18},{10... | collective-permute-start | bytes 491528 | tf_op jit(solution)/shard_map/ppermute | solution.py:482
  24.9 8.0 %collective-permute-start = (f32[80,4,128]{2,1,0:T(4,128)S(1)}, f32[80,4,128]{2,1,0:T(4,128)S(1)}, u32[]{:S(2)}, u32[]{:S(2)}) collective-permute-start(f32[80,4,128]{2,1,0:T(4,128)S(1)} %bitcast.7), channel_id=1, source_target_pairs={{0,8},{8,0},{16,24},{24,16},{1,9},{9,1},{17,25},{25,17},{2,10},{10... | collective-permute-start | bytes 491528 | tf_op jit(solution)/shard_map/ppermute | solution.py:482

commit v7 on v6

--- a/solution.py
+++ b/solution.py
@@ -119,7 +119,7 @@
             new.append(jnp.where(low + count >= LEAF, fresh, tail))
         return tuple(new)
 
-    tails = lax.fori_loop(0, half, step, (jnp.zeros((8, LEAF), F32),) * n_sub, unroll=16)
+    tails = lax.fori_loop(0, half, step, (jnp.zeros((8, LEAF), F32),) * n_sub, unroll=half)
     for e in range(n_sub):
         tiles[leaf_idx[half - 1, n_sub + e], 0:4, :] = tails[e][0:4]
         tiles[leaf_idx[2 * half - 1, n_sub + e], 4:8, :] = tails[e][4:8]
@@ -273,6 +273,7 @@
 
 
 UNROLL = 8
+HEAD = 8
 
 
 def spread_tiles(tile_of, count, wide_ref):
@@ -294,6 +295,7 @@
     live = filled(targets, target_mass) * filled(keys, source_mass)
     if flags is not None:
         live = live * flags.astype(F32)
+    live = jnp.where(iota((8, pairs), 1) < HEAD, 0.0, live)
     row, col = iota((pairs, pairs), 0), iota((pairs, pairs), 1)
     place = jnp.dot(live.astype(BF16), as_bf16(row < col), preferred_element_type=F32).astype(I32)
     move = as_bf16((place[:1] == row) & (live[:1] > 0.0))
@@ -307,10 +309,8 @@
     list_ref[...] = jnp.where(line == 2, count, moved)
 
 
-def pair_loop(list_ref, here_ref, wide_ref, acc_ref):
-    def pair(i):
-        t = list_ref[0, i]
-        s = list_ref[1, i]
+def pair_loop(head_of, copy, list_ref, here_ref, wide_ref, acc_ref):
+    def pair(t, s):
         h, first = s >> 1, (s & 1) * 4
         here = [here_ref[t, c] for c in range(3)]
         sums = None
@@ -329,17 +329,22 @@
 
     def step(j, _):
         for u in range(UNROLL):
-            pair(j * UNROLL + u)
+            pair(list_ref[0, j * UNROLL + u], list_ref[1, j * UNROLL + u])
         return 0
 
+    for i in range(HEAD):
+        pair(*head_of(i))
+    copy.wait()
     lax.fori_loop(0, (list_ref[2, 0] + UNROLL - 1) // UNROLL, step, 0)
 
 
-def local_kernel(ids_ref, src_ref, acc_ref, here_ref, wide_ref, list_vec, list_ref, sem):
+def local_kernel(ids_ref, src_ref, acc_ref, here_ref, wide_ref, list_vec, list_ref, raw_ref, sems):
+    raw = pltpu.make_async_copy(ids_ref, raw_ref, sems.at[1])
+    raw.start()
     leaves = acc_ref.shape[0] - 1
     mass = src_ref[pl.ds(3, leaves, stride=4), :]
     live_pairs(ids_ref[3:4, :], ids_ref[4:5, :], None, mass, ids_ref[4:5, :], mass, list_vec)
-    copy = pltpu.make_async_copy(list_vec, list_ref, sem)
+    copy = pltpu.make_async_copy(list_vec, list_ref, sems.at[0])
     copy.start()
     spread_tiles(lambda h: src_ref[8 * h:8 * h + 8, :], leaves // 2, wide_ref)
     fold = iota((8, LEAF), 0) * 16 + (iota((8, LEAF), 1) & 15)
@@ -349,8 +354,8 @@
             here_ref[t, c] = lane_gather(jnp.broadcast_to(line, (8, LEAF)), fold)
     here_ref[leaves] = jnp.zeros((3, 8, LEAF), F32)
     acc_ref[...] = jnp.zeros_like(acc_ref)
-    copy.wait()
-    pair_loop(list_ref, here_ref, wide_ref, acc_ref)
+    raw.wait()
+    pair_loop(lambda i: (raw_ref[3, i], raw_ref[4, i]), copy, list_ref, here_ref, wide_ref, acc_ref)
 
 
 def local_forces(ids, near):
@@ -371,7 +376,8 @@
             pltpu.VMEM((16, rows // 8, 8, LEAF), F32),
             pltpu.VMEM((8, pairs), I32),
             pltpu.SMEM((8, pairs), I32),
-            pltpu.SemaphoreType.DMA,
+            pltpu.SMEM((8, pairs), I32),
+            pltpu.SemaphoreType.DMA((2,)),
         ],
         compiler_params=params(),
         cost_estimate=pl.CostEstimate(flops=18 * work, transcendentals=work, bytes_accessed=8 * rows * LEAF),
@@ -402,12 +408,14 @@
 def remote_kernel(n_dom, leaf_list, pairs_ref, tgt_ref, vel_ref, local_ref, here_ref, *rest):
     src_refs = rest[:n_dom - 1]
     (accel_ref, kicked_ref, leaf_ref, chosen_ref, wide_ref, acc_ref, list_vec, list_ref,
-     sems) = rest[n_dom - 1:]
+     raw_ref, sems) = rest[n_dom - 1:]
     me = lax.axis_index("dom")
     load = pltpu.make_async_copy(leaf_list, leaf_ref, sems.at[0])
     load.start()
+    raw = pltpu.make_async_copy(pairs_ref, raw_ref, sems.at[2])
+    raw.start()
     leaves = acc_ref.shape[0] - 1
-    acc_ref[...] = jnp.zeros_like(acc_ref)
+    acc_ref[...] = local_ref[...]
     slots = (n_dom - 1) * SLOTS
     live_pairs(
         pairs_ref[0:1, :], pairs_ref[1:2, :], pairs_ref[2:3, :], tgt_ref[pl.ds(3, leaves, stride=4), :],
@@ -421,9 +429,12 @@
             at = 4 * ((k - 1) * SLOTS + j)
             chosen_ref[at:at + 4, :] = src_refs[k - 1][leaf_ref[j, me ^ k]]
     spread_tiles(lambda h: chosen_ref[8 * h:8 * h + 8, :], slots // 2, wide_ref)
-    copy.wait()
-    pair_loop(list_ref, here_ref, wide_ref, acc_ref)
-    total = gravity * unpack_sums([local_ref, acc_ref], leaves)
+    raw.wait()
+    pair_loop(
+        lambda i: (jnp.where(raw_ref[2, i] > 0, raw_ref[0, i], leaves), raw_ref[1, i]),
+        copy, list_ref, here_ref, wide_ref, acc_ref,
+    )
+    total = gravity * unpack_sums([acc_ref], leaves)
     first = iota((8, LEAF), 0) < 4
     per = vel_ref.shape[1]
     for h in range(leaves // 2):
@@ -459,7 +470,8 @@
             pltpu.VMEM((leaves + 1, 4, 8, LEAF), F32),
             pltpu.VMEM(pairs.shape, I32),
             pltpu.SMEM(pairs.shape, I32),
-            pltpu.SemaphoreType.DMA((2,)),
+            pltpu.SMEM(pairs.shape, I32),
+            pltpu.SemaphoreType.DMA((3,)),
         ],
         compiler_params=params(),
         cost_estimate=pl.CostEstimate(flops=18 * work, transcendentals=work, bytes_accessed=24 * rows * LEAF),

time: 42.8 us -> 42.3 us (0.988)
  waiting for transfers between devices: 4.91 us -> 3.92 us
  Pallas kernels: 23.4 us -> 24.1 us
    ppermute x3, waiting for transfers between devices: 1.22 us -> 0.06 us  [on_device(): lax.ppermute(whole, 'dom', [(i, i ^ k) for i in range(n_dom)])]
    pallas_call x1, Pallas kernels: 6.23 us -> 7.38 us  [local_forces(): pl.pallas_call(local_kernel, out_shape=(jax.ShapeDtypeStruct((leaves + 1,...]
  transfers between devices with their start and end apart: 5 -> 5, of which waited for: 3 -> 2; matrix products, arithmetic and copies ran while one was open for 0% -> 0% of each run, Pallas kernels for 23% -> 26%
where the time goes in v7:
time: 42.3 us; the launch traced here: 42 us
  Pallas kernels  24.1 us (57%)
  starting transfers between devices  13.3 us (31%)
  waiting for transfers between devices  3.92 us (9%)
  between operations  0.68 us (2%)
    pallas_call x1, Pallas kernels, remote_forces(): pl.pallas_call(functools.partial(remote_kernel, n_dom), out_shape=(out, o...  9.21 us
    pallas_call x1, Pallas kernels, local_forces(): pl.pallas_call(local_kernel, out_shape=(jax.ShapeDtypeStruct((leaves + 1,...  7.38 us
    all_to_all x1, starting transfers between devices, on_device(): near = lax.all_to_all(near, 'sub', split_axis=0, concat_axis=0, tiled=True)  6.34 us
    pallas_call x1, Pallas kernels, regroup(): pl.pallas_call(functools.partial(regroup_kernel, n_sub, leaves), out_shap...  4.13 us
    all_to_all x1, waiting for transfers between devices, on_device(): near = lax.all_to_all(near, 'sub', split_axis=0, concat_axis=0, tiled=True)  3.86 us
    ppermute x3, starting transfers between devices, on_device(): lax.ppermute(whole, 'dom', [(i, i ^ k) for i in range(n_dom)])  3.55 us
    all_to_all x1, starting transfers between devices, on_device(): far = lax.all_to_all(far, 'sub', split_axis=0, concat_axis=0, tiled=True)  3.38 us
    pallas_call x1, Pallas kernels, regroup_velocities(): pl.pallas_call(functools.partial(velocity_kernel, n_sub, n_dom, leaves),...  3.35 us
  transfers between devices with their start and end apart: 5, of which 2 were waited for; matrix products, arithmetic and copies ran while one was open for 0% of the time, Pallas kernels for 26%

profile of v7, /device:TPU:0, one launch (start us, length us, event | category | flops | bytes accessed | tf_op | source)
XLA Modules:
  0.0 42.0 jit_solution(10624581111177939930)
XLA Ops:
  0.6 4.1 %regroup.1 = (f32[8,40,128]{2,1,0:T(8,128)}, s32[8,64,128]{2,1,0:T(8,128)S(1)}, s32[8,64,128]{2,1,0:T(8,128)S(1)}, s32[8,64,128]{2,1,0:T(8,128)S(1)}, s32[64,128]{1,0:T(8,128)S(1)}, /*index=5*/s32[64,128]{1,0:T(8,128)S(1)}) custom-call(f32[3,8192]{1,0:T(4,128)} %pos_hbm.1, f32[64,128]{1,0:T(8,128)} %bitcast.10, s32[64,128]{1,0:T(8,128)} %bitcast.11), custom_call_target="tpu_custom_call" | custom-call | tf_op jit(solution)/shard_map/regroup/pallas_call | solution.py:198
  4.8 6.3 %all-to-all-start = ((f32[8,40,128]{2,1,0:T(8,128)}), f32[8,40,128]{2,1,0:T(8,128)S(1)}, u32[]{:S(2)}, u32[]{:S(2)}) async-start(f32[8,40,128]{2,1,0:T(8,128)} %get-tuple-element.17), calls=%async_computation | async-start | bytes 327680 | tf_op jit(solution)/shard_map/all_to_all | solution.py:490
  11.1 3.4 %regroup_velocities.1 = (f32[8,40,128]{2,1,0:T(8,128)}, s32[32,128]{1,0:T(8,128)S(1)}, s32[8,192]{1,0:T(8,128)S(1)}) custom-call(f32[3,8192]{1,0:T(4,128)} %vel_hbm.1, s32[4,4,80]{2,1,0:T(4,128)} %bitcast.12, s32[3,192]{1,0:T(4,128)} %ids_hbm.1, s32[2,192]{1,0:T(2,128)} %local_hbm.1, s32[8,64,128]{2,1,0:T(8,128)S(1)} %get-tuple-element.18.off_ref, ...), custom_call_target="tpu_custom_call" | custom-call | flops 13107200 | bytes 3276800 | tf_op jit(solution)/shard_map/regroup_velocities/pallas_call | solution.py:249
  14.5 3.9 %all-to-all-done = f32[8,40,128]{2,1,0:T(8,128)S(1)} async-done(((f32[8,40,128]{2,1,0:T(8,128)}), f32[8,40,128]{2,1,0:T(8,128)S(1)}, u32[]{:S(2)}, u32[]{:S(2)}) %all-to-all-start) | async-done | bytes 163872 | tf_op jit(solution)/shard_map/all_to_all | solution.py:490
  18.3 3.4 %all-to-all-start.1 = ((f32[8,40,128]{2,1,0:T(8,128)}), f32[8,40,128]{2,1,0:T(8,128)S(1)}, u32[]{:S(2)}, u32[]{:S(2)}) async-start(f32[8,40,128]{2,1,0:T(8,128)} %get-tuple-element.29), calls=%async_computation.1 | async-start | bytes 327680 | tf_op jit(solution)/shard_map/all_to_all | solution.py:495
  21.7 2.5 %collective-permute-start.2 = (f32[80,4,128]{2,1,0:T(4,128)S(1)}, f32[80,4,128]{2,1,0:T(4,128)S(1)}, u32[]{:S(2)}, u32[]{:S(2)}) collective-permute-start(f32[80,4,128]{2,1,0:T(4,128)S(1)} %bitcast.5), channel_id=1, source_target_pairs={{0,24},{8,16},{16,8},{24,0},{1,25},{9,17},{17,9},{25,1},{2,26},{10... | collective-permute-start | bytes 491528 | tf_op jit(solution)/shard_map/ppermute | solution.py:494
  24.2 0.5 %collective-permute-start.1 = (f32[80,4,128]{2,1,0:T(4,128)S(1)}, f32[80,4,128]{2,1,0:T(4,128)S(1)}, u32[]{:S(2)}, u32[]{:S(2)}) collective-permute-start(f32[80,4,128]{2,1,0:T(4,128)S(1)} %bitcast.6), channel_id=1, source_target_pairs={{0,16},{8,24},{16,0},{24,8},{1,17},{9,25},{17,1},{25,9},{2,18},{10... | collective-permute-start | bytes 491528 | tf_op jit(solution)/shard_map/ppermute | solution.py:494
  24.7 0.5 %collective-permute-start = (f32[80,4,128]{2,1,0:T(4,128)S(1)}, f32[80,4,128]{2,1,0:T(4,128)S(1)}, u32[]{:S(2)}, u32[]{:S(2)}) collective-permute-start(f32[80,4,128]{2,1,0:T(4,128)S(1)} %bitcast.7), channel_id=1, source_target_pairs={{0,8},{8,0},{16,24},{24,16},{1,9},{9,1},{17,25},{25,17},{2,10},{10... | collective-permute-start | bytes 491528 | tf_op jit(solution)/shard_map/ppermute | solution.py:494
  25.3 7.4 %local_forces.1 = (f32[81,4,8,128]{3,2,1,0:T(8,128)S(1)}, f32[81,3,8,128]{3,2,1,0:T(8,128)S(1)}) custom-call(s32[8,192]{1,0:T(8,128)S(1)} %get-tuple-element.27.ids_ref.pairs_ref, f32[320,128]{1,0:T(8,128)S(1)} %bitcast.8), custom_call_target="tpu_custom_call" | custom-call | flops 56623104 | bytes 327680 | tf_op jit(solution)/shard_map/local_forces/pallas_call | solution.py:367
  32.7 0.0 collective-permute-done.2.rest_2_
  32.7 0.0 collective-permute-done.1.rest_1_
  32.7 0.1 collective-permute-done.rest_0_
  32.7 0.0 all-to-all-done.1.vel_ref
  32.7 9.2 %remote_forces.1 = (f32[3,10240]{1,0:T(4,128)}, f32[3,10240]{1,0:T(4,128)}) custom-call(s32[32,128]{1,0:T(8,128)S(1)} %get-tuple-element.26.leaf_list, s32[8,192]{1,0:T(8,128)S(1)} %get-tuple-element.27.ids_ref.pairs_ref, f32[320,128]{1,0:T(8,128)S(1)} %bitcast.9, f32[8,40,128]{2,1,0:T(8,128)S(1)} %all-to-all-done.1.vel_ref, ...), custom_call_target="tpu_custom_call" | custom-call | flops 56623104 | bytes 983040 | tf_op jit(solution)/shard_map/remote_forces/pallas_call | solution.py:461
Async XLA Ops:
  4.8 13.6 %all-to-all-start = ((f32[8,40,128]{2,1,0:T(8,128)}), f32[8,40,128]{2,1,0:T(8,128)S(1)}, u32[]{:S(2)}, u32[]{:S(2)}) async-start(f32[8,40,128]{2,1,0:T(8,128)} %get-tuple-element.17), calls=%async_computation | async-start | bytes 327680 | tf_op jit(solution)/shard_map/all_to_all | solution.py:490
  18.3 14.4 %all-to-all-start.1 = ((f32[8,40,128]{2,1,0:T(8,128)}), f32[8,40,128]{2,1,0:T(8,128)S(1)}, u32[]{:S(2)}, u32[]{:S(2)}) async-start(f32[8,40,128]{2,1,0:T(8,128)} %get-tuple-element.29), calls=%async_computation.1 | async-start | bytes 327680 | tf_op jit(solution)/shard_map/all_to_all | solution.py:495
  21.7 10.9 %collective-permute-start.2 = (f32[80,4,128]{2,1,0:T(4,128)S(1)}, f32[80,4,128]{2,1,0:T(4,128)S(1)}, u32[]{:S(2)}, u32[]{:S(2)}) collective-permute-start(f32[80,4,128]{2,1,0:T(4,128)S(1)} %bitcast.5), channel_id=1, source_target_pairs={{0,24},{8,16},{16,8},{24,0},{1,25},{9,17},{17,9},{25,1},{2,26},{10... | collective-permute-start | bytes 491528 | tf_op jit(solution)/shard_map/ppermute | solution.py:494
  24.2 8.4 %collective-permute-start.1 = (f32[80,4,128]{2,1,0:T(4,128)S(1)}, f32[80,4,128]{2,1,0:T(4,128)S(1)}, u32[]{:S(2)}, u32[]{:S(2)}) collective-permute-start(f32[80,4,128]{2,1,0:T(4,128)S(1)} %bitcast.6), channel_id=1, source_target_pairs={{0,16},{8,24},{16,0},{24,8},{1,17},{9,25},{17,1},{25,9},{2,18},{10... | collective-permute-start | bytes 491528 | tf_op jit(solution)/shard_map/ppermute | solution.py:494
  24.7 8.0 %collective-permute-start = (f32[80,4,128]{2,1,0:T(4,128)S(1)}, f32[80,4,128]{2,1,0:T(4,128)S(1)}, u32[]{:S(2)}, u32[]{:S(2)}) collective-permute-start(f32[80,4,128]{2,1,0:T(4,128)S(1)} %bitcast.7), channel_id=1, source_target_pairs={{0,8},{8,0},{16,24},{24,16},{1,9},{9,1},{17,25},{25,17},{2,10},{10... | collective-permute-start | bytes 491528 | tf_op jit(solution)/shard_map/ppermute | solution.py:494
